TPU v7x, 32 devices: a whole 2x2x4 slice. The times are simulated.
32 devices in a mesh: seq: 4 (over y, x), dp: 8 (over z, core).
Axes of the slice: x: 2, y: 2, z: 4, core: 2. Of those that a mesh axis runs over, the one named last changes fastest.
Arguments:
- tokens: bfloat16 [32, 1024, 768], P('dp', 'seq'), may hold values from -6 to 6
- encoded: bfloat16 [32, 1024, 768], P('dp', 'seq'), may hold values from -6 to 6
- cotangent: bfloat16 [32, 1024, 768], P('dp', 'seq'), may hold values from -6 to 6
- doc_starts: int32 [32, 4], P('dp'), may hold values from 0 to 1023, as said below
- rel_bucket: int32 [1024], replicated, may hold values from 0 to 31
- self_query: bfloat16 [768, 768], P(('seq', 'dp')), may hold values from -0.02734375 to 0.02734375
- self_key: bfloat16 [768, 768], P(('seq', 'dp')), may hold values from -0.21875 to 0.21875
- self_value: bfloat16 [768, 768], P(('seq', 'dp')), may hold values from -0.21875 to 0.21875
- self_output_weight: bfloat16 [768, 768], P(('seq', 'dp')), may hold values from -0.875 to 0.875
- cross_query: bfloat16 [768, 768], P(('seq', 'dp')), may hold values from -0.02734375 to 0.02734375
- cross_key: bfloat16 [768, 768], P(('seq', 'dp')), may hold values from -0.21875 to 0.21875
- cross_value: bfloat16 [768, 768], P(('seq', 'dp')), may hold values from -0.21875 to 0.21875
- cross_output_weight: bfloat16 [768, 768], P(('seq', 'dp')), may hold values from -3.5 to 3.5
- feed_input_weight: bfloat16 [768, 3072], P(('seq', 'dp')), may hold values from -0.21875 to 0.21875
- feed_output_weight: bfloat16 [3072, 768], P(('seq', 'dp')), may hold values from -0.15625 to 0.15625
- gain_self: bfloat16 [768], P(('seq', 'dp')), may hold values from 0.5 to 1.5
- gain_cross: bfloat16 [768], P(('seq', 'dp')), may hold values from 0.5 to 1.5
- gain_feed: bfloat16 [768], P(('seq', 'dp')), may hold values from 0.5 to 1.5
- mix_pre: float32 [12, 12], replicated, may hold values from -1.75 to 1.75
- mix_post: float32 [12, 12], replicated, may hold values from -1.75 to 1.75
- rel_table: float32 [32, 12], replicated, may hold values from -4 to 4
Outputs:
- output: bfloat16 [32, 1024, 768], P('dp', 'seq')
- grad_tokens: float32 [32, 1024, 768], P('dp', 'seq')
- grad_encoded: float32 [32, 1024, 768], P('dp', 'seq')
- grad_self_query: float32 [768, 768], P(('seq', 'dp'))
- grad_self_key: float32 [768, 768], P(('seq', 'dp'))
- grad_self_value: float32 [768, 768], P(('seq', 'dp'))
- grad_self_out: float32 [768, 768], P(('seq', 'dp'))
- grad_cross_query: float32 [768, 768], P(('seq', 'dp'))
- grad_cross_key: float32 [768, 768], P(('seq', 'dp'))
- grad_cross_value: float32 [768, 768], P(('seq', 'dp'))
- grad_cross_out: float32 [768, 768], P(('seq', 'dp'))
- grad_feed_in: float32 [768, 3072], P(('seq', 'dp'))
- grad_feed_out: float32 [3072, 768], P(('seq', 'dp'))
- grad_gain_self: float32 [768], P(('seq', 'dp'))
- grad_gain_cross: float32 [768], P(('seq', 'dp'))
- grad_gain_feed: float32 [768], P(('seq', 'dp'))
- grad_mix_pre: float32 [12, 12], replicated
- grad_mix_post: float32 [12, 12], replicated
- grad_rel_table: float32 [32, 12], replicated
Inputs may be any that keep to these rules, and one draw needn't show every extreme that they name: `doc_starts`: each stream's 4 document starts rise strictly, and the first is 0.
All inputs are finite; a program needn't handle non-finite values.
Results may differ from a plain program's by a relative error of at most 0.024.
Values may be sent and summed in bfloat16 or wider, within the bound.
A program may use at most 576 MiB of HBM per device.

v0:
```python
import jax
import jax.numpy as jnp
from jax import lax
from jax.sharding import PartitionSpec as P

H = 12
DH = 64
LEN = 1024
SPM = 2


def norm_apply(value_rows, gain):
    return (
        value_rows
        * lax.rsqrt(jnp.mean(value_rows * value_rows, axis=-1, keepdims=True) + 1e-06)
        * gain
    )


def norm_grad(value_rows, gain, gradient_tree):
    unused_value, pullback = jax.vjp(norm_apply, value_rows, gain)
    return pullback(gradient_tree)


def smooth_gate(value_rows):
    return jax.nn.gelu(value_rows, approximate=True)


def smooth_grad(value_rows, gradient_tree):
    unused_value, pullback = jax.vjp(smooth_gate, value_rows)
    return pullback(gradient_tree)[0]


def project(value_rows, weight_matrix):
    return jnp.einsum("tqg,gh->tqh", value_rows, weight_matrix, preferred_element_type=jnp.float32)


def project_back(gradient_tree, weight_matrix):
    return jnp.einsum(
        "wbt,nt->wbn", gradient_tree, weight_matrix, preferred_element_type=jnp.float32
    )


def weight_grad(value_rows, gradient_tree):
    return jnp.einsum("wfk,wfq->kq", value_rows, gradient_tree, preferred_element_type=jnp.float32)


def split_heads(value_rows):
    return value_rows.reshape(value_rows.shape[0], value_rows.shape[1], H, DH)


def merge_heads(value_rows):
    return value_rows.reshape(value_rows.shape[0], value_rows.shape[1], -1)


def softmax_rows(scores):
    row_max = jnp.max(scores, axis=-1, keepdims=True)
    shifted = jnp.exp(scores - row_max)
    row_sum = jnp.sum(shifted, axis=-1, keepdims=True)
    return (shifted / row_sum, row_max + jnp.log(row_sum))


def self_mixed(query_heads, key_heads, mix_pre, bias, allowed):
    logits = jnp.einsum(
        "sqhd,skhd->shqk", query_heads, key_heads, preferred_element_type=jnp.float32
    )
    mixed = (
        jnp.einsum("gh,sgqk->shqk", mix_pre, logits, precision=lax.Precision.HIGHEST) + bias[None]
    )
    return (logits, jnp.where(allowed[:, None], mixed, -1e30))


def per_device(
    tokens,
    encoded,
    cotangent,
    doc_starts,
    rel_bucket,
    self_query,
    self_key,
    self_value,
    self_output_weight,
    cross_query,
    cross_key,
    cross_value,
    cross_output_weight,
    feed_input_weight,
    feed_output_weight,
    gain_self,
    gain_cross,
    gain_feed,
    mix_pre,
    mix_post,
    rel_table,
):
    local_len = tokens.shape[1]
    batches = tokens.shape[0] // SPM
    buckets = rel_table.shape[0]
    query_pos = lax.axis_index("seq") * local_len + jnp.arange(local_len)
    key_pos = jnp.arange(LEN)
    distance = jnp.clip(query_pos[:, None] - key_pos[None, :], 0, LEN - 1)
    causal = query_pos[:, None] >= key_pos[None, :]
    bucket_hot = (rel_bucket[:, None] == jnp.arange(buckets)[None, :]).astype(jnp.float32)
    table_rows = jnp.dot(bucket_hot, rel_table, precision=lax.Precision.HIGHEST)
    bias = jnp.take(table_rows.T, distance, axis=1)
    pair_bucket = jnp.take(rel_bucket, distance.reshape(-1), axis=0)
    pair_hot = (pair_bucket[:, None] == jnp.arange(buckets)[None, :]).astype(jnp.float32)
    shards = (
        self_query,
        self_key,
        self_value,
        self_output_weight,
        cross_query,
        cross_key,
        cross_value,
        cross_output_weight,
        feed_input_weight,
        feed_output_weight,
        gain_self,
        gain_cross,
        gain_feed,
    )
    devices = lax.axis_size(("seq", "dp"))
    grads_init = tuple(
        (jnp.zeros((shard.shape[0] * devices,) + shard.shape[1:], jnp.float32) for shard in shards)
    )
    small_init = (jnp.zeros_like(mix_pre), jnp.zeros_like(mix_post), jnp.zeros_like(rel_table))
    outputs_init = (
        jnp.zeros(tokens.shape, jnp.bfloat16),
        jnp.zeros(tokens.shape, jnp.float32),
        jnp.zeros(encoded.shape, jnp.float32),
    )

    def batch_step(micro_index, carry):
        outputs, gradient_tree, small = carry
        full = (
            lax.all_gather(self_query, ("seq", "dp"), axis=0, tiled=True),
            lax.all_gather(self_key, ("seq", "dp"), axis=0, tiled=True),
            lax.all_gather(self_value, ("seq", "dp"), axis=0, tiled=True),
            lax.all_gather(self_output_weight, ("seq", "dp"), axis=0, tiled=True),
            lax.all_gather(cross_query, ("seq", "dp"), axis=0, tiled=True),
            lax.all_gather(cross_key, ("seq", "dp"), axis=0, tiled=True),
            lax.all_gather(cross_value, ("seq", "dp"), axis=0, tiled=True),
            lax.all_gather(cross_output_weight, ("seq", "dp"), axis=0, tiled=True),
            lax.all_gather(feed_input_weight, ("seq", "dp"), axis=0, tiled=True),
            lax.all_gather(feed_output_weight, ("seq", "dp"), axis=0, tiled=True),
            lax.all_gather(gain_self, ("seq", "dp"), axis=0, tiled=True),
            lax.all_gather(gain_cross, ("seq", "dp"), axis=0, tiled=True),
            lax.all_gather(gain_feed, ("seq", "dp"), axis=0, tiled=True),
        )
        w_query, w_key, w_value, w_out, w_seek, w_find, w_fetch, w_return, w_inner, w_outer = full[
            :10
        ]
        norm_self = full[10].astype(jnp.float32)
        norm_cross = full[11].astype(jnp.float32)
        norm_feed = full[12].astype(jnp.float32)
        first_row = micro_index * SPM
        tok_rows = lax.dynamic_slice_in_dim(tokens, first_row, SPM, 0)
        enc_rows = lax.dynamic_slice_in_dim(encoded, first_row, SPM, 0)
        cot_rows = lax.dynamic_slice_in_dim(cotangent, first_row, SPM, 0)
        starts_now = lax.dynamic_slice_in_dim(doc_starts, first_row, SPM, 0)
        doc_query = jnp.sum(starts_now[:, None, :] <= query_pos[None, :, None], axis=-1)
        doc_key = jnp.sum(starts_now[:, None, :] <= key_pos[None, :, None], axis=-1)
        allowed = causal[None] & (doc_query[:, :, None] == doc_key[:, None, :])
        tok_float = tok_rows.astype(jnp.float32)
        normed_self = norm_apply(tok_float, norm_self).astype(jnp.bfloat16)
        query_local = project(normed_self, w_query).astype(jnp.bfloat16)
        key_local = project(normed_self, w_key).astype(jnp.bfloat16)
        value_local = project(normed_self, w_value).astype(jnp.bfloat16)
        key_all, value_all = (
            lax.all_gather(key_local, "seq", axis=1, tiled=True),
            lax.all_gather(value_local, "seq", axis=1, tiled=True),
        )
        query_heads = split_heads(query_local)
        key_heads = split_heads(key_all)
        value_heads = split_heads(value_all)
        unused_logits, mixed = self_mixed(query_heads, key_heads, mix_pre, bias, allowed)
        probs, self_lse = softmax_rows(mixed)
        blended = jnp.einsum(
            "gh,sgqk->shqk", mix_post, probs, precision=lax.Precision.HIGHEST
        ).astype(jnp.bfloat16)
        attention_result = merge_heads(
            jnp.einsum(
                "shqk,skhd->sqhd", blended, value_heads, preferred_element_type=jnp.float32
            ).astype(jnp.bfloat16)
        )
        hidden_after_self = tok_float + project(attention_result, w_out)
        normed_cross = norm_apply(hidden_after_self, norm_cross).astype(jnp.bfloat16)
        cross_query_now = project(normed_cross, w_seek).astype(jnp.bfloat16)
        cross_key_local = project(enc_rows, w_find).astype(jnp.bfloat16)
        cross_value_local = project(enc_rows, w_fetch).astype(jnp.bfloat16)
        cross_key_all, cross_value_all = (
            lax.all_gather(cross_key_local, "seq", axis=1, tiled=True),
            lax.all_gather(cross_value_local, "seq", axis=1, tiled=True),
        )
        cq_heads = split_heads(cross_query_now)
        ck_heads = split_heads(cross_key_all)
        cv_heads = split_heads(cross_value_all)
        cross_logits = jnp.einsum(
            "sqhd,skhd->shqk", cq_heads, ck_heads, preferred_element_type=jnp.float32
        )
        cross_probs, cross_lse = softmax_rows(cross_logits)
        cross_attention_value = merge_heads(
            jnp.einsum(
                "shqk,skhd->sqhd",
                cross_probs.astype(jnp.bfloat16),
                cv_heads,
                preferred_element_type=jnp.float32,
            ).astype(jnp.bfloat16)
        )
        hidden_after_cross = hidden_after_self + project(cross_attention_value, w_return)
        feed_normalized = norm_apply(hidden_after_cross, norm_feed).astype(jnp.bfloat16)
        inner_pre = project(feed_normalized, w_inner)
        inner_activation = smooth_gate(inner_pre).astype(jnp.bfloat16)
        result = (hidden_after_cross + project(inner_activation, w_outer)).astype(jnp.bfloat16)
        cot_float = cot_rows.astype(jnp.float32)
        back_inner = smooth_grad(inner_pre, project_back(cot_rows, w_outer)).astype(jnp.bfloat16)
        grad_outer = weight_grad(inner_activation, cot_rows)
        grad_inner = weight_grad(feed_normalized, back_inner)
        back_cross_hidden, grad_norm_feed = norm_grad(
            hidden_after_cross, norm_feed, project_back(back_inner, w_inner)
        )
        back_cross_hidden = back_cross_hidden + cot_float
        back_cross_branch = back_cross_hidden.astype(jnp.bfloat16)
        grad_return = weight_grad(cross_attention_value, back_cross_branch)
        back_cross_merged = project_back(back_cross_branch, w_return).astype(jnp.bfloat16)
        back_cross_att = split_heads(back_cross_merged)
        cross_again = jnp.exp(
            jnp.einsum("sqhd,skhd->shqk", cq_heads, ck_heads, preferred_element_type=jnp.float32)
            - cross_lse
        )
        back_cross_probs = jnp.einsum(
            "sqhd,skhd->shqk", back_cross_att, cv_heads, preferred_element_type=jnp.float32
        )
        cross_delta = jnp.sum(back_cross_probs * cross_again, axis=-1, keepdims=True)
        back_cross_logits = (cross_again * (back_cross_probs - cross_delta)).astype(jnp.bfloat16)
        back_cq = merge_heads(
            jnp.einsum(
                "shqk,skhd->sqhd", back_cross_logits, ck_heads, preferred_element_type=jnp.float32
            ).astype(jnp.bfloat16)
        )
        back_cv_part = jnp.einsum(
            "shqk,sqhd->skhd",
            cross_again.astype(jnp.bfloat16),
            back_cross_att,
            preferred_element_type=jnp.float32,
        )
        back_ck_part = jnp.einsum(
            "shqk,sqhd->skhd", back_cross_logits, cq_heads, preferred_element_type=jnp.float32
        )
        back_ck_sum, back_cv_sum = (
            lax.psum_scatter(
                merge_heads(back_ck_part).astype(jnp.bfloat16),
                "seq",
                scatter_dimension=1,
                tiled=True,
            ).astype(jnp.float32),
            lax.psum_scatter(
                merge_heads(back_cv_part).astype(jnp.bfloat16),
                "seq",
                scatter_dimension=1,
                tiled=True,
            ).astype(jnp.float32),
        )
        back_ck = back_ck_sum.astype(jnp.bfloat16)
        back_cv = back_cv_sum.astype(jnp.bfloat16)
        grad_seek = weight_grad(normed_cross, back_cq)
        grad_find = weight_grad(enc_rows, back_ck)
        grad_fetch = weight_grad(enc_rows, back_cv)
        enc_grad = project_back(back_ck, w_find) + project_back(back_cv, w_fetch)
        back_self_hidden, grad_norm_cross = norm_grad(
            hidden_after_self, norm_cross, project_back(back_cq, w_seek)
        )
        back_self_hidden = back_self_hidden + back_cross_hidden
        back_self_branch = back_self_hidden.astype(jnp.bfloat16)
        grad_out = weight_grad(attention_result, back_self_branch)
        back_att_merged = project_back(back_self_branch, w_out).astype(jnp.bfloat16)
        back_attended = split_heads(back_att_merged)
        logits_again, mixed_again = self_mixed(query_heads, key_heads, mix_pre, bias, allowed)
        probs_again = jnp.exp(mixed_again - self_lse)
        back_blended = jnp.einsum(
            "sqhd,skhd->shqk", back_attended, value_heads, preferred_element_type=jnp.float32
        )
        grad_post = jnp.einsum(
            "sgqk,shqk->gh", probs_again, back_blended, precision=lax.Precision.HIGHEST
        )
        back_probs = jnp.einsum(
            "gh,shqk->sgqk", mix_post, back_blended, precision=lax.Precision.HIGHEST
        )
        self_delta = jnp.sum(back_probs * probs_again, axis=-1, keepdims=True)
        back_mixed = probs_again * (back_probs - self_delta)
        grad_pre = jnp.einsum(
            "sgqk,shqk->gh", logits_again, back_mixed, precision=lax.Precision.HIGHEST
        )
        bias_grad = jnp.sum(back_mixed, axis=0)
        grad_table = jnp.dot(
            bias_grad.reshape(bias_grad.shape[0], -1), pair_hot, precision=lax.Precision.HIGHEST
        ).T
        back_logits = jnp.einsum(
            "gh,shqk->sgqk", mix_pre, back_mixed, precision=lax.Precision.HIGHEST
        ).astype(jnp.bfloat16)
        back_query = merge_heads(
            jnp.einsum(
                "sgqk,skgd->sqgd", back_logits, key_heads, preferred_element_type=jnp.float32
            ).astype(jnp.bfloat16)
        )
        blended_again = jnp.einsum(
            "gh,sgqk->shqk", mix_post, probs_again, precision=lax.Precision.HIGHEST
        ).astype(jnp.bfloat16)
        back_v_part = jnp.einsum(
            "shqk,sqhd->skhd", blended_again, back_attended, preferred_element_type=jnp.float32
        )
        back_k_part = jnp.einsum(
            "sgqk,sqgd->skgd", back_logits, query_heads, preferred_element_type=jnp.float32
        )
        back_k_sum, back_v_sum = (
            lax.psum_scatter(
                merge_heads(back_k_part).astype(jnp.bfloat16),
                "seq",
                scatter_dimension=1,
                tiled=True,
            ).astype(jnp.float32),
            lax.psum_scatter(
                merge_heads(back_v_part).astype(jnp.bfloat16),
                "seq",
                scatter_dimension=1,
                tiled=True,
            ).astype(jnp.float32),
        )
        back_key = back_k_sum.astype(jnp.bfloat16)
        back_value = back_v_sum.astype(jnp.bfloat16)
        grad_query = weight_grad(normed_self, back_query)
        grad_key = weight_grad(normed_self, back_key)
        grad_value = weight_grad(normed_self, back_value)
        back_normed = (
            project_back(back_query, w_query)
            + project_back(back_key, w_key)
            + project_back(back_value, w_value)
        )
        token_grad, grad_norm_self = norm_grad(tok_float, norm_self, back_normed)
        token_grad = token_grad + back_self_hidden
        new_outputs = (
            lax.dynamic_update_slice_in_dim(outputs[0], result, first_row, 0),
            lax.dynamic_update_slice_in_dim(outputs[1], token_grad, first_row, 0),
            lax.dynamic_update_slice_in_dim(outputs[2], enc_grad, first_row, 0),
        )
        new_grads = jax.tree.map(
            jnp.add,
            gradient_tree,
            (
                grad_query,
                grad_key,
                grad_value,
                grad_out,
                grad_seek,
                grad_find,
                grad_fetch,
                grad_return,
                grad_inner,
                grad_outer,
                grad_norm_self,
                grad_norm_cross,
                grad_norm_feed,
            ),
        )
        new_small = jax.tree.map(jnp.add, small, (grad_pre, grad_post, grad_table))
        return (new_outputs, new_grads, new_small)

    outputs, gradient_tree, small = lax.fori_loop(
        0, batches, batch_step, (outputs_init, grads_init, small_init)
    )
    summed = lax.psum_scatter(gradient_tree, ("seq", "dp"), scatter_dimension=0, tiled=True)
    small_sum = lax.psum((small[0], small[1], small[2]), ("seq", "dp"))
    return (outputs[0], outputs[1], outputs[2]) + tuple(summed) + tuple(small_sum)


def solution(mesh):
    in_specs = (
        P("dp", "seq", None),
        P("dp", "seq", None),
        P("dp", "seq", None),
        P("dp", None),
        P(),
        P(("seq", "dp"), None),
        P(("seq", "dp"), None),
        P(("seq", "dp"), None),
        P(("seq", "dp"), None),
        P(("seq", "dp"), None),
        P(("seq", "dp"), None),
        P(("seq", "dp"), None),
        P(("seq", "dp"), None),
        P(("seq", "dp"), None),
        P(("seq", "dp"), None),
        P(("seq", "dp")),
        P(("seq", "dp")),
        P(("seq", "dp")),
        P(),
        P(),
        P(),
    )
    out_specs = (
        P("dp", "seq", None),
        P("dp", "seq", None),
        P("dp", "seq", None),
        P(("seq", "dp"), None),
        P(("seq", "dp"), None),
        P(("seq", "dp"), None),
        P(("seq", "dp"), None),
        P(("seq", "dp"), None),
        P(("seq", "dp"), None),
        P(("seq", "dp"), None),
        P(("seq", "dp"), None),
        P(("seq", "dp"), None),
        P(("seq", "dp"), None),
        P(("seq", "dp")),
        P(("seq", "dp")),
        P(("seq", "dp")),
        P(),
        P(),
        P(),
    )
    return jax.shard_map(
        per_device, mesh=mesh, in_specs=in_specs, out_specs=out_specs, check_vma=False
    )
```

profile of v0, /device:TPU:0, one launch (start us, length us, event | category | flops | bytes accessed | tf_op | source)
XLA Modules:
  0.0 6017.0 jit_solution(13881024922410387992)
XLA Ops:
  17.1 1041.2 %gather_fusion.1 = s32[262144]{0:T(1024)S(1)} fusion(s32[1024]{0:T(1024)S(1)} %copy-done.2, s32[262144]{0:T(1024)S(1)} %broadcast_clamp_fusion), kind=kCustom, calls=%fused_computation.1 | custom fusion | bytes 3145728 | tf_op jit(solution)/shard_map/jit(_take)/gather | solution.py:106
  1058.3 861.0 %gather_fusion = f32[262144,12]{1,0:T(8,128)} fusion(f32[12,1024]{0,1:T(8,128)} %copy.244, s32[262144]{0:T(1024)S(1)} %copy-done.64), kind=kCustom, calls=%fused_computation | custom fusion | bytes 26214400 | tf_op jit(solution)/shard_map/jit(_take)/gather | solution.py:105
  1919.3 73.2 %copy.245 = f32[256,1024,12]{1,2,0:T(8,128)} copy(f32[256,1024,12]{2,1,0:T(8,128)} %bitcast.1) | data formatting | bytes 25165824 | tf_op jit(solution)/shard_map/jit(_take)/gather | solution.py:105
  2011.6 2880.9 %while.52 = (s32[]{:T(128)}, bf16[4,256,768]{2,1,0:T(8,128)(2,1)}, f32[4,256,768]{2,1,0:T(8,128)}, f32[4,256,768]{2,1,0:T(8,128)}, f32[768,768]{1,0:T(8,128)}, /...) while((s32[]{:T(128)}, bf16[4,256,768]{2,1,0:T(8,128)(2,1)}, ...), condition=%wide.region_23.24_spmd.clone, body=%wide.region_0.23_spmd.clone.sunk | while | flops 46578810880 | bytes 1859336704 | solution.py:369
  2357.3 85.6 %fusion.429 = (f32[2,12,256]{1,2,0:T(8,128)S(1)}, f32[2,256,1024,12]{2,3,1,0:T(8,128)}) fusion(f32[12,256,1024]{2,0,1:T(8,128)} %get-tuple-element.1887, pred[2,256,1024]{2,1,0:T(8,128)(4,1)} %compare_and_fusion.2, f32[12,12]{1,0:T(8,128)S(1)} %get-tuple-element.1886, f32[2,12,256,1024]{3,2,1,0:T(8,128)} %fusion.428), kind=kOutput, calls=%fused_computation.36.clone.1 | convolution fusion | flops 924837888 | bytes 63464000 | tf_op jit(solution)/shard_map/while/body/eval_jaxpr/gh,sgqk->shqk/dot_general | solution.py:68
  2652.0 62.3 %all-gather.41.cloned.1.call-done = bf16[768,3072]{1,0:T(8,128)(2,1)} async-done(((bf16[24,3072]{1,0:T(8,128)(2,1)}), bf16[768,3072]{1,0:T(8,128)(2,1)}) %all-gather.41.cloned.1.call-update) | async-done | bytes 4718608 | tf_op jit(solution)/shard_map/while/body/eval_jaxpr/all_gather | solution.py:145
  2862.0 89.5 %fusion.443 = (f32[2,12,256]{1,2,0:T(8,128)S(1)}, f32[2,12,256,1024]{3,1,2,0:T(8,128)}, f32[2,256,1024,12]{2,3,1,0:T(8,128)}) fusion(f32[2,12,256]{1,2,0:T(8,128)S(1)} %copy-done.44, f32[12,256,1024]{2,0,1:T(8,128)} %get-tuple-element.1887, f32[2,256,1024,12]{2,3,1,0:T(8,128)} %get-tuple-element.1730, pred[2,256,1024]{2,1,0:T(8,128)(4,1)S(1)} %copy-done.21, ...), kind=kOutput, calls=%fused_computation.8.clone.1 | convolution fusion | flops 937420800 | bytes 113820224 | tf_op jit(solution)/shard_map/while/body/eval_jaxpr/gh,shqk->sgqk/dot_general | solution.py:287
  3251.2 61.3 %fusion.455 = f32[12,12]{1,0:T(8,128)S(1)} fusion(f32[2,12,256,1024]{3,2,1,0:T(8,128)} %fusion.442, f32[2,12,256,1024]{3,1,2,0:T(8,128)} %get-tuple-element.1746, f32[12,12]{1,0:T(8,128)S(1)} %copy-done.85, pred[]{:T(512)S(6)} %compare.3), kind=kOutput, calls=%fused_computation.158.clone.1 | convolution fusion | flops 905969920 | bytes 50332800 | tf_op jit(solution)/shard_map/while/body/eval_jaxpr/sgqk,shqk->gh/dot_general | solution.py:284
  3357.8 62.5 %fusion.454 = f32[12,12]{1,0:T(8,128)S(1)} fusion(f32[2,12,256,1024]{3,1,2,0:T(8,128)} %get-tuple-element.1749, f32[2,12,256,1024]{3,2,1,0:T(8,128)} %fusion.428, f32[12,12]{1,0:T(8,128)S(1)} %copy-done.88, pred[]{:T(512)S(6)} %compare.3), kind=kOutput, calls=%fused_computation.159.clone.1 | convolution fusion | flops 905969920 | bytes 50332800 | tf_op jit(solution)/shard_map/while/body/eval_jaxpr/sgqk,shqk->gh/dot_general | solution.py:292
  3790.1 85.6 %fusion.429 = (f32[2,12,256]{1,2,0:T(8,128)S(1)}, f32[2,256,1024,12]{2,3,1,0:T(8,128)}) fusion(f32[12,256,1024]{2,0,1:T(8,128)} %get-tuple-element.1887, pred[2,256,1024]{2,1,0:T(8,128)(4,1)} %compare_and_fusion.2, f32[12,12]{1,0:T(8,128)S(1)} %get-tuple-element.1886, f32[2,12,256,1024]{3,2,1,0:T(8,128)} %fusion.428), kind=kOutput, calls=%fused_computation.36.clone.1 | convolution fusion | flops 924837888 | bytes 63464000 | tf_op jit(solution)/shard_map/while/body/eval_jaxpr/gh,sgqk->shqk/dot_general | solution.py:68
  4084.7 62.3 %all-gather.41.cloned.1.call-done = bf16[768,3072]{1,0:T(8,128)(2,1)} async-done(((bf16[24,3072]{1,0:T(8,128)(2,1)}), bf16[768,3072]{1,0:T(8,128)(2,1)}) %all-gather.41.cloned.1.call-update) | async-done | bytes 4718608 | tf_op jit(solution)/shard_map/while/body/eval_jaxpr/all_gather | solution.py:145
  4154.0 58.5 all-gather.39.cloned.1.call-done
  4295.0 89.5 %fusion.443 = (f32[2,12,256]{1,2,0:T(8,128)S(1)}, f32[2,12,256,1024]{3,1,2,0:T(8,128)}, f32[2,256,1024,12]{2,3,1,0:T(8,128)}) fusion(f32[2,12,256]{1,2,0:T(8,128)S(1)} %copy-done.44, f32[12,256,1024]{2,0,1:T(8,128)} %get-tuple-element.1887, f32[2,256,1024,12]{2,3,1,0:T(8,128)} %get-tuple-element.1730, pred[2,256,1024]{2,1,0:T(8,128)(4,1)S(1)} %copy-done.21, ...), kind=kOutput, calls=%fused_computation.8.clone.1 | convolution fusion | flops 937420800 | bytes 113820224 | tf_op jit(solution)/shard_map/while/body/eval_jaxpr/gh,shqk->sgqk/dot_general | solution.py:287
  4690.2 61.3 %fusion.455 = f32[12,12]{1,0:T(8,128)S(1)} fusion(f32[2,12,256,1024]{3,2,1,0:T(8,128)} %fusion.442, f32[2,12,256,1024]{3,1,2,0:T(8,128)} %get-tuple-element.1746, f32[12,12]{1,0:T(8,128)S(1)} %copy-done.85, pred[]{:T(512)S(6)} %compare.3), kind=kOutput, calls=%fused_computation.158.clone.1 | convolution fusion | flops 905969920 | bytes 50332800 | tf_op jit(solution)/shard_map/while/body/eval_jaxpr/sgqk,shqk->gh/dot_general | solution.py:284
  4797.2 62.5 %fusion.454 = f32[12,12]{1,0:T(8,128)S(1)} fusion(f32[2,12,256,1024]{3,1,2,0:T(8,128)} %get-tuple-element.1749, f32[2,12,256,1024]{3,2,1,0:T(8,128)} %fusion.428, f32[12,12]{1,0:T(8,128)S(1)} %copy-done.88, pred[]{:T(512)S(6)} %compare.3), kind=kOutput, calls=%fused_computation.159.clone.1 | convolution fusion | flops 905969920 | bytes 50332800 | tf_op jit(solution)/shard_map/while/body/eval_jaxpr/sgqk,shqk->gh/dot_general | solution.py:292
  4996.8 104.6 %reduce-scatter.17.cloned.1.call-done = f32[24,768]{1,0:T(8,128)} async-done(((f32[768,768]{1,0:T(8,128)}), f32[24,768]{1,0:T(8,128)}) %reduce-scatter.17.cloned.1.call-update) | async-done | bytes 73744 | tf_op jit(solution)/shard_map/reduce_scatter | solution.py:372
  5101.3 103.8 %reduce-scatter.19.cloned.1.call-done = f32[24,768]{1,0:T(8,128)} async-done(((f32[768,768]{1,0:T(8,128)}), f32[24,768]{1,0:T(8,128)}) %reduce-scatter.19.cloned.1.call-update) | async-done | bytes 73744 | tf_op jit(solution)/shard_map/reduce_scatter | solution.py:372
  5205.1 104.6 %reduce-scatter.21.cloned.1.call-done = f32[24,768]{1,0:T(8,128)} async-done(((f32[768,768]{1,0:T(8,128)}), f32[24,768]{1,0:T(8,128)}) %reduce-scatter.21.cloned.1.call-update) | async-done | bytes 73744 | tf_op jit(solution)/shard_map/reduce_scatter | solution.py:372
  5309.7 103.8 %reduce-scatter.23.cloned.1.call-done = f32[24,768]{1,0:T(8,128)} async-done(((f32[768,768]{1,0:T(8,128)}), f32[24,768]{1,0:T(8,128)}) %reduce-scatter.23.cloned.1.call-update) | async-done | bytes 73744 | tf_op jit(solution)/shard_map/reduce_scatter | solution.py:372
  5413.5 104.7 %reduce-scatter.25.cloned.1.call-done = f32[24,768]{1,0:T(8,128)} async-done(((f32[768,768]{1,0:T(8,128)}), f32[24,768]{1,0:T(8,128)}) %reduce-scatter.25.cloned.1.call-update) | async-done | bytes 73744 | tf_op jit(solution)/shard_map/reduce_scatter | solution.py:372
  5518.2 103.6 %reduce-scatter.27.cloned.1.call-done = f32[24,768]{1,0:T(8,128)} async-done(((f32[768,768]{1,0:T(8,128)}), f32[24,768]{1,0:T(8,128)}) %reduce-scatter.27.cloned.1.call-update) | async-done | bytes 73744 | tf_op jit(solution)/shard_map/reduce_scatter | solution.py:372
  5621.9 104.6 %reduce-scatter.29.cloned.1.call-done = f32[24,768]{1,0:T(8,128)} async-done(((f32[768,768]{1,0:T(8,128)}), f32[24,768]{1,0:T(8,128)}) %reduce-scatter.29.cloned.1.call-update) | async-done | bytes 73744 | tf_op jit(solution)/shard_map/reduce_scatter | solution.py:372
  5726.5 141.0 %reduce-scatter.31.cloned.1.call-done = f32[24,3072]{1,0:T(8,128)} async-done(((f32[768,3072]{1,0:T(8,128)}), f32[24,3072]{1,0:T(8,128)}) %reduce-scatter.31.cloned.1.call-update) | async-done | bytes 294928 | tf_op jit(solution)/shard_map/reduce_scatter | solution.py:372
  5867.5 142.1 %reduce-scatter.33.cloned.1.call-done = f32[96,768]{1,0:T(8,128)} async-done(((f32[3072,768]{1,0:T(8,128)}), f32[96,768]{1,0:T(8,128)}) %reduce-scatter.33.cloned.1.call-update) | async-done | bytes 294928 | tf_op jit(solution)/shard_map/reduce_scatter | solution.py:372
  (786 shorter events, 2226.6 us)
Async XLA Ops:
  2075.7 440.0 %all-gather.17.cloned.1.call-start = ((), (), s32[]{:S(2)}) async-start(), calls=%async_computation.25 | async-start | bytes 3932160 | tf_op jit(solution)/shard_map/while/body/eval_jaxpr/all_gather | solution.py:172
  2132.6 404.1 %all-gather.31.cloned.1.call-start = ((), (), s32[]{:S(2)}) async-start(), calls=%async_computation.32 | async-start | bytes 1216512 | tf_op jit(solution)/shard_map/while/body/eval_jaxpr/all_gather | solution.py:141
  2133.4 412.3 %all-gather.29.cloned.1.call-start = ((), (), s32[]{:S(2)}) async-start(), calls=%async_computation.31 | async-start | bytes 3932160 | tf_op jit(solution)/shard_map/while/body/eval_jaxpr/all_gather | solution.py:194
  2188.0 403.5 %all-gather.35.cloned.1.call-start = ((), (), s32[]{:S(2)}) async-start(), calls=%async_computation.34 | async-start | bytes 3932160 | tf_op jit(solution)/shard_map/while/body/eval_jaxpr/all_gather | solution.py:193
  2244.0 404.6 %all-gather.37.cloned.1.call-start = ((), (), s32[]{:S(2)}) async-start(), calls=%async_computation.35 | async-start | bytes 1216512 | tf_op jit(solution)/shard_map/while/body/eval_jaxpr/all_gather | solution.py:144
  2244.6 469.6 %all-gather.41.cloned.1.call-start = ((), (), s32[]{:S(2)}) async-start(), calls=%async_computation.37 | async-start | bytes 4866048 | tf_op jit(solution)/shard_map/while/body/eval_jaxpr/all_gather | solution.py:145
  2245.4 534.3 %all-gather.39.cloned.1.call-start = ((), (), s32[]{:S(2)}) async-start(), calls=%async_computation.36 | async-start | bytes 4866048 | tf_op jit(solution)/shard_map/while/body/eval_jaxpr/all_gather | solution.py:146
  2245.9 1174.4 %reduce-scatter.37.cloned.1.call-start = ((), (), s32[]{:S(2)}) async-start(), calls=%async_computation.39 | async-start | bytes 3932160 | tf_op jit(solution)/shard_map/while/body/eval_jaxpr/reduce_scatter | solution.py:317
  3508.4 440.2 %all-gather.17.cloned.1.call-start = ((), (), s32[]{:S(2)}) async-start(), calls=%async_computation.25 | async-start | bytes 3932160 | tf_op jit(solution)/shard_map/while/body/eval_jaxpr/all_gather | solution.py:172
  3564.5 402.4 %all-gather.25.cloned.1.call-start = ((), (), s32[]{:S(2)}) async-start(), calls=%async_computation.29 | async-start | bytes 1216512 | tf_op jit(solution)/shard_map/while/body/eval_jaxpr/all_gather | solution.py:140
  3565.0 404.6 %all-gather.31.cloned.1.call-start = ((), (), s32[]{:S(2)}) async-start(), calls=%async_computation.32 | async-start | bytes 1216512 | tf_op jit(solution)/shard_map/while/body/eval_jaxpr/all_gather | solution.py:141
  3565.6 412.7 %all-gather.29.cloned.1.call-start = ((), (), s32[]{:S(2)}) async-start(), calls=%async_computation.31 | async-start | bytes 3932160 | tf_op jit(solution)/shard_map/while/body/eval_jaxpr/all_gather | solution.py:194
  3620.6 403.6 %all-gather.35.cloned.1.call-start = ((), (), s32[]{:S(2)}) async-start(), calls=%async_computation.34 | async-start | bytes 3932160 | tf_op jit(solution)/shard_map/while/body/eval_jaxpr/all_gather | solution.py:193
  3676.8 404.6 %all-gather.37.cloned.1.call-start = ((), (), s32[]{:S(2)}) async-start(), calls=%async_computation.35 | async-start | bytes 1216512 | tf_op jit(solution)/shard_map/while/body/eval_jaxpr/all_gather | solution.py:144
  3677.3 469.6 %all-gather.41.cloned.1.call-start = ((), (), s32[]{:S(2)}) async-start(), calls=%async_computation.37 | async-start | bytes 4866048 | tf_op jit(solution)/shard_map/while/body/eval_jaxpr/all_gather | solution.py:145
  3678.1 534.4 %all-gather.39.cloned.1.call-start = ((), (), s32[]{:S(2)}) async-start(), calls=%async_computation.36 | async-start | bytes 4866048 | tf_op jit(solution)/shard_map/while/body/eval_jaxpr/all_gather | solution.py:146
  3678.8 1181.0 %reduce-scatter.37.cloned.1.call-start = ((), (), s32[]{:S(2)}) async-start(), calls=%async_computation.39 | async-start | bytes 3932160 | tf_op jit(solution)/shard_map/while/body/eval_jaxpr/reduce_scatter | solution.py:317
  4894.3 415.4 %reduce-scatter.21.cloned.1.call-start = ((), (), s32[]{:S(2)}) async-start(), calls=%async_computation.17 | async-start | bytes 2433024 | tf_op jit(solution)/shard_map/reduce_scatter | solution.py:372
  4895.0 518.5 %reduce-scatter.23.cloned.1.call-start = ((), (), s32[]{:S(2)}) async-start(), calls=%async_computation.18 | async-start | bytes 2433024 | tf_op jit(solution)/shard_map/reduce_scatter | solution.py:372
  4895.7 622.5 %reduce-scatter.25.cloned.1.call-start = ((), (), s32[]{:S(2)}) async-start(), calls=%async_computation.19 | async-start | bytes 2433024 | tf_op jit(solution)/shard_map/reduce_scatter | solution.py:372
  4896.5 725.4 %reduce-scatter.27.cloned.1.call-start = ((), (), s32[]{:S(2)}) async-start(), calls=%async_computation.20 | async-start | bytes 2433024 | tf_op jit(solution)/shard_map/reduce_scatter | solution.py:372
  4897.1 829.4 %reduce-scatter.29.cloned.1.call-start = ((), (), s32[]{:S(2)}) async-start(), calls=%async_computation.21 | async-start | bytes 2433024 | tf_op jit(solution)/shard_map/reduce_scatter | solution.py:372
  4897.7 969.8 %reduce-scatter.31.cloned.1.call-start = ((), (), s32[]{:S(2)}) async-start(), calls=%async_computation.22 | async-start | bytes 9732096 | tf_op jit(solution)/shard_map/reduce_scatter | solution.py:372
  4898.2 1111.4 %reduce-scatter.33.cloned.1.call-start = ((), (), s32[]{:S(2)}) async-start(), calls=%async_computation.23 | async-start | bytes 9732096 | tf_op jit(solution)/shard_map/reduce_scatter | solution.py:372
  (236 other events, 13517.3 us)
Sparse Core Ops, SparseCore 0:
  2015.7 56.9 all-gather.20
  2075.7 53.1 all-gather.14
  2131.9 53.1 all-gather.26
  2187.9 53.1 all-gather.32
  2243.9 53.1 all-gather.18
  2343.6 43.9 all-gather.16
  2390.6 54.1 all-gather.24
  2447.8 53.1 all-gather.30
  2547.5 43.9 all-gather.34
  2594.4 54.1 all-gather.36
  2651.6 62.5 all-gather.40
  2717.1 62.4 all-gather.38
  3452.3 53.0 all-gather.20
  3508.3 53.1 all-gather.14
  3564.5 53.1 all-gather.26
  3620.6 53.1 all-gather.32
  3676.8 53.1 all-gather.18
  3776.4 43.9 all-gather.16
  3823.3 54.1 all-gather.24
  3880.4 53.1 all-gather.30
  3980.2 43.9 all-gather.34
  4027.1 54.1 all-gather.36
  4084.3 62.5 all-gather.40
  4150.0 62.4 all-gather.38
  (12 shorter events, 513.1 us)
Sparse Core Ops, SparseCore 1:
  4898.8 97.9 reduce-scatter.14
  5003.3 97.9 reduce-scatter.16
  5107.0 98.0 reduce-scatter.18
  5211.8 97.8 reduce-scatter.20
  5315.5 97.9 reduce-scatter.22
  5420.2 97.9 reduce-scatter.24
  5523.9 97.9 reduce-scatter.26
  5628.4 98.0 reduce-scatter.28
  5732.8 134.6 reduce-scatter.30
  5875.0 134.5 reduce-scatter.32
where the time goes:
time: 6030 us; the launch traced here: 6020 us
  local copies, waits for them, and re-layouts  2170 us (36%)
  waiting for transfers between devices  1980 us (33%)
  matrix products  1500 us (25%)
  other arithmetic  215 us (4%)
  blocking collectives  122 us (2%)
    reduce_scatter x10, waiting for transfers between devices, per_device(): lax.psum_scatter(gradient_tree, ('seq', 'dp'), scatter_dimension=0, tiled...  1070 us
    gather x1, local copies, waits for them, and re-layouts, per_device(): pair_bucket = jnp.take(rel_bucket, distance.reshape(-1), axis=0)  1040 us
    gather x2, local copies, waits for them, and re-layouts, per_device(): bias = jnp.take(table_rows.T, distance, axis=1)  934 us
    dot_general x2, matrix products, batch_step(): jnp.einsum('gh,shqk->sgqk', mix_post, back_blended, precision=lax.Precisi...  179 us
    dot_general x2, matrix products, self_mixed(): jnp.einsum('gh,sgqk->shqk', mix_pre, logits, precision=lax.Precision.HIGH...  171 us
    dot_general x2, matrix products, batch_step(): jnp.einsum('sgqk,shqk->gh', logits_again, back_mixed, precision=lax.Preci...  125 us
    all_gather x2, waiting for transfers between devices, batch_step(): lax.all_gather(feed_input_weight, ('seq', 'dp'), axis=0, tiled=True)  125 us
    dot_general x2, matrix products, batch_step(): jnp.einsum('sgqk,shqk->gh', probs_again, back_blended, precision=lax.Prec...  123 us
  transfers between devices with their start and end apart: 46, of which 32 were waited for; matrix products, arithmetic and copies ran while one was open for 21% of the time, Pallas kernels for 0%

commit v1 on v0

v1 whole, which is shorter than its diff:
```python
import functools
import jax, jax.numpy as jnp
from jax import lax
from jax.experimental import pallas as pl
from jax.experimental.pallas import tpu as pltpu
F32=jnp.float32; BF=jnp.bfloat16
NEG=-1e30
H=12; DH=64; D=768; L=1024; BLK=256; NBK=L//BLK

def dot(a,b,ca,cb):
    return lax.dot_general(a,b,(((ca,),(cb,)),((),())),preferred_element_type=F32)

def toep_kernel(base_ref, out_ref):
    for dl in range(NBK):
        row = jnp.broadcast_to(base_ref[0, dl], (BLK, 2*BLK))
        t = pltpu.roll(row, 0, 1, stride=1, stride_axis=0)[:, :BLK]
        if dl == 0:
            a = lax.broadcasted_iota(jnp.int32, (BLK,BLK),0); b=lax.broadcasted_iota(jnp.int32,(BLK,BLK),1)
            t = jnp.where(a>=b, t, NEG)
        out_ref[0, dl] = t

def toeplitz(base):
    return pl.pallas_call(toep_kernel, grid=(H,),
        in_specs=[pl.BlockSpec((1,NBK,1,2*BLK), lambda h:(h,0,0,0))],
        out_specs=pl.BlockSpec((1,NBK,BLK,BLK), lambda h:(h,0,0,0)),
        out_shape=jax.ShapeDtypeStruct((H,NBK,BLK,BLK),F32))(base)

def make_base(trow):
    dl = jnp.arange(NBK)[:,None]*BLK
    y = jnp.arange(2*BLK)[None,:]
    rows=[]
    for d in range(NBK):
        lo = d*BLK
        a = trow[:, max(lo-BLK+1,0):lo+1][:, ::-1]
        if d==0: a = jnp.concatenate([a, jnp.zeros((H,BLK-1),F32)],1)
        b = trow[:, lo+1:lo+BLK][:, ::-1]
        rows.append(jnp.concatenate([a, jnp.zeros((H,1),F32), b],1))
    return jnp.stack(rows,1)[:,:,None,:]

def self_fwd_kernel(st_ref, q_ref, k_ref, v_ref, bias_ref, mpre_ref, mpost_ref, att_ref, p_ref, acc_ref, lo_ref):
    s = pl.program_id(0)
    h = pl.program_id(1)
    @pl.when(h==0)
    def _():
        acc_ref[...] = jnp.zeros_like(acc_ref)
        pos = lax.broadcasted_iota(jnp.int32,(L,128),0)
        lo = jnp.zeros((L,128),jnp.int32)
        for d in range(1,4):
            sd = st_ref[s,d]
            lo = jnp.where(pos>=sd, sd, lo)
        lo_ref[...] = lo
    mp = mpre_ref[pl.ds(h,1),:]
    mo = mpost_ref[pl.ds(h,1),:]
    for I in range(NBK):
        r = slice(I*BLK,(I+1)*BLK); n=(I+1)*BLK
        qm = (q_ref[0,r,:].astype(F32)*mp).astype(BF)
        sc = dot(qm, k_ref[0,:n,:],1,1)
        bias = jnp.concatenate([bias_ref[0,I-J] for J in range(I+1)],1) if I else bias_ref[0,0]
        sc = sc + bias
        col = lax.broadcasted_iota(jnp.int32,(BLK,n),1)
        sc = jnp.where(col>=lo_ref[r,:1], sc, NEG)
        m = jnp.max(sc,1,keepdims=True)
        e = jnp.exp(sc-m)
        l = jnp.sum(e,1,keepdims=True)
        p = (e*(1.0/l)).astype(BF)
        p_ref[0,0,r,:n] = p
        acc_ref[r,:] += dot(p, v_ref[0,:n,:],1,0)*mo
    @pl.when(h==H-1)
    def _():
        att_ref[0] = acc_ref[...].astype(BF)

def self_fwd(starts,q,k,v,bias,mpre,mpost):
    B=q.shape[0]
    full=lambda s,h,st:(s,0,0)
    return pl.pallas_call(self_fwd_kernel,
      grid_spec=pltpu.PrefetchScalarGridSpec(num_scalar_prefetch=1, grid=(B,H),
        in_specs=[pl.BlockSpec((1,L,D),full)]*3+[pl.BlockSpec((1,NBK,BLK,BLK),lambda s,h,st:(h,0,0,0)),
                  pl.BlockSpec((H,D),lambda s,h,st:(0,0)),pl.BlockSpec((H,D),lambda s,h,st:(0,0))],
        out_specs=[pl.BlockSpec((1,L,D),full),pl.BlockSpec((1,1,L,L),lambda s,h,st:(s,h,0,0))],
        scratch_shapes=[pltpu.VMEM((L,D),F32),pltpu.VMEM((L,128),jnp.int32)]),
      out_shape=[jax.ShapeDtypeStruct((B,L,D),BF),jax.ShapeDtypeStruct((B,H,L,L),BF)],
      compiler_params=pltpu.CompilerParams(vmem_limit_bytes=56<<20),
      cost_estimate=pl.CostEstimate(flops=B*48_000_000_000,bytes_accessed=B*40_000_000,transcendentals=B*8_000_000),
      name="self_fwd")(starts,q,k,v,bias,mpre,mpost)

def self_bwd_kernel(q_ref,k_ref,v_ref,ba_ref,p_ref,mpre_ref,mpost_ref,
      dq_ref,dk_ref,dv_ref,gpre_ref,gpost_ref,diag_ref,
      qT,baT,dqa,dkT,dvT,dm):
    h=pl.program_id(1)
    @pl.when(h==0)
    def _():
        qT[...]=q_ref[0].T
        baT[...]=ba_ref[0].T
        dqa[...]=jnp.zeros_like(dqa)
        dkT[...]=jnp.zeros_like(dkT)
        dvT[...]=jnp.zeros_like(dvT)
        gpre_ref[...]=jnp.zeros_like(gpre_ref)
        gpost_ref[...]=jnp.zeros_like(gpost_ref)
    mp = mpre_ref[pl.ds(h,1),:]
    mo = mpost_ref[pl.ds(h,1),:]
    gp = jnp.zeros((8,D),F32)
    dacc=[None]*NBK
    for I in range(NBK):
        r = slice(I*BLK,(I+1)*BLK); n=(I+1)*BLK
        bam=(ba_ref[0,r,:].astype(F32)*mo).astype(BF)
        dp=dot(bam,v_ref[0,:n,:],1,1)
        p=p_ref[0,0,r,:n].astype(F32)
        dl=jnp.sum(dp*p,1,keepdims=True)
        d=p*(dp-dl)
        for J in range(I+1):
            t=d[:,J*BLK:(J+1)*BLK]
            dacc[I-J]= t if dacc[I-J] is None else dacc[I-J]+t
        db=d.astype(BF)
        dm[r,:n]=db
        R=dot(db,k_ref[0,:n,:],1,0)
        dqa[r,:]+=R*mp
        gp = gp + jnp.sum((R*q_ref[0,r,:].astype(F32)).reshape(BLK//8,8,D),0)
    gpre_ref[0,pl.ds(h,1),:]=jnp.sum(gp,0,keepdims=True)
    for dlt in range(NBK):
        x=jnp.concatenate([jnp.zeros((BLK,BLK),F32),dacc[dlt]],1)
        n=BLK//2
        while n>=1:
            x=x[:n]+pltpu.roll(x[n:],2*BLK-n,1)
            n//=2
        diag_ref[0,0,dlt]=x
    mpc=jnp.transpose(jnp.broadcast_to(mp,(8,D)))[:,:1]
    moc=jnp.transpose(jnp.broadcast_to(mo,(8,D)))[:,:1]
    gq=jnp.zeros((8,D),F32)
    for J in range(NBK):
        c=slice(J*BLK,(J+1)*BLK); i0=J*BLK
        T=dot(baT[:,i0:],p_ref[0,0,i0:,c],1,0)
        dvT[:,c]+=T*moc
        vv=v_ref[0,c,:].astype(F32)
        gq=gq+jnp.sum((T.T*vv).reshape(BLK//8,8,D),0)
        U=dot(qT[:,i0:],dm[i0:,c],1,0)
        dkT[:,c]+=U*mpc
    gpost_ref[0,pl.ds(h,1),:]=jnp.sum(gq,0,keepdims=True)
    @pl.when(h==H-1)
    def _():
        dq_ref[0]=dqa[...].astype(BF)
        dk_ref[0]=dkT[...].T.astype(BF)
        dv_ref[0]=dvT[...].T.astype(BF)

def self_bwd(q,k,v,ba,p,mpre,mpost):
    B=q.shape[0]
    full=lambda s,h:(s,0,0)
    one=pl.BlockSpec((1,L,D),full)
    lane=pl.BlockSpec((H,D),lambda s,h:(0,0))
    return pl.pallas_call(self_bwd_kernel,grid=(B,H),
      in_specs=[one]*4+[pl.BlockSpec((1,1,L,L),lambda s,h:(s,h,0,0)),lane,lane],
      out_specs=[one]*3+[pl.BlockSpec((1,H,D),full)]*2+[pl.BlockSpec((1,1,NBK,1,2*BLK),lambda s,h:(s,h,0,0,0))],
      out_shape=[jax.ShapeDtypeStruct((B,L,D),BF)]*3+[jax.ShapeDtypeStruct((B,H,D),F32)]*2+[jax.ShapeDtypeStruct((B,H,NBK,1,2*BLK),F32)],
      scratch_shapes=[pltpu.VMEM((D,L),BF)]*2+[pltpu.VMEM((L,D),F32)]+[pltpu.VMEM((D,L),F32)]*2+[pltpu.VMEM((L,L),BF)],
      compiler_params=pltpu.CompilerParams(vmem_limit_bytes=58<<20),
      cost_estimate=pl.CostEstimate(flops=B*121_000_000_000,bytes_accessed=B*40_000_000,transcendentals=0),
      name="self_bwd")(q,k,v,ba,p,mpre,mpost)
def cross_fwd_kernel(q_ref,k_ref,v_ref,att_ref,p_ref):
    first=lax.broadcasted_iota(jnp.int32,(1,128),1)<DH
    k=k_ref[0]; v=v_ref[0]
    for I in range(NBK):
        r=slice(I*BLK,(I+1)*BLK)
        q=q_ref[0,r,:]
        outs=[]
        for e in range(2):
            qe=jnp.where(first if e==0 else ~first,q,jnp.zeros_like(q))
            sc=dot(qe,k,1,1)
            m=jnp.max(sc,1,keepdims=True)
            ex=jnp.exp(sc-m)
            l=jnp.sum(ex,1,keepdims=True)
            p=(ex*(1.0/l)).astype(BF)
            p_ref[0,e,r,:]=p
            outs.append(dot(p,v,1,0))
        att_ref[0,r,:]=jnp.where(first,outs[0],outs[1]).astype(BF)
def cross_fwd(q,k,v):
    B=q.shape[0]
    pair=pl.BlockSpec((1,L,128),lambda s,h:(s,0,h))
    return pl.pallas_call(cross_fwd_kernel,grid=(B,H//2),in_specs=[pair]*3,
      out_specs=[pair,pl.BlockSpec((1,2,L,L),lambda s,h:(s,h,0,0))],
      out_shape=[jax.ShapeDtypeStruct((B,L,D),BF),jax.ShapeDtypeStruct((B,H,L,L),BF)],
      compiler_params=pltpu.CompilerParams(vmem_limit_bytes=40<<20),
      cost_estimate=pl.CostEstimate(flops=B*26_000_000_000,bytes_accessed=B*35_000_000,transcendentals=B*12_000_000),
      name="cross_fwd")(q,k,v)
def cross_bwd_kernel(q_ref,k_ref,v_ref,do_ref,p_ref,dq_ref,dk_ref,dv_ref,qT,doT,ds):
    first=lax.broadcasted_iota(jnp.int32,(1,128),1)<DH
    topT=lax.broadcasted_iota(jnp.int32,(128,1),0)<DH
    k=k_ref[0]; v=v_ref[0]
    qT[...]=q_ref[0].T; doT[...]=do_ref[0].T
    dqs=[]; dks=[]; dvs=[]
    for e in range(2):
        fe=first if e==0 else ~first
        dq=[]
        for I in range(NBK):
            r=slice(I*BLK,(I+1)*BLK)
            do=do_ref[0,r,:]
            dp=dot(jnp.where(fe,do,jnp.zeros_like(do)),v,1,1)
            p=p_ref[0,e,r,:].astype(F32)
            dl=jnp.sum(dp*p,1,keepdims=True)
            d=(p*(dp-dl)).astype(BF)
            ds[e,r,:]=d
            x=dot(d,k,1,0)
            if e==0: dq_ref[0,r,:]=x.astype(BF)
            else: dq_ref[0,r,:]=jnp.where(first,dq_ref[0,r,:],x.astype(BF))
        dvs.append(dot(doT[...],p_ref[0,e],1,0))
        dks.append(dot(qT[...],ds[e],1,0))
    dk_ref[0]=jnp.where(topT,dks[0],dks[1]).T.astype(BF)
    dv_ref[0]=jnp.where(topT,dvs[0],dvs[1]).T.astype(BF)
def cross_bwd(q,k,v,do,p):
    B=q.shape[0]
    pair=pl.BlockSpec((1,L,128),lambda s,h:(s,0,h))
    return pl.pallas_call(cross_bwd_kernel,grid=(B,H//2),
      in_specs=[pair]*4+[pl.BlockSpec((1,2,L,L),lambda s,h:(s,h,0,0))],
      out_specs=[pair]*3,
      out_shape=[jax.ShapeDtypeStruct((B,L,D),BF)]*3,
      scratch_shapes=[pltpu.VMEM((128,L),BF)]*2+[pltpu.VMEM((2,L,L),BF)],
      compiler_params=pltpu.CompilerParams(vmem_limit_bytes=40<<20),
      cost_estimate=pl.CostEstimate(flops=B*26_000_000_000,bytes_accessed=B*35_000_000,transcendentals=0),
      name="cross_bwd")(q,k,v,do,p)
from jax.sharding import PartitionSpec as P
AX = ("seq", "dp")
GATE = 0.7978845608028654


def mm(a, b):
    return jnp.dot(a, b, preferred_element_type=F32)


def mm_t(a, b):
    return lax.dot_general(a, b, (((1,), (1,)), ((), ())), preferred_element_type=F32)


def wgrad(a, b):
    return lax.dot_general(a, b, (((0,), (0,)), ((), ())), preferred_element_type=F32)


def norm(x, g):
    r = lax.rsqrt(jnp.mean(x * x, -1, keepdims=True) + 1e-6)
    return x * r * g


def norm_grad(x, g, dn):
    r = lax.rsqrt(jnp.mean(x * x, -1, keepdims=True) + 1e-6)
    gd = g * dn
    dx = r * gd - x * (r * r * r) * jnp.mean(gd * x, -1, keepdims=True)
    return dx, jnp.sum(dn * x * r, 0)


def gelu_pair(x):
    t = jnp.tanh(GATE * (x + 0.044715 * x * x * x))
    y = 0.5 * x * (1.0 + t)
    d = 0.5 * (1.0 + t) + 0.5 * x * (1.0 - t * t) * GATE * (1.0 + 3 * 0.044715 * x * x)
    return y, d


def gather(w):
    return lax.all_gather(w, AX, axis=0, tiled=True)


def scatter(g):
    return lax.psum_scatter(g.astype(BF), AX, scatter_dimension=0, tiled=True).astype(F32)


def per_device(tokens, encoded, cotangent, doc_starts, rel_bucket, sq, sk, sv, so, cq, ck, cv, co, fi, fo,
               gs, gc, gf, mix_pre, mix_post, rel_table):
    nseq = lax.axis_size("seq")
    nb = tokens.shape[0] // nseq
    buckets = rel_table.shape[0]
    to_stream = lambda x: lax.all_to_all(x, "seq", 0, 1, tiled=True)
    from_stream = lambda x: lax.all_to_all(x, "seq", 1, 0, tiled=True)
    gains = jnp.pad(jnp.stack([gs, gc, gf], 1), ((0, 0), (0, 125)))
    w1 = gather(jnp.concatenate([sq, sk, sv, gains], 1))
    w2 = gather(jnp.concatenate([so, cq, ck, cv, co], 1))
    w3 = gather(fi)
    w4 = gather(fo)
    wqkv = w1[:, :3 * D]
    g_all = w1[:, 3 * D:3 * D + 3].astype(F32).T
    g_self, g_cross, g_feed = g_all[0], g_all[1], g_all[2]
    w_o, w_cq, w_ckv, w_co = w2[:, :D], w2[:, D:2 * D], w2[:, 2 * D:4 * D], w2[:, 4 * D:]
    x = to_stream(tokens).reshape(nb * L, D).astype(F32)
    enc = to_stream(encoded).reshape(nb * L, D)
    cot = to_stream(cotangent).reshape(nb * L, D)
    starts = lax.dynamic_slice_in_dim(doc_starts, lax.axis_index("seq") * nb, nb, 0)
    hot = (rel_bucket[:, None] == jnp.arange(buckets)[None, :]).astype(F32)
    trow = lax.dot_general(rel_table, hot, (((0,), (1,)), ((), ())), precision=lax.Precision.HIGHEST)
    bias = toeplitz(make_base(trow))
    mpre = jnp.repeat(mix_pre.T, DH, axis=1)
    mpost = jnp.repeat(mix_post, DH, axis=1)
    s3 = lambda a: a.reshape(nb, L, D)
    s2 = lambda a: a.reshape(nb * L, D)
    n1 = norm(x, g_self).astype(BF)
    qkv = mm(n1, wqkv).astype(BF)
    q, k, v = qkv[:, :D], qkv[:, D:2 * D], qkv[:, 2 * D:]
    att, p = self_fwd(starts, s3(q), s3(k), s3(v), bias, mpre, mpost)
    att = s2(att)
    h1 = x + mm(att, w_o)
    n2 = norm(h1, g_cross).astype(BF)
    cqx = mm(n2, w_cq).astype(BF)
    ckv = mm(enc, w_ckv).astype(BF)
    ckx, cvx = ckv[:, :D], ckv[:, D:]
    catt, cp = cross_fwd(s3(cqx), s3(ckx), s3(cvx))
    catt = s2(catt)
    h2 = h1 + mm(catt, w_co)
    n3 = norm(h2, g_feed).astype(BF)
    inner, dgelu = gelu_pair(mm(n3, w3))
    inner = inner.astype(BF)
    out = (h2 + mm(inner, w4)).astype(BF)
    bi = (mm_t(cot, w4) * dgelu).astype(BF)
    g_fo = scatter(wgrad(inner, cot))
    g_fi = scatter(wgrad(n3, bi))
    dx, d_gf = norm_grad(h2, g_feed, mm_t(bi, w3))
    bh2 = cot.astype(F32) + dx
    bcb = bh2.astype(BF)
    bca = mm_t(bcb, w_co).astype(BF)
    gw_co = wgrad(catt, bcb)
    dcq, dck, dcv = cross_bwd(s3(cqx), s3(ckx), s3(cvx), s3(bca), cp)
    dcq, dck, dcv = s2(dcq), s2(dck), s2(dcv)
    dckv = jnp.concatenate([dck, dcv], 1)
    gw_cq = wgrad(n2, dcq)
    gw_ckv = wgrad(enc, dckv)
    g_enc = mm_t(dckv, w_ckv)
    dx, d_gc = norm_grad(h1, g_cross, mm_t(dcq, w_cq))
    bh1 = bh2 + dx
    bsb = bh1.astype(BF)
    bat = mm_t(bsb, w_o).astype(BF)
    gw_o = wgrad(att, bsb)
    r_mid = scatter(jnp.concatenate([gw_co, gw_cq, gw_ckv, gw_o], 1))
    dq, dk, dv, gpre, gpost, diag = self_bwd(s3(q), s3(k), s3(v), s3(bat), p, mpre, mpost)
    dqkv = jnp.concatenate([s2(dq), s2(dk), s2(dv)], 1)
    gw_qkv = wgrad(n1, dqkv)
    dx, d_gs = norm_grad(x, g_self, mm_t(dqkv, wqkv))
    g_tok = bh1 + dx
    r_end = scatter(gw_qkv)
    gpre = jnp.sum(gpre, 0).reshape(H, H, DH).sum(-1).T
    gpost = jnp.sum(gpost, 0).reshape(H, H, DH).sum(-1)
    dg = jnp.sum(diag, 0)[:, :, 0, ::-1]
    gt = 0.0
    for d in range(NBK):
        gt = gt + jnp.pad(dg[:, d], ((0, 0), (d * BLK + 1, L - d * BLK - 1)))
    gt = gt[:, BLK:BLK + L]
    gtab = lax.dot_general(hot, gt, (((0,), (1,)), ((), ())), precision=lax.Precision.HIGHEST)
    gpre, gpost, gtab, dgain = lax.psum((gpre, gpost, gtab, jnp.stack([d_gs, d_gc, d_gf])), AX)
    rows = gs.shape[0]
    me = lax.axis_index("seq") * lax.axis_size("dp") + lax.axis_index("dp")
    dgain = lax.dynamic_slice_in_dim(dgain, me * rows, rows, 1)
    o3 = lambda a: from_stream(s3(a))
    return (o3(out), o3(g_tok), o3(g_enc),
            r_end[:, :D], r_end[:, D:2 * D], r_end[:, 2 * D:], r_mid[:, 4 * D:],
            r_mid[:, D:2 * D], r_mid[:, 2 * D:3 * D], r_mid[:, 3 * D:4 * D], r_mid[:, :D],
            g_fi, g_fo, dgain[0], dgain[1], dgain[2], gpre, gpost, gtab)


def solution(mesh):
    act = P("dp", "seq", None)
    w = P(("seq", "dp"), None)
    g = P(("seq", "dp"))
    return jax.shard_map(per_device, mesh=mesh,
        in_specs=(act, act, act, P("dp", None), P()) + (w,) * 10 + (g,) * 3 + (P(),) * 3,
        out_specs=(act,) * 3 + (w,) * 10 + (g,) * 3 + (P(),) * 3, check_vma=False)
```

time: 6030 us -> 937 us (0.16)
  local copies, waits for them, and re-layouts: 2170 us -> 81.1 us
  waiting for transfers between devices: 1980 us -> 354 us
  matrix products: 1500 us -> 140 us
  Pallas kernels: 0 us -> 208 us
  other arithmetic: 215 us -> 29.1 us
    gather x3 -> x0, local copies, waits for them, and re-layouts: 1980 us -> none  [the longest x1 1040 us: per_device(): pair_bucket = jnp.take(rel_bucket, distance.reshape(-1), axis=0)]
    dot_general x101 -> x23, matrix products: 1500 us -> 140 us  [the longest x7 51.2 us: mm_t(): lax.dot_general(a, b, (((1,), (1,)), ((), ())), preferred_element_type=F32)]
    reduce_scatter x18 -> x3, waiting for transfers between devices: 1070 us -> 98.8 us  [scatter(): lax.psum_scatter(g.astype(BF), AX, scatter_dimension=0, tiled=True)]
    all_gather x28 -> x4, waiting for transfers between devices: 893 us -> 88.7 us  [gather(): return lax.all_gather(w, AX, axis=0, tiled=True)]
    pallas_call x0 -> x5, Pallas kernels: none -> 208 us  [the longest x1 76.5 us: self_bwd(): pl.pallas_call(self_bwd_kernel, grid=(B, H), in_specs=[one] * 4 + [pl.Blo...]
    reduce_sum x12 -> x3, other arithmetic: 143 us -> 3.12 us  [the longest x1 2.93 us: norm(): r = lax.rsqrt(jnp.mean(x * x, -1, keepdims=True) + 1e-06)]
    unnamed x10 -> x9, waiting for transfers between devices: 5.83 us -> 117 us
    while x400 -> x0, local copies, waits for them, and re-layouts: 86.6 us -> none
  transfers between devices with their start and end apart: 46 -> 14, of which waited for: 32 -> 10; matrix products, arithmetic and copies ran while one was open for 21% -> 20% of each run, Pallas kernels for 0% -> 10%
where the time goes in v1:
time: 937 us; the launch traced here: 931 us
  waiting for transfers between devices  354 us (38%)
  Pallas kernels  208 us (22%)
  matrix products  140 us (15%)
  local copies, waits for them, and re-layouts  81.1 us (9%)
  blocking collectives  75.5 us (8%)
  other arithmetic  29.1 us (3%)
  starting transfers between devices  27.6 us (3%)
  between operations  15.3 us (2%)
    unnamed x9, waiting for transfers between devices  117 us
    reduce_scatter x3, waiting for transfers between devices, scatter(): lax.psum_scatter(g.astype(BF), AX, scatter_dimension=0, tiled=True)  98.8 us
    all_gather x4, waiting for transfers between devices, gather(): return lax.all_gather(w, AX, axis=0, tiled=True)  88.7 us
    pallas_call x1, Pallas kernels, self_bwd(): pl.pallas_call(self_bwd_kernel, grid=(B, H), in_specs=[one] * 4 + [pl.Blo...  76.5 us
    psum x1, blocking collectives, per_device(): lax.psum((gpre, gpost, gtab, jnp.stack([d_gs, d_gc, d_gf])), AX)  75.5 us
    pallas_call x1, Pallas kernels, self_fwd(): pl.pallas_call(self_fwd_kernel, grid_spec=pltpu.PrefetchScalarGridSpec(nu...  54.4 us
    dot_general x7, matrix products, mm_t(): lax.dot_general(a, b, (((1,), (1,)), ((), ())), preferred_element_type=F32)  51.2 us
    dot_general x7, matrix products, mm(): return jnp.dot(a, b, preferred_element_type=F32)  46.6 us
  transfers between devices with their start and end apart: 14, of which 10 were waited for; matrix products, arithmetic and copies ran while one was open for 20% of the time, Pallas kernels for 10%

profile of v1, /device:TPU:0, one launch (start us, length us, event | category | flops | bytes accessed | tf_op | source)
XLA Modules:
  0.0 930.6 jit_solution(10410316767522267758)
XLA Ops:
  21.1 19.1 %all-to-all-done = bf16[4,256,768]{2,1,0:T(8,128)(2,1)S(1)} async-done(((bf16[4,256,768]{2,1,0:T(8,128)(2,1)}), bf16[4,256,768]{2,1,0:T(8,128)(2,1)S(1)}, u32[]{:S(2)}, u32[]{:S(2)}) %all-to-all-start) | async-done | bytes 1572896 | tf_op jit(solution)/shard_map/all_to_all | solution.py:267
  47.3 9.4 %shard_map.348.bias_ref = f32[12,4,256,256]{3,2,1,0:T(8,128)} custom-call(f32[12,4,1,512]{3,2,1,0:T(1,128)} %broadcast_in_dim.9.base_ref), custom_call_target="tpu_custom_call" | custom-call | tf_op jit(solution)/shard_map/pallas_call | solution.py:23
  73.9 15.8 %all-gather.5.cloned.1.call-done = bf16[768,2432]{1,0:T(8,128)(2,1)} async-done(((bf16[24,2432]{1,0:T(8,128)(2,1)}), bf16[768,2432]{1,0:T(8,128)(2,1)}) %all-gather.5.cloned.1.call-update) | async-done | bytes 3735568 | tf_op jit(solution)/shard_map/all_gather | solution.py:255
  100.0 54.4 %self_fwd.1 = (bf16[1,1024,768]{2,1,0:T(8,128)(2,1)}, bf16[1,12,1024,1024]{3,2,1,0:T(8,128)(2,1)}) custom-call(s32[1,4]{1,0:T(1,128)} %constant_dynamic-slice_fusion.1.st_ref, bf16[1,1024,768]{2,1,0:T(8,128)(2,1)} %get-tuple-element.136.q_ref, bf16[1,1024,768]{2,1,0:T(8,128)(2,1)} %get-tuple-element.135.k_ref, ...), custom_call_target="tpu_custom_call" | custom-call | flops 48000000000 | bytes 40000000 | tf_op jit(solution)/shard_map/self_fwd/pallas_call | solution.py:75
  175.3 33.2 %cross_fwd.1 = (bf16[1,1024,768]{2,1,0:T(8,128)(2,1)S(1)}, bf16[1,12,1024,1024]{3,2,1,0:T(8,128)(2,1)}) custom-call(bf16[1,1024,768]{2,1,0:T(8,128)(2,1)S(1)} %fusion.37.q_ref, bf16[1,1024,768]{2,1,0:T(8,128)(2,1)S(1)} %get-tuple-element.138.k_ref, bf16[1,1024,768]{2,1,0:T(8,128)(2,1)S(1)} %get-tuple-element.137.v_ref), custom_call_target="tpu_custom_call" | custom-call | flops 25999998976 | bytes 35000000 | tf_op jit(solution)/shard_map/cross_fwd/pallas_call | solution.py:177
  213.7 12.2 %all-gather.9.cloned.1.call-done = bf16[768,3072]{1,0:T(8,128)(2,1)} async-done(((bf16[24,3072]{1,0:T(8,128)(2,1)}), bf16[768,3072]{1,0:T(8,128)(2,1)}) %all-gather.9.cloned.1.call-update) | async-done | bytes 4718608 | tf_op jit(solution)/shard_map/all_gather | solution.py:255
  225.9 11.0 %fusion.62 = f32[1024,3072]{1,0:T(8,128)} fusion(bf16[768,3072]{1,0:T(8,128)(2,1)} %all-gather.9.cloned.1.call-done, f32[1024,768]{0,1:T(8,128)} %get-tuple-element.172, f32[768]{0:T(1024)S(1)} %get-tuple-element.127, f32[1024]{0:T(1024)S(1)} %get-tuple-element.161), kind=kOutput, calls=%fused_computation.133 | convolution fusion | flops 4834197504 | bytes 20454400 | tf_op jit(solution)/shard_map/dot_general | solution.py:224
  236.9 54.4 %all-gather.11.cloned.1.call-done = bf16[3072,768]{1,0:T(8,128)(2,1)} async-done(((bf16[96,768]{1,0:T(8,128)(2,1)}), bf16[3072,768]{1,0:T(8,128)(2,1)}) %all-gather.11.cloned.1.call-update) | async-done | bytes 4718608 | tf_op jit(solution)/shard_map/all_gather | solution.py:255
  291.3 16.8 %fusion.6 = bf16[1024,3072]{1,0:T(8,128)(2,1)} fusion(f32[1024,3072]{1,0:T(8,128)} %fusion.62, bf16[1024,768]{1,0:T(8,128)(2,1)} %bitcast.21, bf16[3072,768]{1,0:T(8,128)(2,1)} %all-gather.11.cloned.1.call-done), kind=kOutput, calls=%fused_computation.8 | convolution fusion | flops 4891607040 | bytes 25165824 | tf_op jit(solution)/shard_map/dot_general | solution.py:228
  308.1 8.3 multiply_reduce_fusion
  321.0 34.5 %cross_bwd.1 = (bf16[1,1024,768]{2,1,0:T(8,128)(2,1)S(1)}, bf16[1,1024,768]{2,1,0:T(8,128)(2,1)S(1)}, bf16[1,1024,768]{2,1,0:T(8,128)(2,1)S(1)}) custom-call(bf16[1,1024,768]{2,1,0:T(8,128)(2,1)S(1)} %copy-done.11, bf16[1,1024,768]{2,1,0:T(8,128)(2,1)S(1)} %get-tuple-element.138.k_ref, bf16[1,1024,768]{2,1,0:T(8,128)(2,1)S(1)} %get-tuple-element.137.v_ref, ...), custom_call_target="tpu_custom_call" | custom-call | flops 25999998976 | bytes 35000000 | tf_op jit(solution)/shard_map/cross_bwd/pallas_call | solution.py:210
  365.7 76.5 %self_bwd.1 = (bf16[1,1024,768]{2,1,0:T(8,128)(2,1)}, bf16[1,1024,768]{2,1,0:T(8,128)(2,1)}, bf16[1,1024,768]{2,1,0:T(8,128)(2,1)}, f32[1,12,768]{2,1,0:T(8,128)...) custom-call(bf16[1,1024,768]{2,1,0:T(8,128)(2,1)} %get-tuple-element.136.q_ref, ...), custom_call_target="tpu_custom_call" | custom-call | flops 121000001536 | bytes 40000000 | tf_op jit(solution)/shard_map/self_bwd/pallas_call | solution.py:149
  452.2 10.2 %convolution_convert_fusion.2 = bf16[768,3072]{1,0:T(8,128)(2,1)} fusion(bf16[1024,3072]{1,0:T(8,128)(2,1)} %fusion.6, f32[1024,768]{0,1:T(8,128)S(1)} %copy-done.13, f32[768]{0:T(1024)S(1)} %copy-done.29, f32[1024]{0:T(1024)S(1)} %copy-done.31), kind=kOutput, calls=%fused_computation.13 | convolution fusion | flops 4836556800 | bytes 14162944 | tf_op jit(solution)/shard_map/dot_general | solution.py:232
  462.4 12.3 %convolution_convert_fusion.1 = bf16[3072,768]{1,0:T(8,128)(2,1)} fusion(bf16[1024,768]{1,0:T(8,128)(2,1)} %bitcast.21, f32[1024,3072]{1,0:T(8,128)} %fusion.62), kind=kOutput, calls=%fused_computation.12 | convolution fusion | flops 4862509056 | bytes 18874368 | tf_op jit(solution)/shard_map/dot_general | solution.py:232
  492.0 8.5 copy.151
  500.6 11.5 %fusion.40 = bf16[1,1024,768]{1,2,0:T(8,128)(2,1)} fusion(f32[1024,768]{0,1:T(8,128)} %get-tuple-element.172, bf16[3072,768]{1,0:T(8,128)(2,1)} %all-gather.11.cloned.1.call-done, f32[1024,3072]{1,0:T(8,128)} %fusion.62), kind=kOutput, calls=%fused_computation.70 | convolution fusion | flops 4861722624 | bytes 22020096 | tf_op jit(solution)/shard_map/dot_general | solution.py:224
  512.0 8.3 copy.125
  520.9 12.4 %reduce.10 = bf16[1024,768]{1,0:T(8,128)(2,1)} reduce(bf16[1024,1,768]{2,1,0:T(2,128)(2,1)} %bitcast.125, bf16[]{:T(256)} %broadcast.157), dimensions={1}, to_apply=%bitcast.100.reduce_sub_computation | reduce | bytes 3145730
  541.6 8.6 multiply_reduce_fusion.2
  552.7 8.4 copy.130
  575.6 27.2 %all-to-all-done.4 = f32[1,1024,768]{2,0,1:T(1,128)} async-done(((f32[1,1024,768]{2,0,1:T(1,128)}), f32[1,1024,768]{2,0,1:T(1,128)}, u32[]{:S(2)}, u32[]{:S(2)}) %all-to-all-start.4) | async-done | bytes 3145760 | tf_op jit(solution)/shard_map/all_to_all | solution.py:268
  608.5 75.5 %all-reduce.5 = (f32[3,768]{1,0:T(4,128)S(1)}, f32[12,12]{0,1:T(8,128)S(1)}, f32[12,12]{1,0:T(8,128)}, f32[32,12]{0,1:T(8,128)}) all-reduce(f32[3,768]{1,0:T(4,128)S(1)} %pad_maximum_fusion.11, f32[12,12]{0,1:T(8,128)S(1)} %bitcast.141, f32[12,12]{1,0:T(8,128)S(1)} %reduce_sum.118, ...), channel_id=1, replica_groups=mesh['seq'=4,'dp'=8] {'seq','dp'}, use_global_device_ids=true, to_apply=%region_13.14 | all-reduce | flops 2976 | bytes 23808 | tf_op jit(solution)/shard_map/psum | solution.py:340
  701.9 98.8 %reduce-scatter.11.cloned.1.call-done = bf16[96,768]{1,0:T(8,128)(2,1)} async-done(((bf16[3072,768]{1,0:T(8,128)(2,1)}), bf16[96,768]{1,0:T(8,128)(2,1)}) %reduce-scatter.11.cloned.1.call-update) | async-done | bytes 147472 | tf_op jit(solution)/shard_map/reduce_scatter | solution.py:259
  802.3 115.8 %reduce-scatter.13.cloned.1.call-done = bf16[24,3840]{1,0:T(8,128)(2,1)} async-done(((bf16[768,3840]{1,0:T(8,128)(2,1)}), bf16[24,3840]{1,0:T(8,128)(2,1)}) %reduce-scatter.13.cloned.1.call-update) | async-done | bytes 184336
  (235 shorter events, 172.1 us)
Async XLA Ops:
  7.2 82.5 %all-gather.5.cloned.1.call-start = ((), (), s32[]{:S(2)}) async-start(), calls=%async_computation.10 | async-start | bytes 3852288 | tf_op jit(solution)/shard_map/all_gather | solution.py:255
  9.5 151.2 %all-gather.7.cloned.1.call-start = ((), (), s32[]{:S(2)}) async-start(), calls=%async_computation.11 | async-start | bytes 6082560 | tf_op jit(solution)/shard_map/all_gather | solution.py:255
  14.2 211.7 %all-gather.9.cloned.1.call-start = ((), (), s32[]{:S(2)}) async-start(), calls=%async_computation.12 | async-start | bytes 4866048 | tf_op jit(solution)/shard_map/all_gather | solution.py:255
  14.9 25.3 %all-to-all-start = ((bf16[4,256,768]{2,1,0:T(8,128)(2,1)}), bf16[4,256,768]{2,1,0:T(8,128)(2,1)S(1)}, u32[]{:S(2)}, u32[]{:S(2)}) async-start(bf16[4,256,768]{2,1,0:T(8,128)(2,1)} %param.21), calls=%async_computation | async-start | bytes 3145728 | tf_op jit(solution)/shard_map/all_to_all | solution.py:267
  20.1 271.2 %all-gather.11.cloned.1.call-start = ((), (), s32[]{:S(2)}) async-start(), calls=%async_computation.13 | async-start | bytes 4866048 | tf_op jit(solution)/shard_map/all_gather | solution.py:255
  40.2 26.5 %all-to-all-start.3 = ((bf16[4,256,768]{2,1,0:T(8,128)(2,1)}), bf16[4,256,768]{2,1,0:T(8,128)(2,1)}, u32[]{:S(2)}, u32[]{:S(2)}) async-start(bf16[4,256,768]{2,1,0:T(8,128)(2,1)} %param.23), calls=%async_computation.3 | async-start | bytes 3145728 | tf_op jit(solution)/shard_map/all_to_all | solution.py:267
  61.3 99.5 %copy-start.14 = (f32[1024,768]{0,1:T(8,128)}, f32[1024,768]{0,1:T(8,128)S(1)}, u32[]{:S(2)}) copy-start(f32[1024,768]{0,1:T(8,128)S(1)} %copy.149) | copy-start | bytes 9437188
  66.7 99.1 %all-to-all-start.1 = ((bf16[4,256,768]{2,1,0:T(8,128)(2,1)}), bf16[4,256,768]{2,1,0:T(8,128)(2,1)}, u32[]{:S(2)}, u32[]{:S(2)}) async-start(bf16[4,256,768]{2,1,0:T(8,128)(2,1)} %param.22), calls=%async_computation.1 | async-start | bytes 3145728 | tf_op jit(solution)/shard_map/all_to_all | solution.py:267
  71.1 627.7 %reduce-scatter.7.cloned.1.call-start = ((), (), s32[]{:S(2)}) async-start(), calls=%async_computation.14 | async-start | bytes 3649536 | tf_op jit(solution)/shard_map/reduce_scatter | solution.py:259
  91.3 225.1 %copy-start.28 = (f32[768]{0:T(1024)}, f32[768]{0:T(1024)S(1)}, u32[]{:S(2)}) copy-start(f32[768]{0:T(1024)S(1)} %get-tuple-element.127) | copy-start | bytes 9220
  91.3 268.8 %copy-start.40 = (f32[768]{0:T(1024)}, f32[768]{0:T(1024)S(1)}, u32[]{:S(2)}) copy-start(f32[768]{0:T(1024)S(1)} %get-tuple-element.128) | copy-start | bytes 9220
  165.7 194.4 %copy-start.42 = (f32[1024]{0:T(1024)}, f32[1024]{0:T(1024)S(1)}, u32[]{:S(2)}) copy-start(f32[1024]{0:T(1024)S(1)} %get-tuple-element.159) | copy-start | bytes 12292
  213.7 102.7 %copy-start.30 = (f32[1024]{0:T(1024)}, f32[1024]{0:T(1024)S(1)}, u32[]{:S(2)}) copy-start(f32[1024]{0:T(1024)S(1)} %get-tuple-element.161) | copy-start | bytes 12292
  317.2 42.9 %copy-start.24 = (f32[1024,768]{0,1:T(8,128)}, f32[1024,768]{0,1:T(8,128)S(1)}, u32[]{:S(2)}) copy-start(f32[1024,768]{0,1:T(8,128)S(1)} %subtract_add_fusion.1) | copy-start | bytes 9437188
  321.0 34.5 %copy-start.18 = (f32[1024,768]{0,1:T(8,128)S(1)}, f32[1024,768]{0,1:T(8,128)}, u32[]{:S(2)}) copy-start(f32[1024,768]{0,1:T(8,128)} %get-tuple-element.170) | copy-start | bytes 9437188
  365.7 76.5 %copy-start.15 = (f32[1024,768]{0,1:T(8,128)S(1)}, f32[1024,768]{0,1:T(8,128)}, u32[]{:S(2)}) copy-start(f32[1024,768]{0,1:T(8,128)} %copy-done.14) | copy-start | bytes 9437188
  365.7 76.5 %copy-start.37 = (f32[1,2,4,128]{3,1,2,0:T(2,128)S(1)}, f32[1,2,4,128]{3,1,2,0:T(2,128)}, u32[]{:S(2)}) copy-start(f32[1,2,4,128]{3,1,2,0:T(2,128)} %copy-done.36) | copy-start | bytes 12292
  365.7 76.6 %copy-start.39 = (f32[768]{0:T(1024)S(1)}, f32[768]{0:T(1024)}, u32[]{:S(2)}) copy-start(f32[768]{0:T(1024)} %copy-done.38) | copy-start | bytes 9220
  450.3 249.9 %reduce-scatter.9.cloned.1.call-start = ((), (), s32[]{:S(2)}) async-start(), calls=%async_computation.15 | async-start | bytes 4866048 | tf_op jit(solution)/shard_map/reduce_scatter | solution.py:259
  462.4 338.3 %reduce-scatter.11.cloned.1.call-start = ((), (), s32[]{:S(2)}) async-start(), calls=%async_computation.16 | async-start | bytes 4866048 | tf_op jit(solution)/shard_map/reduce_scatter | solution.py:259
  474.7 443.4 %reduce-scatter.13.cloned.1.call-start = ((), (), s32[]{:S(2)}) async-start(), calls=%async_computation.17 | async-start | bytes 6082560
  537.0 24.6 %all-to-all-start.2 = ((bf16[4,2,98304]{2,1,0:T(2,128)(2,1)}), bf16[4,2,98304]{2,1,0:T(2,128)(2,1)}, u32[]{:S(2)}, u32[]{:S(2)}) async-start(bf16[4,2,98304]{2,1,0:T(2,128)(2,1)} %reshape.251), calls=%async_computation.2 | async-start | bytes 3145728 | tf_op jit(solution)/shard_map/all_to_all | solution.py:268
  561.6 41.2 %all-to-all-start.4 = ((f32[1,1024,768]{2,0,1:T(1,128)}), f32[1,1024,768]{2,0,1:T(1,128)}, u32[]{:S(2)}, u32[]{:S(2)}) async-start(f32[1,1024,768]{2,0,1:T(1,128)} %copy.130), calls=%async_computation.4 | async-start | bytes 6291456 | tf_op jit(solution)/shard_map/all_to_all | solution.py:268
  602.8 94.0 %all-to-all-start.5 = ((f32[1,1024,768]{2,0,1:T(1,128)}), f32[1,1024,768]{2,0,1:T(1,128)S(1)}, u32[]{:S(2)}, u32[]{:S(2)}) async-start(f32[1,1024,768]{2,0,1:T(1,128)} %copy.131), calls=%async_computation.5 | async-start | bytes 6291456 | tf_op jit(solution)/shard_map/all_to_all | solution.py:268
  (40 other events, 439.7 us)
Sparse Core Ops, SparseCore 0:
  11.5 78.1 all-gather.4
  93.3 67.4 all-gather.6
  163.8 62.0 all-gather.8
  228.8 62.4 all-gather.10
  450.4 101.9 reduce-scatter.6
  557.7 130.3 reduce-scatter.8
  694.6 106.0 reduce-scatter.10
  806.3 111.7 reduce-scatter.12

commit v2 on v1

v2 whole, which is shorter than its diff:
```python
import functools

import jax
import jax.numpy as jnp
from jax import lax
from jax.experimental import pallas as pl
from jax.experimental.pallas import tpu as pltpu
from jax.sharding import PartitionSpec as P

F32 = jnp.float32
BF = jnp.bfloat16
NEG = -1e30
H, DH, D, L = 12, 64, 768, 1024
BLK = 256
NBK = L // BLK


def dot(a, b, ca, cb):
    return lax.dot_general(a, b, (((ca,), (cb,)), ((), ())), preferred_element_type=F32)


def toep_kernel(base_ref, out_ref):
    for d in range(NBK):
        row = jnp.broadcast_to(base_ref[0, d], (BLK, 2 * BLK))
        t = pltpu.roll(row, 0, 1, stride=1, stride_axis=0)[:, :BLK]
        if d == 0:
            a = lax.broadcasted_iota(jnp.int32, (BLK, BLK), 0)
            b = lax.broadcasted_iota(jnp.int32, (BLK, BLK), 1)
            t = jnp.where(a >= b, t, NEG)
        out_ref[0, d] = t


def toeplitz(base):
    return pl.pallas_call(
        toep_kernel, grid=(H,), in_specs=[pl.BlockSpec((1, NBK, 1, 2 * BLK), lambda h: (h, 0, 0, 0))],
        out_specs=pl.BlockSpec((1, NBK, BLK, BLK), lambda h: (h, 0, 0, 0)),
        out_shape=jax.ShapeDtypeStruct((H, NBK, BLK, BLK), F32), name="bias_tiles")(base)


def make_base(trow):
    rows = []
    for d in range(NBK):
        lo = d * BLK
        a = trow[:, max(lo - BLK + 1, 0):lo + 1][:, ::-1]
        if d == 0:
            a = jnp.concatenate([a, jnp.zeros((H, BLK - 1), F32)], 1)
        b = trow[:, lo + 1:lo + BLK][:, ::-1]
        rows.append(jnp.concatenate([a, jnp.zeros((H, 1), F32), b], 1))
    return jnp.stack(rows, 1)[:, :, None, :]


ANY = pl.BlockSpec(memory_space=pl.ANY)
VM = pl.BlockSpec(memory_space=pltpu.VMEM)
DMA = pltpu.SemaphoreType.DMA
EPS = 1e-6
GATE = 0.7978845608028654


def cst(shape):
    return pl.BlockSpec(shape, lambda *a: (0,) * len(shape), pipeline_mode=pl.Buffered(1))


def col(shape, j):
    return pl.BlockSpec(shape, lambda *a: (0, j), pipeline_mode=pl.Buffered(1))


def sds(shape, dt):
    return jax.ShapeDtypeStruct(shape, dt)


def rows8(v):
    return jnp.sum(v.reshape(v.shape[0] // 8, 8, v.shape[1]), 0)


def norm(x, g):
    return x * lax.rsqrt(jnp.mean(x * x, -1, keepdims=True) + EPS) * g


def norm_grad(x, g, dn):
    r = lax.rsqrt(jnp.mean(x * x, -1, keepdims=True) + EPS)
    gd = g * dn
    dx = r * gd - x * (r * r * r) * jnp.mean(gd * x, -1, keepdims=True)
    return dx, rows8(dn * x * r)


def gelu_pair(x):
    x2 = x * x
    t = jnp.tanh(x * (GATE + GATE * 0.044715 * x2))
    hp = 0.5 + 0.5 * t
    y = x * hp
    d = hp + 0.5 * x * (1.0 - t * t) * (GATE + 3 * GATE * 0.044715 * x2)
    return y, d


def blocks(n=NBK):
    return [slice(i * BLK, (i + 1) * BLK) for i in range(n)]


def self_fwd_kernel(st_ref, x_ref, w_ref, gn_ref, bias_ref, mpre_ref, mpost_ref,
                    q_ref, k_ref, v_ref, att_ref, gain_ref, p_ref, acc_ref, lo_ref):
    h = pl.program_id(0)

    @pl.when(h == 0)
    def _():
        acc_ref[...] = jnp.zeros_like(acc_ref)
        gt = gn_ref[...].astype(F32).T
        gain_ref[...] = gt[:8]
        g = gt[:1]
        for r in blocks():
            n1 = norm(x_ref[r, :].astype(F32), g).astype(BF)
            for j, o in enumerate((q_ref, k_ref, v_ref)):
                o[r, :] = dot(n1, w_ref[:, j * D:(j + 1) * D], 1, 0).astype(BF)
        pos = lax.broadcasted_iota(jnp.int32, (L, 128), 0)
        lo = jnp.zeros((L, 128), jnp.int32)
        for d in range(1, st_ref.shape[0]):
            sd = st_ref[d]
            lo = jnp.where(pos >= sd, sd, lo)
        lo_ref[...] = lo

    mp = mpre_ref[pl.ds(h, 1), :]
    mo = mpost_ref[pl.ds(h, 1), :]

    def scores(i):
        n = (i + 1) * BLK
        qm = (q_ref[i * BLK:n, :].astype(F32) * mp).astype(BF)
        return dot(qm, k_ref[:n, :], 1, 1)

    sc = scores(NBK - 1)
    for i in reversed(range(NBK)):
        nxt = scores(i - 1) if i else None
        n = (i + 1) * BLK
        r = slice(i * BLK, n)
        bias = jnp.concatenate([bias_ref[0, i - j] for j in range(i + 1)], 1) if i else bias_ref[0, 0]
        c = lax.broadcasted_iota(jnp.int32, (BLK, n), 1)
        sc = jnp.where(c >= lo_ref[r, :1], sc + bias, NEG)
        e = jnp.exp(sc - jnp.max(sc, 1, keepdims=True))
        p = (e * (1.0 / jnp.sum(e, 1, keepdims=True))).astype(BF)
        p_ref[0, r, :n] = p
        acc_ref[r, :] += dot(p, v_ref[:n, :], 1, 0) * mo
        sc = nxt

    @pl.when(h == H - 1)
    def _():
        att_ref[...] = acc_ref[...].astype(BF)


def self_fwd(starts, x, w1, bias, mpre, mpost):
    one = cst((L, D))
    return pl.pallas_call(
        self_fwd_kernel,
        grid_spec=pltpu.PrefetchScalarGridSpec(
            num_scalar_prefetch=1, grid=(H,),
            in_specs=[one, col((D, 3 * D), 0), col((D, 128), 18),
                      pl.BlockSpec((1, NBK, BLK, BLK), lambda h, st: (h, 0, 0, 0)), cst((H, D)), cst((H, D))],
            out_specs=[one] * 4 + [cst((8, D)), pl.BlockSpec((1, L, L), lambda h, st: (h, 0, 0))],
            scratch_shapes=[pltpu.VMEM((L, D), F32), pltpu.VMEM((L, 128), jnp.int32)]),
        out_shape=[sds((L, D), BF)] * 4 + [sds((8, D), F32), sds((H, L, L), BF)],
        compiler_params=pltpu.CompilerParams(vmem_limit_bytes=56 << 20),
        cost_estimate=pl.CostEstimate(flops=52_000_000_000, bytes_accessed=45_000_000, transcendentals=8_000_000),
        name="self_fwd")(starts, x, w1, w1, bias, mpre, mpost)


def cross_fwd_kernel(x_ref, att_ref, wo_ref, wq_ref, wk_ref, wv_ref, enc_ref, gain_ref,
                     h1_ref, n2_ref, q_ref, k_ref, v_ref, catt_ref, p_ref):
    h = pl.program_id(0)

    @pl.when(h == 0)
    def _():
        g = gain_ref[1:2, :]
        for r in blocks():
            h1 = x_ref[r, :].astype(F32) + dot(att_ref[r, :], wo_ref[...], 1, 0)
            h1_ref[r, :] = h1
            n2 = norm(h1, g).astype(BF)
            n2_ref[r, :] = n2
            q_ref[r, :] = dot(n2, wq_ref[...], 1, 0).astype(BF)
            k_ref[r, :] = dot(enc_ref[r, :], wk_ref[...], 1, 0).astype(BF)
            v_ref[r, :] = dot(enc_ref[r, :], wv_ref[...], 1, 0).astype(BF)

    cols = pl.ds(pl.multiple_of(h * 128, 128), 128)
    first = lax.broadcasted_iota(jnp.int32, (1, 128), 1) < DH
    k = k_ref[:, cols]
    v = v_ref[:, cols]
    steps = [(r, e) for r in blocks() for e in range(2)]

    def scores(r, e):
        q = q_ref[r, cols]
        return dot(jnp.where(first if e == 0 else ~first, q, jnp.zeros_like(q)), k, 1, 1)

    sc = scores(*steps[0])
    keep = None
    for n, (r, e) in enumerate(steps):
        nxt = scores(*steps[n + 1]) if n + 1 < len(steps) else None
        ex = jnp.exp(sc - jnp.max(sc, 1, keepdims=True))
        p = (ex * (1.0 / jnp.sum(ex, 1, keepdims=True))).astype(BF)
        p_ref[e, r, :] = p
        o = dot(p, v, 1, 0)
        if e == 0:
            keep = o
        else:
            catt_ref[r, cols] = jnp.where(first, keep, o).astype(BF)
        sc = nxt


def cross_fwd(x, att, wmid, enc, gains):
    one = cst((L, D))
    return pl.pallas_call(
        cross_fwd_kernel, grid=(H // 2,),
        in_specs=[one, one] + [col((D, D), j) for j in range(4)] + [one, cst((8, D))],
        out_specs=[one] * 6 + [pl.BlockSpec((2, L, L), lambda h: (h, 0, 0))],
        out_shape=[sds((L, D), F32)] + [sds((L, D), BF)] * 5 + [sds((H, L, L), BF)],
        compiler_params=pltpu.CompilerParams(vmem_limit_bytes=56 << 20),
        cost_estimate=pl.CostEstimate(flops=31_000_000_000, bytes_accessed=50_000_000, transcendentals=12_000_000),
        name="cross_fwd")(x, att, wmid, wmid, wmid, wmid, enc, gains)


def feed_kernel(h1_ref, catt_ref, wco_ref, cot_ref, gain_ref, fi_ref, fo_ref,
                out_ref, bh2_ref, bca_ref, gw_ref, dg_ref,
                n3, n3t, cott, acc, dn, inner, bi):
    a = pl.program_id(0)
    g = gain_ref[2:3, :]

    @pl.when(a == 0)
    def _():
        for r in blocks():
            h2 = h1_ref[r, :] + dot(catt_ref[r, :], wco_ref[...], 1, 0)
            bh2_ref[r, :] = h2
            acc[r, :] = h2
            n3[r, :] = norm(h2, g).astype(BF)
        n3t[...] = n3[...].T
        cott[...] = cot_ref[...].T
        dn[...] = jnp.zeros_like(dn)

    for r in blocks():
        u = dot(n3[r, :], fi_ref[...], 1, 0)
        y, d = gelu_pair(u)
        y = y.astype(BF)
        inner[r, :] = y
        gy = dot(cot_ref[r, :], fo_ref[...], 1, 1)
        b = (gy * d).astype(BF)
        bi[r, :] = b
        acc[r, :] += dot(y, fo_ref[...], 1, 0)
        dn[r, :] += dot(b, fi_ref[...], 1, 1)
    gw_ref[:, :D] = dot(n3t[...], bi[...], 1, 0).astype(BF)
    gw_ref[:, D:] = dot(cott[...], inner[...], 1, 0).T.astype(BF)

    @pl.when(a == pl.num_programs(0) - 1)
    def _():
        dg = jnp.zeros((8, D), F32)
        for r in blocks():
            out_ref[r, :] = acc[r, :].astype(BF)
            dx, s = norm_grad(bh2_ref[r, :], g, dn[r, :])
            dg = dg + s
            b2 = cot_ref[r, :].astype(F32) + dx
            bh2_ref[r, :] = b2
            bca_ref[r, :] = dot(b2.astype(BF), wco_ref[...], 1, 1).astype(BF)
        dg_ref[...] = dg


def feed(h1, catt, wmid, cot, gains, wfeed):
    one = cst((L, D))
    nf = wfeed.shape[1] // (2 * D)
    return pl.pallas_call(
        feed_kernel, grid=(nf,),
        in_specs=[one, one, col((D, D), 4), one, cst((8, D)),
                  pl.BlockSpec((D, D), lambda a: (0, 2 * a)), pl.BlockSpec((D, D), lambda a: (0, 2 * a + 1))],
        out_specs=[one, one, one, pl.BlockSpec((D, 2 * D), lambda a: (0, a)), cst((8, D))],
        out_shape=[sds((L, D), BF), sds((L, D), F32), sds((L, D), BF), sds((D, wfeed.shape[1]), BF), sds((8, D), F32)],
        scratch_shapes=[pltpu.VMEM((L, D), BF), pltpu.VMEM((D, L), BF), pltpu.VMEM((D, L), BF), pltpu.VMEM((L, D), F32),
                        pltpu.VMEM((L, D), F32), pltpu.VMEM((L, D), BF), pltpu.VMEM((L, D), BF)],
        compiler_params=pltpu.CompilerParams(vmem_limit_bytes=60 << 20),
        cost_estimate=pl.CostEstimate(flops=32_000_000_000, bytes_accessed=50_000_000, transcendentals=3_000_000),
        name="feed")(h1, catt, wmid, cot, gains, wfeed, wfeed)


def cross_bwd_kernel(q_ref, k_ref, v_ref, do_ref, p_ref, gain_ref,
                     n2_h, enc_h, att_h, catt_h, h1_h, bh2_h, w_h,
                     gw_ref, genc_ref, bh1_ref, bat_ref, dg_ref,
                     qt, dot_, ds, dq, dk, dv, n2, enc, att, catt, h1, bh2, w, sems):
    h = pl.program_id(0)
    late = [(n2_h, n2), (enc_h, enc), (att_h, att), (catt_h, catt), (h1_h, h1), (bh2_h, bh2)]
    late += [(w_h.at[:, pl.ds(0, 4 * D)], w)]
    copies = [pltpu.make_async_copy(a, b, sems.at[i]) for i, (a, b) in enumerate(late)]

    @pl.when(h == 0)
    def _():
        for c in copies:
            c.start()

    cols = pl.ds(pl.multiple_of(h * 128, 128), 128)
    first = lax.broadcasted_iota(jnp.int32, (1, 128), 1) < DH
    top = lax.broadcasted_iota(jnp.int32, (128, 1), 0) < DH
    k = k_ref[...]
    v = v_ref[...]
    qt[...] = q_ref[...].T
    dot_[...] = do_ref[...].T
    dks, dvs = [], []
    for e in range(2):
        fe = first if e == 0 else ~first
        for r in blocks():
            do = do_ref[r, :]
            dp = dot(jnp.where(fe, do, jnp.zeros_like(do)), v, 1, 1)
            p = p_ref[e, r, :].astype(F32)
            d = (p * (dp - jnp.sum(dp * p, 1, keepdims=True))).astype(BF)
            ds[e, r, :] = d
            o = dot(d, k, 1, 0).astype(BF)
            dq[r, cols] = o if e == 0 else jnp.where(first, dq[r, cols], o)
        dvs.append(dot(dot_[...], p_ref[e], 1, 0))
        dks.append(dot(qt[...], ds[e], 1, 0))
    dk[:, cols] = jnp.where(top, dks[0], dks[1]).T.astype(BF)
    dv[:, cols] = jnp.where(top, dvs[0], dvs[1]).T.astype(BF)

    @pl.when(h == H // 2 - 1)
    def _():
        for c in copies:
            c.wait()
        g = gain_ref[1:2, :]
        dg = jnp.zeros((8, D), F32)
        gw_ref[:, D:2 * D] = dot(n2[...], dq[...], 0, 0).astype(BF)
        gw_ref[:, 2 * D:3 * D] = dot(enc[...], dk[...], 0, 0).astype(BF)
        gw_ref[:, 3 * D:4 * D] = dot(enc[...], dv[...], 0, 0).astype(BF)
        for r in blocks():
            genc_ref[r, :] = (dot(dk[r, :], w[:, 2 * D:3 * D], 1, 1) + dot(dv[r, :], w[:, 3 * D:], 1, 1)).astype(genc_ref.dtype)
            dx, s = norm_grad(h1[r, :], g, dot(dq[r, :], w[:, D:2 * D], 1, 1))
            dg = dg + s
            b2 = bh2[r, :]
            b1 = b2 + dx
            bh1_ref[r, :] = b1
            b1 = b1.astype(BF)
            n2[r, :] = b1
            enc[r, :] = b2.astype(BF)
            bat_ref[r, :] = dot(b1, w[:, :D], 1, 1).astype(BF)
        gw_ref[:, :D] = dot(att[...], n2[...], 0, 0).astype(BF)
        gw_ref[:, 4 * D:] = dot(catt[...], enc[...], 0, 0).astype(BF)
        dg_ref[...] = dg


def cross_bwd(q, k, v, do, p, gains, n2, enc, att, catt, h1, bh2, wmid):
    one = cst((L, D))
    pair = pl.BlockSpec((L, 128), lambda h: (0, h))
    act = pltpu.VMEM((L, D), BF)
    return pl.pallas_call(
        cross_bwd_kernel, grid=(H // 2,),
        in_specs=[pair] * 4 + [pl.BlockSpec((2, L, L), lambda h: (h, 0, 0)), cst((8, D))] + [ANY] * 7,
        out_specs=[cst((D, 5 * D)), one, one, one, cst((8, D))],
        out_shape=[sds((D, 5 * D), BF), sds((L, D), BF), sds((L, D), F32), sds((L, D), BF), sds((8, D), F32)],
        scratch_shapes=[pltpu.VMEM((128, L), BF)] * 2 + [pltpu.VMEM((2, L, L), BF)] + [act] * 7
        + [pltpu.VMEM((L, D), F32)] * 2 + [pltpu.VMEM((D, 4 * D), BF), DMA((7,))],
        compiler_params=pltpu.CompilerParams(vmem_limit_bytes=60 << 20),
        cost_estimate=pl.CostEstimate(flops=37_000_000_000, bytes_accessed=70_000_000, transcendentals=0),
        name="cross_bwd")(q, k, v, do, p, gains, n2, enc, att, catt, h1, bh2, wmid)


def self_bwd_kernel(q_ref, k_ref, v_ref, ba_ref, p_ref, mpre_ref, mpost_ref, gain_ref, x_h, bh1_h, w_h,
                    gw_ref, gtok_ref, gpre_ref, gpost_ref, diag_ref, dg_ref,
                    qt, bat, dqa, dkt, dvt, dm, x, bh1, w, sems):
    h = pl.program_id(0)
    late = [(x_h, x), (bh1_h, bh1), (w_h.at[:, pl.ds(0, 3 * D)], w)]
    copies = [pltpu.make_async_copy(a, b, sems.at[i]) for i, (a, b) in enumerate(late)]

    @pl.when(h == 0)
    def _():
        for c in copies:
            c.start()
        qt[...] = q_ref[...].T
        bat[...] = ba_ref[...].T
        dqa[...] = jnp.zeros_like(dqa)
        dkt[...] = jnp.zeros_like(dkt)
        dvt[...] = jnp.zeros_like(dvt)

    mp = mpre_ref[pl.ds(h, 1), :]
    mo = mpost_ref[pl.ds(h, 1), :]
    gp = jnp.zeros((8, D), F32)
    dacc = [None] * NBK
    for i, r in enumerate(blocks()):
        n = (i + 1) * BLK
        bam = (ba_ref[r, :].astype(F32) * mo).astype(BF)
        dp = dot(bam, v_ref[:n, :], 1, 1)
        p = p_ref[0, r, :n].astype(F32)
        d = p * (dp - jnp.sum(dp * p, 1, keepdims=True))
        for j in range(i + 1):
            t = d[:, j * BLK:(j + 1) * BLK]
            dacc[i - j] = t if dacc[i - j] is None else dacc[i - j] + t
        db = d.astype(BF)
        dm[r, :n] = db
        rr = dot(db, k_ref[:n, :], 1, 0)
        dqa[r, :] += rr * mp
        gp = gp + rows8(rr * q_ref[r, :].astype(F32))
    gpre_ref[pl.ds(h, 1), :] = jnp.sum(gp, 0, keepdims=True)
    for t in range(NBK):
        y = jnp.concatenate([jnp.zeros((BLK, BLK), F32), dacc[t]], 1)
        n = BLK // 2
        while n >= 1:
            y = y[:n] + pltpu.roll(y[n:], 2 * BLK - n, 1)
            n //= 2
        diag_ref[0, t] = y
    mpc = jnp.broadcast_to(mp, (8, D)).T[:, :1]
    moc = jnp.broadcast_to(mo, (8, D)).T[:, :1]
    gq = jnp.zeros((8, D), F32)
    for c in blocks():
        i0 = c.start
        t = dot(bat[:, i0:], p_ref[0, i0:, c], 1, 0)
        dvt[:, c] += t * moc
        gq = gq + rows8(t.T * v_ref[c, :].astype(F32))
        u = dot(qt[:, i0:], dm[i0:, c], 1, 0)
        dkt[:, c] += u * mpc
    gpost_ref[pl.ds(h, 1), :] = jnp.sum(gq, 0, keepdims=True)

    @pl.when(h == H - 1)
    def _():
        for c in copies:
            c.wait()
        g = gain_ref[:1, :]
        dg = jnp.zeros((8, D), F32)
        for r in blocks():
            xr = x[r, :].astype(F32)
            n1 = norm(xr, g).astype(BF)
            dk = dkt[:, r].T.astype(BF)
            dv = dvt[:, r].T.astype(BF)
            dq = dqa[r, :].astype(BF)
            bat[:, r] = n1.T
            dm[r, :D] = dq
            dqa[r, :] = dk.astype(F32)
            back = dot(dq, w[:, :D], 1, 1) + dot(dk, w[:, D:2 * D], 1, 1) + dot(dv, w[:, 2 * D:], 1, 1)
            dx, s = norm_grad(xr, g, back)
            dg = dg + s
            gtok_ref[r, :] = (bh1[r, :] + dx).astype(gtok_ref.dtype)
        gw_ref[:, :D] = dot(bat[...], dm[:, :D], 1, 0).astype(BF)
        gw_ref[:, D:2 * D] = dot(bat[...], dqa[...].astype(BF), 1, 0).astype(BF)
        gw_ref[:, 2 * D:] = dot(bat[...], dvt[...].astype(BF), 1, 1).astype(BF)
        dg_ref[...] = dg


def self_bwd(q, k, v, ba, p, mpre, mpost, gains, x, bh1, w1):
    one = cst((L, D))
    return pl.pallas_call(
        self_bwd_kernel, grid=(H,),
        in_specs=[one] * 4 + [pl.BlockSpec((1, L, L), lambda h: (h, 0, 0)), cst((H, D)), cst((H, D)), cst((8, D))] + [ANY] * 3,
        out_specs=[cst((D, 3 * D)), one, cst((H, D)), cst((H, D)),
                   pl.BlockSpec((1, NBK, 1, 2 * BLK), lambda h: (h, 0, 0, 0)), cst((8, D))],
        out_shape=[sds((D, 3 * D), BF), sds((L, D), BF), sds((H, D), F32), sds((H, D), F32),
                   sds((H, NBK, 1, 2 * BLK), F32), sds((8, D), F32)],
        scratch_shapes=[pltpu.VMEM((D, L), BF)] * 2 + [pltpu.VMEM((L, D), F32)] + [pltpu.VMEM((D, L), F32)] * 2
        + [pltpu.VMEM((L, L), BF), pltpu.VMEM((L, D), BF), pltpu.VMEM((L, D), F32), pltpu.VMEM((D, 3 * D), BF), DMA((3,))],
        compiler_params=pltpu.CompilerParams(vmem_limit_bytes=60 << 20),
        cost_estimate=pl.CostEstimate(flops=128_000_000_000, bytes_accessed=50_000_000, transcendentals=0),
        name="self_bwd")(q, k, v, ba, p, mpre, mpost, gains, x, bh1, w1)


MESH = pl.DeviceIdType.MESH
NS, NZ, NCORE = 4, 4, 2
CHUNK = D


def place():
    s = lax.axis_index("seq")
    d = lax.axis_index("dp")
    return s, d // NCORE, d % NCORE


def flat(s, z, c):
    return (s * NZ + z) * NCORE + c


def partners(s, z, c):
    zs = [{"seq": s, "dp": ((z + k) % NZ) * NCORE + c} for k in (1, 2, 3)]
    ss = [{"seq": (s + k) % NS, "dp": z * NCORE + c} for k in (1, 2, 3)]
    return zs, ss, {"seq": s, "dp": z * NCORE + 1 - c}


def meet(devices):
    bar = pltpu.get_barrier_semaphore()
    for p in devices:
        pl.semaphore_signal(bar, inc=1, device_id=p, device_id_type=MESH)
    pl.semaphore_wait(bar, len(devices))


def remote(src, dst, ssem, rsem, dev):
    return pltpu.make_async_remote_copy(src, dst, ssem, rsem, device_id=dev, device_id_type=MESH)


def weights_in_kernel(w_ref, x_ref, out_ref, xo_ref, ssem, rsem, xs, xr, lsem):
    s, z, c = place()
    zs, ss, co = partners(s, z, c)
    own = flat(s, z, c)
    local = [pltpu.make_async_copy(w_ref, out_ref.at[own], lsem.at[0]),
             pltpu.make_async_copy(x_ref.at[s], xo_ref.at[s], lsem.at[1])]
    for cp in local:
        cp.start()
    meet(zs + ss + [co])
    sends = []

    def send(i, dev, src=None):
        n = len(sends)
        cp = remote(out_ref.at[i] if src is None else src, out_ref.at[i], ssem.at[n], rsem.at[i], dev)
        cp.start()
        sends.append(cp)

    def arrived(i):
        remote(out_ref.at[i], out_ref.at[i], ssem.at[0], rsem.at[i], co).wait_recv()

    for p in zs:
        send(own, p, w_ref)
    xc = []
    for k in (1, 2, 3):
        cp = remote(x_ref.at[(s + k) % NS], xo_ref.at[s], xs.at[k - 1], xr.at[k - 1], ss[k - 1])
        cp.start()
        xc.append(cp)
    for p in ss:
        send(own, p, w_ref)
    send(own, co, w_ref)
    for k in (1, 2, 3):
        i = flat(s, (z + NZ - k) % NZ, c)
        arrived(i)
        for p in ss:
            send(i, p)
        send(i, co)
    for kz in range(NZ):
        for k in (1, 2, 3):
            i = flat((s + NS - k) % NS, (z + NZ - kz) % NZ, c)
            arrived(i)
            send(i, co)
    for kz in range(NZ):
        for k in range(NS):
            arrived(flat((s + k) % NS, (z + kz) % NZ, 1 - c))
    for cp in xc:
        cp.wait_recv()
    for cp in sends + xc:
        cp.wait_send()
    for cp in local:
        cp.wait()


def weights_in(w, x, cid):
    r, n = w.shape
    return pl.pallas_call(
        weights_in_kernel, in_specs=[ANY, ANY], out_specs=[ANY, ANY],
        out_shape=[sds((NS * NZ * NCORE, r, n), w.dtype), sds(x.shape, x.dtype)],
        scratch_shapes=[DMA((31,)), DMA((32,)), DMA((3,)), DMA((3,)), DMA((2,))],
        compiler_params=pltpu.CompilerParams(collective_id=cid, has_side_effects=True),
        name="weights_in")(w, x)


def grads_out_kernel(n, *refs):
    gs, small = refs[:n], refs[n]
    outs, osmall = refs[n + 1:2 * n + 1], refs[2 * n + 1]
    rc, acc, rx, sz, rz, own, mc, mx, mz, cs, cr, xs, xr, zsm, zr, ms, mr = refs[2 * n + 2:]
    s, z, c = place()
    zs, ss, co = partners(s, z, c)
    chunks = [(g, o, pl.ds(j * CHUNK, CHUNK)) for g, o in zip(gs, outs) for j in range(g.shape[2] // CHUNK)]
    meet(zs + ss + [co])
    cs0 = remote(small, mc, ms.at[0], mr.at[0], co)
    cs0.start()
    order = [(k, kz) for k in (2, 1, 3, 0) for kz in (1, 2, 3, 0)]
    sent = [cs0]
    cc = []
    for q, (g, o, cols) in enumerate(chunks):
        cq = []
        for m, (k, kz) in enumerate(order):
            i = flat((s + k) % NS, (z + kz) % NZ, 1 - c)
            cp = remote(g.at[i, :, cols], rc.at[q, flat((s + k) % NS, (z + kz) % NZ, 0) // NCORE], cs.at[q, m],
                        cr.at[q, flat((s + k) % NS, (z + kz) % NZ, 0) // NCORE], co)
            cp.start()
            cq.append(cp)
        cc.append(cq)
        sent += cq
    cs0.wait_recv()
    mx[s] = small[...] + mc[...]
    mxs = []
    for k in (1, 2, 3):
        cp = remote(mx.at[s], mx.at[s], ms.at[k], mr.at[k], ss[k - 1])
        cp.start()
        mxs.append(cp)
    sent += mxs

    def xy_arrived(q, kz):
        g, o, cols = chunks[q]
        v = own[q % 2, kz]
        for k in (2, 1, 3):
            remote(acc.at[0, 0], rx.at[q, kz, k - 1], xs.at[0, 0], xr.at[q, kz, k - 1], ss[k - 1]).wait_recv()
            v = v + rx[q, kz, k - 1].astype(F32)
        if kz:
            sz[q, kz - 1] = v.astype(BF)
            cp = remote(sz.at[q, kz - 1], rz.at[q, kz - 1], zsm.at[q, kz - 1], zr.at[q, kz - 1], zs[kz - 1])
            cp.start()
            sent.append(cp)
        else:
            o[:, cols] = v

    for q, (g, o, cols) in enumerate(chunks):
        for m, (k, kz) in enumerate(order):
            js, jz = (s + k) % NS, (z + kz) % NZ
            cc[q][m].wait_recv()
            v = g[flat(js, jz, c), :, cols].astype(F32) + rc[q, js * NZ + jz].astype(F32)
            if k:
                acc[q, m] = v.astype(BF)
                cp = remote(acc.at[q, m], rx.at[q, kz, k - 1], xs.at[q, m], xr.at[q, kz, k - 1], ss[k - 1])
                cp.start()
                sent.append(cp)
            else:
                own[q % 2, kz] = v
        if q:
            for kz in (1, 2, 3, 0):
                xy_arrived(q - 1, kz)
        if q == 0:
            for cp in mxs:
                cp.wait_recv()
            mz[z] = (mx[0] + mx[1]) + (mx[2] + mx[3])
            mzs = []
            for k in (1, 2, 3):
                cp = remote(mz.at[z], mz.at[z], ms.at[3 + k], mr.at[3 + k], zs[k - 1])
                cp.start()
                mzs.append(cp)
            sent += mzs
    for kz in (1, 2, 3, 0):
        xy_arrived(len(chunks) - 1, kz)
    for cp in mzs:
        cp.wait_recv()
    osmall[...] = (mz[0] + mz[1]) + (mz[2] + mz[3])
    for q, (g, o, cols) in enumerate(chunks):
        for kz in (1, 2, 3):
            remote(sz.at[0, 0], rz.at[q, kz - 1], zsm.at[0, 0], zr.at[q, kz - 1], zs[0]).wait_recv()
            o[:, cols] += rz[q, kz - 1].astype(F32)
    for cp in sent:
        cp.wait_send()


def grads_out(gs, small, cid):
    r = gs[0].shape[1]
    q = sum(g.shape[2] for g in gs) // CHUNK
    sm = pltpu.VMEM(small.shape, F32)
    sm4 = pltpu.VMEM((4,) + small.shape, F32)
    return pl.pallas_call(
        functools.partial(grads_out_kernel, len(gs)),
        in_specs=[VM] * (len(gs) + 1), out_specs=[VM] * (len(gs) + 1),
        out_shape=[sds(g.shape[1:], F32) for g in gs] + [sds(small.shape, F32)],
        scratch_shapes=[pltpu.VMEM((q, 16, r, CHUNK), BF), pltpu.VMEM((q, 12, r, CHUNK), BF), pltpu.VMEM((q, 4, 3, r, CHUNK), BF),
                        pltpu.VMEM((q, 3, r, CHUNK), BF), pltpu.VMEM((q, 3, r, CHUNK), BF), pltpu.VMEM((2, 4, r, CHUNK), F32),
                        sm, sm4, sm4, DMA((q, 16)), DMA((q, 16)), DMA((q, 12)), DMA((q, 4, 3)), DMA((q, 3)), DMA((q, 3)),
                        DMA((7,)), DMA((7,))],
        compiler_params=pltpu.CompilerParams(collective_id=cid, has_side_effects=True, vmem_limit_bytes=56 << 20),
        name="grads_out")(*gs, small)


AX = ("seq", "dp")


def gather(w):
    return lax.all_gather(w, AX, axis=0, tiled=True)


def scatter(g):
    return lax.psum_scatter(g, AX, scatter_dimension=0, tiled=True).astype(F32)


def per_device(tokens, encoded, cotangent, doc_starts, rel_bucket, sq, sk, sv, so, cq, ck, cv, co, fi, fo,
               gs, gc, gf, mix_pre, mix_post, rel_table):
    nseq, ndp = lax.axis_size("seq"), lax.axis_size("dp")
    rows = sq.shape[0]
    nf = fo.shape[0] // rows
    ndev = nseq * ndp
    buckets = rel_table.shape[0]
    near = nseq == NS and ndp == NZ * NCORE and rows % 8 == 0
    to_stream = lambda x: lax.all_to_all(x, "seq", 0, 1, tiled=True).reshape(L, D)
    from_stream = lambda x: lax.all_to_all(x.reshape(1, L, D), "seq", 1, 0, tiled=True)
    gains = jnp.pad(jnp.stack([gs, gc, gf], 1), ((0, 0), (0, 125)))
    w1 = jnp.concatenate([sq, sk, sv, gains], 1)
    wmid = jnp.concatenate([so, cq, ck, cv, co], 1)
    wfeed = jnp.stack([fi.reshape(rows, D, nf).transpose(0, 2, 1), fo.reshape(rows, nf, D)], 2).reshape(rows, 2 * nf * D)
    if near:
        w1, x = weights_in(w1, tokens, 1)
        w1 = w1.reshape(D, -1)
        x = x.reshape(L, D)
    else:
        w1 = gather(w1)
        x = to_stream(tokens)
    wmid = gather(wmid)
    wfeed = gather(wfeed)
    enc = to_stream(encoded)
    cot = to_stream(cotangent)
    starts = lax.dynamic_index_in_dim(doc_starts, lax.axis_index("seq"), 0, keepdims=False)
    hot = (rel_bucket[:, None] == jnp.arange(buckets)[None, :]).astype(F32)
    trow = lax.dot_general(rel_table, hot, (((0,), (1,)), ((), ())), precision=lax.Precision.HIGHEST)
    bias = toeplitz(make_base(trow))
    mpre = jnp.repeat(mix_pre.T, DH, axis=1)
    mpost = jnp.repeat(mix_post, DH, axis=1)
    q, k, v, att, gain, p = self_fwd(starts, x, w1, bias, mpre, mpost)
    h1, n2, cqx, ckx, cvx, catt, cp = cross_fwd(x, att, wmid, enc, gain)
    out, bh2, bca, gw_feed, dgf = feed(h1, catt, wmid, cot, gain, wfeed)
    r_feed = scatter(gw_feed).reshape(rows, nf, 2, D)
    gw_mid, g_enc, bh1, bat, dgc = cross_bwd(cqx, ckx, cvx, bca, cp, gain, n2, enc, att, catt, h1, bh2, wmid)
    gw_qkv, g_tok, gpre, gpost, diag, dgs = self_bwd(q, k, v, bat, p, mpre, mpost, gain, x, bh1, w1)
    gpre = gpre.reshape(H, H, DH).sum(-1).T
    gpost = gpost.reshape(H, H, DH).sum(-1)
    dg = diag[:, :, 0, ::-1]
    gt = 0.0
    for d in range(NBK):
        gt = gt + jnp.pad(dg[:, d], ((0, 0), (d * BLK + 1, L - d * BLK - 1)))
    gt = gt[:, BLK:BLK + L]
    gtab = lax.dot_general(hot, gt, (((0,), (1,)), ((), ())), precision=lax.Precision.HIGHEST)
    dgain = jnp.stack([dgs.sum(0), dgc.sum(0), dgf.sum(0)])
    if near:
        parts = [dgain, gpre, gpost, gtab]
        vec = jnp.concatenate([a.reshape(-1) for a in parts])
        vec = jnp.pad(vec, (0, 3072 - vec.shape[0])).reshape(24, 128)
        r_mid, r_qkv, vec = grads_out([gw_mid.reshape(ndev, rows, -1), gw_qkv.reshape(ndev, rows, -1)], vec, 2)
        vec = vec.reshape(-1)
        o = 0
        got = []
        for a in parts:
            got.append(vec[o:o + a.size].reshape(a.shape))
            o += a.size
        dgain, gpre, gpost, gtab = got
    else:
        r_mid, r_qkv = scatter(gw_mid), scatter(gw_qkv)
        dgain, gpre, gpost, gtab = lax.psum((dgain, gpre, gpost, gtab), AX)
    me = lax.axis_index("seq") * ndp + lax.axis_index("dp")
    dgain = lax.dynamic_slice_in_dim(dgain, me * rows, rows, 1)
    m = lambda a, j: a[:, j * D:(j + 1) * D]
    return (from_stream(out), from_stream(g_tok).astype(F32), from_stream(g_enc).astype(F32),
            m(r_qkv, 0), m(r_qkv, 1), m(r_qkv, 2), m(r_mid, 0), m(r_mid, 1), m(r_mid, 2), m(r_mid, 3), m(r_mid, 4),
            r_feed[:, :, 0].transpose(0, 2, 1).reshape(rows, nf * D), r_feed[:, :, 1].reshape(rows * nf, D),
            dgain[0], dgain[1], dgain[2], gpre, gpost, gtab)


def solution(mesh):
    act = P("dp", "seq", None)
    w = P(AX, None)
    g = P(AX)
    return jax.shard_map(
        per_device, mesh=mesh, in_specs=(act, act, act, P("dp", None), P()) + (w,) * 10 + (g,) * 3 + (P(),) * 3,
        out_specs=(act,) * 3 + (w,) * 10 + (g,) * 3 + (P(),) * 3, check_vma=False)
```

time: 937 us -> 586 us (0.63)
  waiting for transfers between devices: 354 us -> 11.1 us
  Pallas kernels: 208 us -> 423 us
  matrix products: 140 us -> 1.08 us
  blocking collectives: 75.5 us -> 0 us
  local copies, waits for them, and re-layouts: 81.1 us -> 66.8 us
    pallas_call x3 -> x6, Pallas kernels: 144 us -> 353 us  [the longest x1 84.7 us: self_bwd(): pl.pallas_call(self_bwd_kernel, grid=(H,), in_specs=[one] * 4 + [pl.Block...]
    dot_general x21 -> x0, matrix products: 139 us -> none  [the longest x7 51.2 us: mm_t(): lax.dot_general(a, b, (((1,), (1,)), ((), ())), preferred_element_type=F32)]
    unnamed x9 -> x3, waiting for transfers between devices: 117 us -> 0.05 us
    reduce_scatter x3 -> x1, waiting for transfers between devices: 98.8 us -> 0.01 us  [scatter(): return lax.psum_scatter(g, AX, scatter_dimension=0, tiled=True).astype(F32)]
    all_gather x4 -> x2, waiting for transfers between devices: 88.7 us -> 10.8 us  [gather(): return lax.all_gather(w, AX, axis=0, tiled=True)]
    psum x1 -> x0, blocking collectives: 75.5 us -> none  [per_device(): lax.psum((gpre, gpost, gtab, jnp.stack([d_gs, d_gc, d_gf])), AX)]
    all_to_all x6 -> x5, waiting for transfers between devices: 49.2 us -> 0.3 us  [the longest x3 0.3 us: per_device(): lax.all_to_all(x.reshape(1, L, D), 'seq', 1, 0, tiled=True)]
    unnamed x2 -> x3, other arithmetic: 12.4 us -> 36.1 us
  transfers between devices with their start and end apart: 14 -> 8, of which waited for: 10 -> 2; matrix products, arithmetic and copies ran while one was open for 20% -> 16% of each run, Pallas kernels for 10% -> 66%
where the time goes in v2:
time: 586 us; the launch traced here: 576 us
  Pallas kernels  423 us (72%)
  local copies, waits for them, and re-layouts  66.8 us (11%)
  other arithmetic  37.3 us (6%)
  starting transfers between devices  22.6 us (4%)
  between operations  14.5 us (2%)
  waiting for transfers between devices  11.1 us (2%)
    pallas_call x1, Pallas kernels, self_bwd(): pl.pallas_call(self_bwd_kernel, grid=(H,), in_specs=[one] * 4 + [pl.Block...  84.7 us
    pallas_call x1, Pallas kernels, grads_out(): pl.pallas_call(functools.partial(grads_out_kernel, len(gs)), in_specs=[VM...  78.9 us
    pallas_call x1, Pallas kernels, self_fwd(): pl.pallas_call(self_fwd_kernel, grid_spec=pltpu.PrefetchScalarGridSpec(nu...  60 us
    pallas_call x1, Pallas kernels, weights_in(): pl.pallas_call(weights_in_kernel, in_specs=[ANY, ANY], out_specs=[ANY, AN...  57.3 us
    pallas_call x1, Pallas kernels, cross_bwd(): pl.pallas_call(cross_bwd_kernel, grid=(H // 2,), in_specs=[pair] * 4 + [p...  52.5 us
    pallas_call x1, Pallas kernels, feed(): pl.pallas_call(feed_kernel, grid=(nf,), in_specs=[one, one, col((D, D), 4...  44.4 us
    unnamed x3, other arithmetic  36.1 us
    unnamed x69, local copies, waits for them, and re-layouts  35.8 us
  transfers between devices with their start and end apart: 8, of which 2 were waited for; matrix products, arithmetic and copies ran while one was open for 16% of the time, Pallas kernels for 66%

profile of v2, /device:TPU:0, one launch (start us, length us, event | category | flops | bytes accessed | tf_op | source)
XLA Modules:
  0.0 576.4 jit_solution(17430111643244639065)
XLA Ops:
  15.9 5.3 all-to-all-start
  26.2 9.5 %bias_tiles.1.bias_ref = f32[12,4,256,256]{3,2,1,0:T(8,128)} custom-call(f32[12,4,1,512]{3,2,1,0:T(1,128)} %broadcast_in_dim.15.base_ref), custom_call_target="tpu_custom_call" | custom-call | tf_op jit(solution)/shard_map/bias_tiles/pallas_call | solution.py:34
  36.4 57.3 %weights_in.1 = (bf16[32,24,2432]{2,1,0:T(8,128)(2,1)}, bf16[4,256,768]{2,1,0:T(8,128)(2,1)}) custom-call(bf16[24,2432]{1,0:T(8,128)(2,1)} %fusion.6.w_ref, bf16[4,256,768]{2,1,0:T(8,128)(2,1)} %x_ref.1), custom_call_target="tpu_custom_call" | custom-call | tf_op jit(solution)/shard_map/weights_in/pallas_call | solution.py:535
  94.9 60.0 %self_fwd.1 = (bf16[1024,768]{1,0:T(8,128)(2,1)}, bf16[1024,768]{1,0:T(8,128)(2,1)}, bf16[1024,768]{1,0:T(8,128)(2,1)}, bf16[1024,768]{1,0:T(8,128)(2,1)}, f32[8...) custom-call(s32[4]{0:T(128)} %dynamic-slice_bitcast_fusion.st_ref, bf16[1024,768]{1,0:T(8,128)(2,1)} %bitcast.108, ...), custom_call_target="tpu_custom_call" | custom-call | flops 51999997952 | bytes 45000000 | tf_op jit(solution)/shard_map/self_fwd/pallas_call | solution.py:149
  156.2 3.6 all-to-all-start.1
  160.3 35.5 %cross_fwd.1 = (f32[1024,768]{1,0:T(8,128)}, bf16[1024,768]{1,0:T(8,128)(2,1)}, bf16[1024,768]{1,0:T(8,128)(2,1)}, bf16[1024,768]{1,0:T(8,128)(2,1)}, bf16[1024,...) custom-call(bf16[1024,768]{1,0:T(8,128)(2,1)} %bitcast.109, ...), custom_call_target="tpu_custom_call" | custom-call | flops 31000000512 | bytes 50000000 | tf_op jit(solution)/shard_map/cross_fwd/pallas_call | solution.py:206
  195.8 10.8 %all-gather.5.cloned.1.call-done.fi_ref.fo_ref = bf16[768,6144]{1,0:T(8,128)(2,1)} async-done(((bf16[24,6144]{1,0:T(8,128)(2,1)}), bf16[768,6144]{1,0:T(8,128)(2,1)}) %all-gather.5.cloned.1.call-update) | async-done | bytes 9437200 | tf_op jit(solution)/shard_map/all_gather | solution.py:648
  206.6 44.4 %feed.1 = (bf16[1024,768]{1,0:T(8,128)(2,1)}, f32[1024,768]{1,0:T(8,128)}, bf16[1024,768]{1,0:T(8,128)(2,1)}, bf16[768,6144]{1,0:T(8,128)(2,1)}, f32[8,768]{1,0:T(8,128)}) custom-call(f32[1024,768]{1,0:T(8,128)} %get-tuple-element.57.h1_ref.h1_h, bf16[1024,768]{1,0:T(8,128)(2,1)} %get-tuple-element.58.catt_ref.catt_h, ...), custom_call_target="tpu_custom_call" | custom-call | flops 32000000000 | bytes 50000000 | tf_op jit(solution)/shard_map/feed/pallas_call | solution.py:262
  251.0 52.5 %cross_bwd.1 = (bf16[768,3840]{1,0:T(8,128)(2,1)}, bf16[1024,768]{1,0:T(8,128)(2,1)}, f32[1024,768]{1,0:T(8,128)}, bf16[1024,768]{1,0:T(8,128)(2,1)}, f32[8,768]{1,0:T(8,128)}) custom-call(bf16[1024,768]{1,0:T(8,128)(2,1)} %get-tuple-element.63.q_ref, bf16[1024,768]{1,0:T(8,128)(2,1)} %get-tuple-element.64.k_ref, bf16[1024,768]{1,0:T(8,128)(2,1)} %get-tuple-element.65.v_ref, ...), custom_call_target="tpu_custom_call" | custom-call | flops 36999999488 | bytes 70000000 | tf_op jit(solution)/shard_map/cross_bwd/pallas_call | solution.py:341
  303.5 84.7 %self_bwd.1 = (bf16[768,2304]{1,0:T(8,128)(2,1)}, bf16[1024,768]{1,0:T(8,128)(2,1)}, f32[12,768]{1,0:T(8,128)}, f32[12,768]{1,0:T(8,128)}, f32[12,4,1,512]{3,2,1,0:T(1,128)}, /*index=5*/f32[8,768]{1,0:T(8,128)}) custom-call(bf16[1024,768]{1,0:T(8,128)(2,1)} %get-tuple-element.60.q_ref, bf16[1024,768]{1,0:T(8,128)(2,1)} %get-tuple-element.61.k_ref, ...), custom_call_target="tpu_custom_call" | custom-call | flops 128000000000 | bytes 50000000 | tf_op jit(solution)/shard_map/self_bwd/pallas_call | solution.py:435
  388.2 3.8 copy.150
  392.6 12.0 %reduce.3 = bf16[1024,768]{1,0:T(8,128)(2,1)} reduce(bf16[1024,1,768]{2,1,0:T(2,128)(2,1)S(1)} %bitcast.74, bf16[]{:T(256)} %broadcast.29), dimensions={1}, to_apply=%bitcast.71.reduce_sub_computation | reduce | bytes 3145730
  404.6 3.7 reshape.174
  408.3 4.4 all-to-all-start.3
  412.6 3.8 copy.151
  416.5 12.2 %reduce.2 = bf16[1024,768]{1,0:T(8,128)(2,1)} reduce(bf16[1024,1,768]{2,1,0:T(2,128)(2,1)S(1)} %bitcast.76, bf16[]{:T(256)} %broadcast.29), dimensions={1}, to_apply=%bitcast.72.reduce_sub_computation | reduce | bytes 3145730
  428.7 3.7 reshape.178
  432.7 4.3 all-to-all-start.2
  438.0 3.8 copy.149
  441.8 12.0 %reduce.4 = bf16[1024,768]{1,0:T(8,128)(2,1)} reduce(bf16[1024,1,768]{2,1,0:T(2,128)(2,1)S(1)} %bitcast.75, bf16[]{:T(256)} %broadcast.29), dimensions={1}, to_apply=%bitcast.70.reduce_sub_computation | reduce | bytes 3145730
  453.8 3.7 reshape.176
  458.3 4.5 all-to-all-start.4
  464.3 78.9 %grads_out.1 = (f32[24,3840]{1,0:T(8,128)}, f32[24,2304]{1,0:T(8,128)}, f32[24,128]{1,0:T(8,128)}) custom-call(bf16[32,24,3840]{2,1,0:T(8,128)(2,1)} %bitcast.81, bf16[32,24,2304]{2,1,0:T(8,128)(2,1)} %bitcast.82, f32[24,128]{1,0:T(8,128)} %pad_bitcast_fusion.refs_2_), custom_call_target="tpu_custom_call" | custom-call | tf_op jit(solution)/shard_map/grads_out/pallas_call | solution.py:632
  559.5 3.1 reshape.177
  (145 shorter events, 44.3 us)
Async XLA Ops:
  7.2 14.4 %copy-start = (f32[32,12]{0,1:T(8,128)S(1)}, f32[32,12]{0,1:T(8,128)}, u32[]{:S(2)}) copy-start(f32[32,12]{0,1:T(8,128)} %param.41) | copy-start | bytes 4612
  7.2 153.1 %all-gather.3.cloned.1.call-start = ((), (), s32[]{:S(2)}) async-start(), calls=%async_computation.6 | async-start | bytes 6082560 | tf_op jit(solution)/shard_map/all_gather | solution.py:648
  11.8 194.8 %all-gather.5.cloned.1.call-start = ((), (), s32[]{:S(2)}) async-start(), calls=%async_computation.7 | async-start | bytes 9732096 | tf_op jit(solution)/shard_map/all_gather | solution.py:648
  15.9 5.5 copy-start.16
  15.9 5.4 copy-start.17
  15.9 5.4 copy-start.18
  15.9 5.6 copy-start.14
  15.9 5.6 copy-start.19
  15.9 139.0 %all-to-all-start = ((bf16[4,256,768]{2,1,0:T(8,128)(2,1)}), bf16[4,256,768]{2,1,0:T(8,128)(2,1)S(1)}, u32[]{:S(2)}, u32[]{:S(2)}) async-start(bf16[4,256,768]{2,1,0:T(8,128)(2,1)} %param.22), calls=%async_computation | async-start | bytes 3145728 | tf_op jit(solution)/shard_map/all_to_all | solution.py:663
  26.2 9.5 %copy-start.8 = (bf16[24,768]{1,0:T(8,128)(2,1)S(1)}, bf16[24,768]{1,0:T(8,128)(2,1)}, u32[]{:S(2)}) copy-start(bf16[24,768]{1,0:T(8,128)(2,1)} %param.28) | copy-start | bytes 110596
  26.2 9.5 %copy-start.9 = (bf16[24,768]{1,0:T(8,128)(2,1)S(1)}, bf16[24,768]{1,0:T(8,128)(2,1)}, u32[]{:S(2)}) copy-start(bf16[24,768]{1,0:T(8,128)(2,1)} %param.27) | copy-start | bytes 110596
  26.2 9.5 %copy-start.10 = (bf16[24,768]{1,0:T(8,128)(2,1)S(1)}, bf16[24,768]{1,0:T(8,128)(2,1)}, u32[]{:S(2)}) copy-start(bf16[24,768]{1,0:T(8,128)(2,1)} %param.26) | copy-start | bytes 110596
  156.2 39.6 %all-to-all-start.1 = ((bf16[4,256,768]{2,1,0:T(8,128)(2,1)}), bf16[4,256,768]{2,1,0:T(8,128)(2,1)S(1)}, u32[]{:S(2)}, u32[]{:S(2)}) async-start(bf16[4,256,768]{2,1,0:T(8,128)(2,1)} %param.23), calls=%async_computation.1 | async-start | bytes 3145728 | tf_op jit(solution)/shard_map/all_to_all | solution.py:663
  159.7 404.6 %reduce-scatter.2.cloned.1.call-start = ((), (), s32[]{:S(2)}) async-start(), calls=%async_computation.8 | async-start | bytes 9732096 | tf_op jit(solution)/shard_map/reduce_scatter | solution.py:652
  195.8 10.8 %copy-start.3 = (bf16[4,256,768]{2,1,0:T(8,128)(2,1)}, bf16[4,256,768]{2,1,0:T(8,128)(2,1)S(1)}, u32[]{:S(2)}) copy-start(bf16[4,256,768]{2,1,0:T(8,128)(2,1)S(1)} %all-to-all-done.1) | copy-start | bytes 4718596
  408.3 24.4 %all-to-all-start.3 = ((bf16[4,2,98304]{2,1,0:T(2,128)(2,1)}), bf16[4,2,98304]{2,1,0:T(2,128)(2,1)}, u32[]{:S(2)}, u32[]{:S(2)}) async-start(bf16[4,2,98304]{2,1,0:T(2,128)(2,1)} %reshape.174), calls=%async_computation.3 | async-start | bytes 3145728 | tf_op jit(solution)/shard_map/all_to_all | solution.py:664
  432.4 4.7 copy-start.13
  432.4 4.7 copy-start.12
  432.4 4.8 copy-start.11
  432.4 4.8 copy-start.5
  432.7 25.6 %all-to-all-start.2 = ((bf16[4,2,98304]{2,1,0:T(2,128)(2,1)}), bf16[4,2,98304]{2,1,0:T(2,128)(2,1)}, u32[]{:S(2)}, u32[]{:S(2)}) async-start(bf16[4,2,98304]{2,1,0:T(2,128)(2,1)} %reshape.178), calls=%async_computation.2 | async-start | bytes 3145728 | tf_op jit(solution)/shard_map/all_to_all | solution.py:664
  458.3 4.5 copy-start.7
  458.3 4.9 copy-start.6
  458.3 101.2 %all-to-all-start.4 = ((bf16[4,2,98304]{2,1,0:T(2,128)(2,1)}), bf16[4,2,98304]{2,1,0:T(2,128)(2,1)}, u32[]{:S(2)}, u32[]{:S(2)}) async-start(bf16[4,2,98304]{2,1,0:T(2,128)(2,1)} %reshape.176), calls=%async_computation.4 | async-start | bytes 3145728 | tf_op jit(solution)/shard_map/all_to_all | solution.py:664
  (5 other events, 11.8 us)
Sparse Core Ops, SparseCore 0:
  11.9 93.3 all-gather.2
  108.9 97.6 all-gather.4
  251.2 133.3 reduce-scatter.1

commit v3 on v2

--- a/solution.py
+++ b/solution.py
@@ -52,6 +52,300 @@
 ANY = pl.BlockSpec(memory_space=pl.ANY)
 VM = pl.BlockSpec(memory_space=pltpu.VMEM)
 DMA = pltpu.SemaphoreType.DMA
+MESH = pl.DeviceIdType.MESH
+NS, NZ, NCORE = 4, 4, 2
+ND = NS * NZ * NCORE
+
+
+def sds(shape, dt):
+    return jax.ShapeDtypeStruct(shape, dt)
+
+
+def params(mib, cid):
+    if cid is None:
+        return pltpu.CompilerParams(vmem_limit_bytes=mib << 20)
+    return pltpu.CompilerParams(vmem_limit_bytes=mib << 20, collective_id=cid, has_side_effects=True)
+
+
+def split(refs, n, *groups):
+    out = list(refs[:n])
+    for g in groups:
+        out.append(refs[n:n + g])
+        n += g
+    return out
+
+
+def place():
+    s = lax.axis_index("seq")
+    d = lax.axis_index("dp")
+    return s, d // NCORE, d % NCORE
+
+
+def flat(s, z, c):
+    return (s * NZ + z) * NCORE + c
+
+
+def partners(s, z, c):
+    zs = [{"seq": s, "dp": ((z + k) % NZ) * NCORE + c} for k in (1, 2, 3)]
+    ss = [{"seq": (s + k) % NS, "dp": z * NCORE + c} for k in (1, 2, 3)]
+    return zs, ss, {"seq": s, "dp": z * NCORE + 1 - c}
+
+
+def meet(devices):
+    bar = pltpu.get_barrier_semaphore()
+    for p in devices:
+        pl.semaphore_signal(bar, inc=1, device_id=p, device_id_type=MESH)
+    pl.semaphore_wait(bar, len(devices))
+
+
+def meet_all():
+    zs, ss, co = partners(*place())
+    meet(zs + ss + [co])
+
+
+def meet_seq():
+    meet(partners(*place())[1])
+
+
+def remote(src, dst, ssem, rsem, dev):
+    return pltpu.make_async_remote_copy(src, dst, ssem, rsem, device_id=dev, device_id_type=MESH)
+
+
+class Exchange:
+    def __init__(self, src, dst, ss, rs, ls):
+        self.s, z, c = place()
+        self.src, self.dst, self.ss, self.rs, self.ls = src, dst, ss, rs, ls
+        self.to = partners(self.s, z, c)[1]
+
+    @staticmethod
+    def sems():
+        return [DMA((3,)), DMA((3,)), DMA(())]
+
+    def local(self):
+        return pltpu.make_async_copy(self.src.at[self.s], self.dst.at[self.s], self.ls)
+
+    def copy(self, k):
+        return remote(self.src.at[(self.s + k) % NS], self.dst.at[self.s], self.ss.at[k - 1], self.rs.at[k - 1], self.to[k - 1])
+
+    def start(self):
+        for k in (2, 1, 3):
+            self.copy(k).start()
+        self.local().start()
+
+    def end(self):
+        for k in (1, 2, 3):
+            self.copy(k).wait_recv()
+            self.copy(k).wait_send()
+        self.local().wait()
+
+
+class Gather:
+    def __init__(self, w, out, ssem, rsem, lsem):
+        self.w, self.out, self.ssem, self.rsem, self.lsem = w, out, ssem, rsem, lsem
+        self.s, self.z, self.c = place()
+        self.zs, self.ss, self.co = partners(self.s, self.z, self.c)
+        self.own = flat(self.s, self.z, self.c)
+
+    @staticmethod
+    def sems():
+        return [DMA((ND - 1,)), DMA((ND,)), DMA(())]
+
+    def send(self, i, dev, n, src=None):
+        remote(self.out.at[i] if src is None else src, self.out.at[i], self.ssem.at[n], self.rsem.at[i], dev).start()
+
+    def got(self, i):
+        remote(self.out.at[i], self.out.at[i], self.ssem.at[0], self.rsem.at[i], self.co).wait_recv()
+
+    def local(self):
+        return pltpu.make_async_copy(self.w, self.out.at[self.own], self.lsem)
+
+    def start(self):
+        for k in range(3):
+            self.send(self.own, self.zs[k], k, self.w)
+        for k in range(3):
+            self.send(self.own, self.ss[k], 3 + k, self.w)
+        self.send(self.own, self.co, 6, self.w)
+        self.local().start()
+
+    def line(self, k):
+        i = flat(self.s, (self.z + NZ - k) % NZ, self.c)
+        self.got(i)
+        for j in range(3):
+            self.send(i, self.ss[j], 4 * k + 3 + j)
+        self.send(i, self.co, 4 * k + 6)
+
+    def plane(self, kz):
+        for k in (1, 2, 3):
+            i = flat((self.s + NS - k) % NS, (self.z + NZ - kz) % NZ, self.c)
+            self.got(i)
+            self.send(i, self.co, 19 + 3 * kz + k - 1)
+
+    def end(self):
+        for kz in range(NZ):
+            for k in range(NS):
+                self.got(flat((self.s + k) % NS, (self.z + kz) % NZ, 1 - self.c))
+        for n in range(ND - 1):
+            remote(self.w, self.out.at[self.own], self.ssem.at[n], self.rsem.at[0], self.co).wait_send()
+        self.local().wait()
+
+
+ORDER = [(k, kz) for k in (2, 1, 3, 0) for kz in (1, 2, 3, 0)]
+
+
+class Scatter:
+    def __init__(self, g, out, mine, rc, acc, rx, own, sz, rz, lsem, cs, cr, xs, xr, zsem, zr):
+        self.g, self.out = g, out
+        self.mine, self.rc, self.acc, self.rx, self.own, self.sz, self.rz = mine, rc, acc, rx, own, sz, rz
+        self.lsem, self.cs, self.cr, self.xs, self.xr, self.zsem, self.zr = lsem, cs, cr, xs, xr, zsem, zr
+        self.s, self.z, self.c = place()
+        self.zs, self.ss, self.co = partners(self.s, self.z, self.c)
+
+    @staticmethod
+    def bufs(shape):
+        b = tuple(shape[1:])
+        v = lambda *n: pltpu.VMEM(n + b, BF)
+        return [v(16), v(16), v(12), v(4, 3), pltpu.VMEM((4,) + b, F32), v(3), v(3),
+                DMA((16,)), DMA((16,)), DMA((16,)), DMA((12,)), DMA((4, 3)), DMA((3,)), DMA((3,))]
+
+    def dest(self, m):
+        k, kz = ORDER[m]
+        return (self.s + k) % NS, (self.z + kz) % NZ
+
+    def core(self, m):
+        js, jz = self.dest(m)
+        return remote(self.g.at[flat(js, jz, 1 - self.c)], self.rc.at[js * NZ + jz], self.cs.at[m], self.cr.at[js * NZ + jz], self.co)
+
+    def load(self, m):
+        js, jz = self.dest(m)
+        return pltpu.make_async_copy(self.g.at[flat(js, jz, self.c)], self.mine.at[m], self.lsem.at[m])
+
+    def xy(self, m):
+        k, kz = ORDER[m]
+        return remote(self.acc.at[m], self.rx.at[kz, k - 1], self.xs.at[m], self.xr.at[kz, k - 1], self.ss[k - 1])
+
+    def zz(self, kz):
+        return remote(self.sz.at[kz - 1], self.rz.at[kz - 1], self.zsem.at[kz - 1], self.zr.at[kz - 1], self.zs[kz - 1])
+
+    def start(self):
+        for m in range(16):
+            self.core(m).start()
+        for m in range(16):
+            self.load(m).start()
+
+    def plane(self, lo, hi):
+        for m in range(lo, hi):
+            k, kz = ORDER[m]
+            js, jz = self.dest(m)
+            self.load(m).wait()
+            remote(self.mine.at[0], self.rc.at[js * NZ + jz], self.cs.at[m], self.cr.at[js * NZ + jz], self.co).wait_recv()
+            v = self.mine[m].astype(F32) + self.rc[js * NZ + jz].astype(F32)
+            if k:
+                self.acc[m] = v.astype(BF)
+                self.xy(m).start()
+            else:
+                self.own[kz] = v
+
+    def line(self, lo, hi):
+        for kz in (1, 2, 3, 0)[lo:hi]:
+            v = self.own[kz]
+            for k in (2, 1, 3):
+                remote(self.acc.at[0], self.rx.at[kz, k - 1], self.xs.at[0], self.xr.at[kz, k - 1], self.ss[k - 1]).wait_recv()
+                v = v + self.rx[kz, k - 1].astype(F32)
+            if kz:
+                self.sz[kz - 1] = v.astype(BF)
+                self.zz(kz).start()
+            else:
+                self.own[0] = v
+
+    def end(self):
+        v = self.own[0]
+        for kz in (1, 2, 3):
+            self.zz(kz).wait_recv()
+            v = v + self.rz[kz - 1].astype(F32)
+        self.out[...] = v
+        for m in range(16):
+            self.core(m).wait_send()
+        for m in range(12):
+            self.xy(m).wait_send()
+        for kz in (1, 2, 3):
+            self.zz(kz).wait_send()
+
+
+def weights_in_kernel(w_ref, x_ref, out_ref, xo_ref, ga, gb, gc, xa, xb, xc):
+    gat = Gather(w_ref, out_ref, ga, gb, gc)
+    exc = Exchange(x_ref, xo_ref, xa, xb, xc)
+    meet_all()
+    gat.start()
+    exc.start()
+    for k in (1, 2, 3):
+        gat.line(k)
+    for kz in range(NZ):
+        gat.plane(kz)
+    gat.end()
+    exc.end()
+
+
+def weights_in(w, x, cid):
+    return pl.pallas_call(
+        weights_in_kernel, in_specs=[ANY, ANY], out_specs=[ANY, ANY],
+        out_shape=[sds((ND,) + w.shape, w.dtype), sds(x.shape, x.dtype)],
+        scratch_shapes=Gather.sems() + Exchange.sems(),
+        compiler_params=params(16, cid), name="weights_in")(w, x)
+
+
+def grads_out_kernel(n, *refs):
+    gs, small, gt = refs[:n], refs[n], refs[n + 1]
+    outs, osmall, go = refs[n + 2:2 * n + 2], refs[2 * n + 2], refs[2 * n + 3]
+    refs = refs[2 * n + 4:]
+    nb = len(Scatter.bufs(gs[0].shape))
+    mc, mx, mz, ms, mr, e1, e2, e3 = refs[:8]
+    sca = [Scatter(gs[j], outs[j], *refs[8 + j * nb:8 + (j + 1) * nb]) for j in range(n)]
+    s, z, c = place()
+    zs, ss, co = partners(s, z, c)
+    exc = Exchange(gt, go, e1, e2, e3)
+    meet_all()
+    first = remote(small, mc, ms.at[0], mr.at[0], co)
+    first.start()
+    for a in sca:
+        a.start()
+    exc.start()
+    first.wait_recv()
+    mx[s] = small[...] + mc[...]
+    xy = [remote(mx.at[s], mx.at[s], ms.at[k], mr.at[k], ss[k - 1]) for k in (1, 2, 3)]
+    for cp in xy:
+        cp.start()
+    sca[0].plane(0, 16)
+    for cp in xy:
+        cp.wait_recv()
+    mz[z] = (mx[0] + mx[1]) + (mx[2] + mx[3])
+    zz = [remote(mz.at[z], mz.at[z], ms.at[3 + k], mr.at[3 + k], zs[k - 1]) for k in (1, 2, 3)]
+    for cp in zz:
+        cp.start()
+    for j in range(1, n):
+        sca[j].plane(0, 16)
+        sca[j - 1].line(0, 4)
+    sca[n - 1].line(0, 4)
+    for cp in zz:
+        cp.wait_recv()
+    osmall[...] = (mz[0] + mz[1]) + (mz[2] + mz[3])
+    for a in sca:
+        a.end()
+    exc.end()
+    for cp in [first] + xy + zz:
+        cp.wait_send()
+
+
+def grads_out(gs, small, gt, cid):
+    sm = pltpu.VMEM(small.shape, F32)
+    sm4 = pltpu.VMEM((4,) + small.shape, F32)
+    return pl.pallas_call(
+        functools.partial(grads_out_kernel, len(gs)),
+        in_specs=[ANY] * len(gs) + [VM, ANY], out_specs=[VM] * (len(gs) + 1) + [ANY],
+        out_shape=[sds(g.shape[1:], F32) for g in gs] + [sds(small.shape, F32), sds(gt.shape, BF)],
+        scratch_shapes=[sm, sm4, sm4, DMA((7,)), DMA((7,))] + Exchange.sems() + sum([Scatter.bufs(g.shape) for g in gs], []),
+        compiler_params=params(56, cid), name="grads_out")(*gs, small, gt)
+
+
 EPS = 1e-6
 GATE = 0.7978845608028654
 
@@ -62,10 +356,6 @@
 
 def col(shape, j):
     return pl.BlockSpec(shape, lambda *a: (0, j), pipeline_mode=pl.Buffered(1))
-
-
-def sds(shape, dt):
-    return jax.ShapeDtypeStruct(shape, dt)
 
 
 def rows8(v):
@@ -96,9 +386,28 @@
     return [slice(i * BLK, (i + 1) * BLK) for i in range(n)]
 
 
-def self_fwd_kernel(st_ref, x_ref, w_ref, gn_ref, bias_ref, mpre_ref, mpost_ref,
-                    q_ref, k_ref, v_ref, att_ref, gain_ref, p_ref, acc_ref, lo_ref):
+def self_fwd_kernel(near, st_ref, x_ref, w_ref, gn_ref, bias_ref, mpre_ref, mpost_ref, *refs):
+    if near:
+        wm_h, enc_h, q_ref, k_ref, v_ref, att_ref, gain_ref, p_ref, wo_h, eo_h, acc_ref, lo_ref, ags, exs = split(refs, 12, 3, 3)
+        gat = Gather(wm_h, wo_h, *ags)
+        exc = Exchange(enc_h, eo_h, *exs)
+    else:
+        q_ref, k_ref, v_ref, att_ref, gain_ref, p_ref, acc_ref, lo_ref = refs
     h = pl.program_id(0)
+
+    if near:
+        @pl.when(h == 0)
+        def _():
+            meet_all()
+            gat.start()
+            exc.start()
+
+        for hh, fns in ((2, [lambda: gat.line(1)]), (3, [lambda: gat.line(2), lambda: gat.line(3)]),
+                        (7, [lambda: gat.plane(0), lambda: gat.plane(1)]), (9, [lambda: gat.plane(2), lambda: gat.plane(3)])):
+            @pl.when(h == hh)
+            def _(fns=fns):
+                for f in fns:
+                    f()
 
     @pl.when(h == 0)
     def _():
@@ -142,27 +451,44 @@
     @pl.when(h == H - 1)
     def _():
         att_ref[...] = acc_ref[...].astype(BF)
-
-
-def self_fwd(starts, x, w1, bias, mpre, mpost):
+        if near:
+            gat.end()
+            exc.end()
+
+
+def self_fwd(starts, x, w1, bias, mpre, mpost, far=None, cid=None):
     one = cst((L, D))
+    near = far is not None
+    extra_out = [sds((ND,) + far[0].shape, BF), sds(far[1].shape, BF)] if near else []
     return pl.pallas_call(
-        self_fwd_kernel,
+        functools.partial(self_fwd_kernel, near),
         grid_spec=pltpu.PrefetchScalarGridSpec(
             num_scalar_prefetch=1, grid=(H,),
             in_specs=[one, col((D, 3 * D), 0), col((D, 128), 18),
-                      pl.BlockSpec((1, NBK, BLK, BLK), lambda h, st: (h, 0, 0, 0)), cst((H, D)), cst((H, D))],
-            out_specs=[one] * 4 + [cst((8, D)), pl.BlockSpec((1, L, L), lambda h, st: (h, 0, 0))],
-            scratch_shapes=[pltpu.VMEM((L, D), F32), pltpu.VMEM((L, 128), jnp.int32)]),
-        out_shape=[sds((L, D), BF)] * 4 + [sds((8, D), F32), sds((H, L, L), BF)],
-        compiler_params=pltpu.CompilerParams(vmem_limit_bytes=56 << 20),
+                      pl.BlockSpec((1, NBK, BLK, BLK), lambda h, st: (h, 0, 0, 0)), cst((H, D)), cst((H, D))]
+            + [ANY] * (2 * near),
+            out_specs=[one] * 4 + [cst((8, D)), pl.BlockSpec((1, L, L), lambda h, st: (h, 0, 0))] + [ANY] * (2 * near),
+            scratch_shapes=[pltpu.VMEM((L, D), F32), pltpu.VMEM((L, 128), jnp.int32)]
+            + (Gather.sems() + Exchange.sems() if near else [])),
+        out_shape=[sds((L, D), BF)] * 4 + [sds((8, D), F32), sds((H, L, L), BF)] + extra_out,
+        compiler_params=params(56, cid),
         cost_estimate=pl.CostEstimate(flops=52_000_000_000, bytes_accessed=45_000_000, transcendentals=8_000_000),
-        name="self_fwd")(starts, x, w1, w1, bias, mpre, mpost)
-
-
-def cross_fwd_kernel(x_ref, att_ref, wo_ref, wq_ref, wk_ref, wv_ref, enc_ref, gain_ref,
-                     h1_ref, n2_ref, q_ref, k_ref, v_ref, catt_ref, p_ref):
+        name="self_fwd")(starts, x, w1, w1, bias, mpre, mpost, *(far or ()))
+
+
+def cross_fwd_kernel(near, x_ref, att_ref, wo_ref, wq_ref, wk_ref, wv_ref, enc_ref, gain_ref, *refs):
+    if near:
+        cot_h, h1_ref, n2_ref, q_ref, k_ref, v_ref, catt_ref, p_ref, co_h, exs = split(refs, 9, 3)
+        exc = Exchange(cot_h, co_h, *exs)
+    else:
+        h1_ref, n2_ref, q_ref, k_ref, v_ref, catt_ref, p_ref = refs
     h = pl.program_id(0)
+
+    if near:
+        @pl.when(h == 0)
+        def _():
+            meet_seq()
+            exc.start()
 
     @pl.when(h == 0)
     def _():
@@ -200,17 +526,24 @@
             catt_ref[r, cols] = jnp.where(first, keep, o).astype(BF)
         sc = nxt
 
-
-def cross_fwd(x, att, wmid, enc, gains):
+    if near:
+        @pl.when(h == H // 2 - 1)
+        def _():
+            exc.end()
+
+
+def cross_fwd(x, att, wmid, enc, gains, far=None, cid=None):
     one = cst((L, D))
+    near = far is not None
     return pl.pallas_call(
-        cross_fwd_kernel, grid=(H // 2,),
-        in_specs=[one, one] + [col((D, D), j) for j in range(4)] + [one, cst((8, D))],
-        out_specs=[one] * 6 + [pl.BlockSpec((2, L, L), lambda h: (h, 0, 0))],
-        out_shape=[sds((L, D), F32)] + [sds((L, D), BF)] * 5 + [sds((H, L, L), BF)],
-        compiler_params=pltpu.CompilerParams(vmem_limit_bytes=56 << 20),
+        functools.partial(cross_fwd_kernel, near), grid=(H // 2,),
+        in_specs=[one, one] + [col((D, D), j) for j in range(4)] + [one, cst((8, D))] + [ANY] * near,
+        out_specs=[one] * 6 + [pl.BlockSpec((2, L, L), lambda h: (h, 0, 0))] + [ANY] * near,
+        out_shape=[sds((L, D), F32)] + [sds((L, D), BF)] * 5 + [sds((H, L, L), BF)] + [sds(f.shape, BF) for f in far or ()],
+        scratch_shapes=Exchange.sems() if near else [],
+        compiler_params=params(56, cid),
         cost_estimate=pl.CostEstimate(flops=31_000_000_000, bytes_accessed=50_000_000, transcendentals=12_000_000),
-        name="cross_fwd")(x, att, wmid, wmid, wmid, wmid, enc, gains)
+        name="cross_fwd")(x, att, wmid, wmid, wmid, wmid, enc, gains, *(far or ()))
 
 
 def feed_kernel(h1_ref, catt_ref, wco_ref, cot_ref, gain_ref, fi_ref, fo_ref,
@@ -350,10 +683,35 @@
         name="cross_bwd")(q, k, v, do, p, gains, n2, enc, att, catt, h1, bh2, wmid)
 
 
-def self_bwd_kernel(q_ref, k_ref, v_ref, ba_ref, p_ref, mpre_ref, mpost_ref, gain_ref, x_h, bh1_h, w_h,
-                    gw_ref, gtok_ref, gpre_ref, gpost_ref, diag_ref, dg_ref,
-                    qt, bat, dqa, dkt, dvt, dm, x, bh1, w, sems):
+def self_bwd_kernel(near, q_ref, k_ref, v_ref, ba_ref, p_ref, mpre_ref, mpost_ref, gain_ref, x_h, bh1_h, w_h, *refs):
+    if near:
+        gm_h, out_h, ge_h = refs[:3]
+        gq_ref, gk_ref, gv_ref, gtok_ref, gpre_ref, gpost_ref, diag_ref, dg_ref, rm_ref, oo_h, go_h = refs[3:14]
+        qt, bat, dqa, dkt, dvt, dm, x, bh1, w, sems, sca, ex1, ex2 = split(refs[14:], 10, len(Scatter.bufs(gm_h.shape)), 3, 3)
+        sca = Scatter(gm_h, rm_ref, *sca)
+        exc = [Exchange(out_h, oo_h, *ex1), Exchange(ge_h, go_h, *ex2)]
+    else:
+        gq_ref, gk_ref, gv_ref, gtok_ref, gpre_ref, gpost_ref, diag_ref, dg_ref = refs[:8]
+        qt, bat, dqa, dkt, dvt, dm, x, bh1, w, sems = refs[8:]
     h = pl.program_id(0)
+
+    if near:
+        @pl.when(h == 0)
+        def _():
+            meet_all()
+            sca.start()
+            for e in exc:
+                e.start()
+
+        for hh, lo, hi in ((1, 0, 6), (2, 6, 12), (3, 12, 16)):
+            @pl.when(h == hh)
+            def _(lo=lo, hi=hi):
+                sca.plane(lo, hi)
+
+        for hh, lo, hi in ((9, 0, 2), (10, 2, 4)):
+            @pl.when(h == hh)
+            def _(lo=lo, hi=hi):
+                sca.line(lo, hi)
     late = [(x_h, x), (bh1_h, bh1), (w_h.at[:, pl.ds(0, 3 * D)], w)]
     copies = [pltpu.make_async_copy(a, b, sems.at[i]) for i, (a, b) in enumerate(late)]
 
@@ -424,221 +782,34 @@
             dx, s = norm_grad(xr, g, back)
             dg = dg + s
             gtok_ref[r, :] = (bh1[r, :] + dx).astype(gtok_ref.dtype)
-        gw_ref[:, :D] = dot(bat[...], dm[:, :D], 1, 0).astype(BF)
-        gw_ref[:, D:2 * D] = dot(bat[...], dqa[...].astype(BF), 1, 0).astype(BF)
-        gw_ref[:, 2 * D:] = dot(bat[...], dvt[...].astype(BF), 1, 1).astype(BF)
+        gq_ref[...] = dot(bat[...], dm[:, :D], 1, 0).astype(BF)
+        gk_ref[...] = dot(bat[...], dqa[...].astype(BF), 1, 0).astype(BF)
+        gv_ref[...] = dot(bat[...], dvt[...].astype(BF), 1, 1).astype(BF)
         dg_ref[...] = dg
-
-
-def self_bwd(q, k, v, ba, p, mpre, mpost, gains, x, bh1, w1):
+        if near:
+            sca.end()
+            for e in exc:
+                e.end()
+
+
+def self_bwd(q, k, v, ba, p, mpre, mpost, gains, x, bh1, w1, far=None, cid=None):
     one = cst((L, D))
+    near = far is not None
+    more = [cst(far[0].shape[1:]), ANY, ANY] if near else []
+    more_out = [sds(far[0].shape[1:], F32)] + [sds(f.shape, BF) for f in far[1:]] if near else []
     return pl.pallas_call(
-        self_bwd_kernel, grid=(H,),
-        in_specs=[one] * 4 + [pl.BlockSpec((1, L, L), lambda h: (h, 0, 0)), cst((H, D)), cst((H, D)), cst((8, D))] + [ANY] * 3,
-        out_specs=[cst((D, 3 * D)), one, cst((H, D)), cst((H, D)),
-                   pl.BlockSpec((1, NBK, 1, 2 * BLK), lambda h: (h, 0, 0, 0)), cst((8, D))],
-        out_shape=[sds((D, 3 * D), BF), sds((L, D), BF), sds((H, D), F32), sds((H, D), F32),
-                   sds((H, NBK, 1, 2 * BLK), F32), sds((8, D), F32)],
+        functools.partial(self_bwd_kernel, near), grid=(H,),
+        in_specs=[one] * 4 + [pl.BlockSpec((1, L, L), lambda h: (h, 0, 0)), cst((H, D)), cst((H, D)), cst((8, D))] + [ANY] * (3 + 3 * near),
+        out_specs=[cst((D, D))] * 3 + [one, cst((H, D)), cst((H, D)),
+                   pl.BlockSpec((1, NBK, 1, 2 * BLK), lambda h: (h, 0, 0, 0)), cst((8, D))] + more,
+        out_shape=[sds((D, D), BF)] * 3 + [sds((L, D), BF), sds((H, D), F32), sds((H, D), F32),
+                   sds((H, NBK, 1, 2 * BLK), F32), sds((8, D), F32)] + more_out,
         scratch_shapes=[pltpu.VMEM((D, L), BF)] * 2 + [pltpu.VMEM((L, D), F32)] + [pltpu.VMEM((D, L), F32)] * 2
-        + [pltpu.VMEM((L, L), BF), pltpu.VMEM((L, D), BF), pltpu.VMEM((L, D), F32), pltpu.VMEM((D, 3 * D), BF), DMA((3,))],
-        compiler_params=pltpu.CompilerParams(vmem_limit_bytes=60 << 20),
+        + [pltpu.VMEM((L, L), BF), pltpu.VMEM((L, D), BF), pltpu.VMEM((L, D), F32), pltpu.VMEM((D, 3 * D), BF), DMA((3,))]
+        + (Scatter.bufs(far[0].shape) + Exchange.sems() * 2 if near else []),
+        compiler_params=params(61, cid),
         cost_estimate=pl.CostEstimate(flops=128_000_000_000, bytes_accessed=50_000_000, transcendentals=0),
-        name="self_bwd")(q, k, v, ba, p, mpre, mpost, gains, x, bh1, w1)
-
-
-MESH = pl.DeviceIdType.MESH
-NS, NZ, NCORE = 4, 4, 2
-CHUNK = D
-
-
-def place():
-    s = lax.axis_index("seq")
-    d = lax.axis_index("dp")
-    return s, d // NCORE, d % NCORE
-
-
-def flat(s, z, c):
-    return (s * NZ + z) * NCORE + c
-
-
-def partners(s, z, c):
-    zs = [{"seq": s, "dp": ((z + k) % NZ) * NCORE + c} for k in (1, 2, 3)]
-    ss = [{"seq": (s + k) % NS, "dp": z * NCORE + c} for k in (1, 2, 3)]
-    return zs, ss, {"seq": s, "dp": z * NCORE + 1 - c}
-
-
-def meet(devices):
-    bar = pltpu.get_barrier_semaphore()
-    for p in devices:
-        pl.semaphore_signal(bar, inc=1, device_id=p, device_id_type=MESH)
-    pl.semaphore_wait(bar, len(devices))
-
-
-def remote(src, dst, ssem, rsem, dev):
-    return pltpu.make_async_remote_copy(src, dst, ssem, rsem, device_id=dev, device_id_type=MESH)
-
-
-def weights_in_kernel(w_ref, x_ref, out_ref, xo_ref, ssem, rsem, xs, xr, lsem):
-    s, z, c = place()
-    zs, ss, co = partners(s, z, c)
-    own = flat(s, z, c)
-    local = [pltpu.make_async_copy(w_ref, out_ref.at[own], lsem.at[0]),
-             pltpu.make_async_copy(x_ref.at[s], xo_ref.at[s], lsem.at[1])]
-    for cp in local:
-        cp.start()
-    meet(zs + ss + [co])
-    sends = []
-
-    def send(i, dev, src=None):
-        n = len(sends)
-        cp = remote(out_ref.at[i] if src is None else src, out_ref.at[i], ssem.at[n], rsem.at[i], dev)
-        cp.start()
-        sends.append(cp)
-
-    def arrived(i):
-        remote(out_ref.at[i], out_ref.at[i], ssem.at[0], rsem.at[i], co).wait_recv()
-
-    for p in zs:
-        send(own, p, w_ref)
-    xc = []
-    for k in (1, 2, 3):
-        cp = remote(x_ref.at[(s + k) % NS], xo_ref.at[s], xs.at[k - 1], xr.at[k - 1], ss[k - 1])
-        cp.start()
-        xc.append(cp)
-    for p in ss:
-        send(own, p, w_ref)
-    send(own, co, w_ref)
-    for k in (1, 2, 3):
-        i = flat(s, (z + NZ - k) % NZ, c)
-        arrived(i)
-        for p in ss:
-            send(i, p)
-        send(i, co)
-    for kz in range(NZ):
-        for k in (1, 2, 3):
-            i = flat((s + NS - k) % NS, (z + NZ - kz) % NZ, c)
-            arrived(i)
-            send(i, co)
-    for kz in range(NZ):
-        for k in range(NS):
-            arrived(flat((s + k) % NS, (z + kz) % NZ, 1 - c))
-    for cp in xc:
-        cp.wait_recv()
-    for cp in sends + xc:
-        cp.wait_send()
-    for cp in local:
-        cp.wait()
-
-
-def weights_in(w, x, cid):
-    r, n = w.shape
-    return pl.pallas_call(
-        weights_in_kernel, in_specs=[ANY, ANY], out_specs=[ANY, ANY],
-        out_shape=[sds((NS * NZ * NCORE, r, n), w.dtype), sds(x.shape, x.dtype)],
-        scratch_shapes=[DMA((31,)), DMA((32,)), DMA((3,)), DMA((3,)), DMA((2,))],
-        compiler_params=pltpu.CompilerParams(collective_id=cid, has_side_effects=True),
-        name="weights_in")(w, x)
-
-
-def grads_out_kernel(n, *refs):
-    gs, small = refs[:n], refs[n]
-    outs, osmall = refs[n + 1:2 * n + 1], refs[2 * n + 1]
-    rc, acc, rx, sz, rz, own, mc, mx, mz, cs, cr, xs, xr, zsm, zr, ms, mr = refs[2 * n + 2:]
-    s, z, c = place()
-    zs, ss, co = partners(s, z, c)
-    chunks = [(g, o, pl.ds(j * CHUNK, CHUNK)) for g, o in zip(gs, outs) for j in range(g.shape[2] // CHUNK)]
-    meet(zs + ss + [co])
-    cs0 = remote(small, mc, ms.at[0], mr.at[0], co)
-    cs0.start()
-    order = [(k, kz) for k in (2, 1, 3, 0) for kz in (1, 2, 3, 0)]
-    sent = [cs0]
-    cc = []
-    for q, (g, o, cols) in enumerate(chunks):
-        cq = []
-        for m, (k, kz) in enumerate(order):
-            i = flat((s + k) % NS, (z + kz) % NZ, 1 - c)
-            cp = remote(g.at[i, :, cols], rc.at[q, flat((s + k) % NS, (z + kz) % NZ, 0) // NCORE], cs.at[q, m],
-                        cr.at[q, flat((s + k) % NS, (z + kz) % NZ, 0) // NCORE], co)
-            cp.start()
-            cq.append(cp)
-        cc.append(cq)
-        sent += cq
-    cs0.wait_recv()
-    mx[s] = small[...] + mc[...]
-    mxs = []
-    for k in (1, 2, 3):
-        cp = remote(mx.at[s], mx.at[s], ms.at[k], mr.at[k], ss[k - 1])
-        cp.start()
-        mxs.append(cp)
-    sent += mxs
-
-    def xy_arrived(q, kz):
-        g, o, cols = chunks[q]
-        v = own[q % 2, kz]
-        for k in (2, 1, 3):
-            remote(acc.at[0, 0], rx.at[q, kz, k - 1], xs.at[0, 0], xr.at[q, kz, k - 1], ss[k - 1]).wait_recv()
-            v = v + rx[q, kz, k - 1].astype(F32)
-        if kz:
-            sz[q, kz - 1] = v.astype(BF)
-            cp = remote(sz.at[q, kz - 1], rz.at[q, kz - 1], zsm.at[q, kz - 1], zr.at[q, kz - 1], zs[kz - 1])
-            cp.start()
-            sent.append(cp)
-        else:
-            o[:, cols] = v
-
-    for q, (g, o, cols) in enumerate(chunks):
-        for m, (k, kz) in enumerate(order):
-            js, jz = (s + k) % NS, (z + kz) % NZ
-            cc[q][m].wait_recv()
-            v = g[flat(js, jz, c), :, cols].astype(F32) + rc[q, js * NZ + jz].astype(F32)
-            if k:
-                acc[q, m] = v.astype(BF)
-                cp = remote(acc.at[q, m], rx.at[q, kz, k - 1], xs.at[q, m], xr.at[q, kz, k - 1], ss[k - 1])
-                cp.start()
-                sent.append(cp)
-            else:
-                own[q % 2, kz] = v
-        if q:
-            for kz in (1, 2, 3, 0):
-                xy_arrived(q - 1, kz)
-        if q == 0:
-            for cp in mxs:
-                cp.wait_recv()
-            mz[z] = (mx[0] + mx[1]) + (mx[2] + mx[3])
-            mzs = []
-            for k in (1, 2, 3):
-                cp = remote(mz.at[z], mz.at[z], ms.at[3 + k], mr.at[3 + k], zs[k - 1])
-                cp.start()
-                mzs.append(cp)
-            sent += mzs
-    for kz in (1, 2, 3, 0):
-        xy_arrived(len(chunks) - 1, kz)
-    for cp in mzs:
-        cp.wait_recv()
-    osmall[...] = (mz[0] + mz[1]) + (mz[2] + mz[3])
-    for q, (g, o, cols) in enumerate(chunks):
-        for kz in (1, 2, 3):
-            remote(sz.at[0, 0], rz.at[q, kz - 1], zsm.at[0, 0], zr.at[q, kz - 1], zs[0]).wait_recv()
-            o[:, cols] += rz[q, kz - 1].astype(F32)
-    for cp in sent:
-        cp.wait_send()
-
-
-def grads_out(gs, small, cid):
-    r = gs[0].shape[1]
-    q = sum(g.shape[2] for g in gs) // CHUNK
-    sm = pltpu.VMEM(small.shape, F32)
-    sm4 = pltpu.VMEM((4,) + small.shape, F32)
-    return pl.pallas_call(
-        functools.partial(grads_out_kernel, len(gs)),
-        in_specs=[VM] * (len(gs) + 1), out_specs=[VM] * (len(gs) + 1),
-        out_shape=[sds(g.shape[1:], F32) for g in gs] + [sds(small.shape, F32)],
-        scratch_shapes=[pltpu.VMEM((q, 16, r, CHUNK), BF), pltpu.VMEM((q, 12, r, CHUNK), BF), pltpu.VMEM((q, 4, 3, r, CHUNK), BF),
-                        pltpu.VMEM((q, 3, r, CHUNK), BF), pltpu.VMEM((q, 3, r, CHUNK), BF), pltpu.VMEM((2, 4, r, CHUNK), F32),
-                        sm, sm4, sm4, DMA((q, 16)), DMA((q, 16)), DMA((q, 12)), DMA((q, 4, 3)), DMA((q, 3)), DMA((q, 3)),
-                        DMA((7,)), DMA((7,))],
-        compiler_params=pltpu.CompilerParams(collective_id=cid, has_side_effects=True, vmem_limit_bytes=56 << 20),
-        name="grads_out")(*gs, small)
+        name="self_bwd")(q, k, v, ba, p, mpre, mpost, gains, x, bh1, w1, *(far or ()))
 
 
 AX = ("seq", "dp")
@@ -673,22 +844,35 @@
     else:
         w1 = gather(w1)
         x = to_stream(tokens)
-    wmid = gather(wmid)
+        wmid = gather(wmid)
+        enc = to_stream(encoded)
+        cot = to_stream(cotangent)
     wfeed = gather(wfeed)
-    enc = to_stream(encoded)
-    cot = to_stream(cotangent)
     starts = lax.dynamic_index_in_dim(doc_starts, lax.axis_index("seq"), 0, keepdims=False)
     hot = (rel_bucket[:, None] == jnp.arange(buckets)[None, :]).astype(F32)
     trow = lax.dot_general(rel_table, hot, (((0,), (1,)), ((), ())), precision=lax.Precision.HIGHEST)
     bias = toeplitz(make_base(trow))
     mpre = jnp.repeat(mix_pre.T, DH, axis=1)
     mpost = jnp.repeat(mix_post, DH, axis=1)
-    q, k, v, att, gain, p = self_fwd(starts, x, w1, bias, mpre, mpost)
-    h1, n2, cqx, ckx, cvx, catt, cp = cross_fwd(x, att, wmid, enc, gain)
+    if near:
+        q, k, v, att, gain, p, wmid, enc = self_fwd(starts, x, w1, bias, mpre, mpost, (wmid, encoded), 2)
+        wmid = wmid.reshape(D, -1)
+        enc = enc.reshape(L, D)
+        h1, n2, cqx, ckx, cvx, catt, cp, cot = cross_fwd(x, att, wmid, enc, gain, (cotangent,), 3)
+        cot = cot.reshape(L, D)
+    else:
+        q, k, v, att, gain, p = self_fwd(starts, x, w1, bias, mpre, mpost)
+        h1, n2, cqx, ckx, cvx, catt, cp = cross_fwd(x, att, wmid, enc, gain)
     out, bh2, bca, gw_feed, dgf = feed(h1, catt, wmid, cot, gain, wfeed)
     r_feed = scatter(gw_feed).reshape(rows, nf, 2, D)
     gw_mid, g_enc, bh1, bat, dgc = cross_bwd(cqx, ckx, cvx, bca, cp, gain, n2, enc, att, catt, h1, bh2, wmid)
-    gw_qkv, g_tok, gpre, gpost, diag, dgs = self_bwd(q, k, v, bat, p, mpre, mpost, gain, x, bh1, w1)
+    blk = lambda a: a.reshape(nseq, L // nseq, D)
+    if near:
+        far = (gw_mid.reshape(ndev, rows, -1), blk(out), blk(g_enc))
+        gw_q, gw_k, gw_v, g_tok, gpre, gpost, diag, dgs, r_mid, out, g_enc = self_bwd(
+            q, k, v, bat, p, mpre, mpost, gain, x, bh1, w1, far, 4)
+    else:
+        gw_q, gw_k, gw_v, g_tok, gpre, gpost, diag, dgs = self_bwd(q, k, v, bat, p, mpre, mpost, gain, x, bh1, w1)
     gpre = gpre.reshape(H, H, DH).sum(-1).T
     gpost = gpost.reshape(H, H, DH).sum(-1)
     dg = diag[:, :, 0, ::-1]
@@ -702,7 +886,7 @@
         parts = [dgain, gpre, gpost, gtab]
         vec = jnp.concatenate([a.reshape(-1) for a in parts])
         vec = jnp.pad(vec, (0, 3072 - vec.shape[0])).reshape(24, 128)
-        r_mid, r_qkv, vec = grads_out([gw_mid.reshape(ndev, rows, -1), gw_qkv.reshape(ndev, rows, -1)], vec, 2)
+        r_q, r_k, r_v, vec, g_tok = grads_out([a.reshape(ndev, rows, -1) for a in (gw_q, gw_k, gw_v)], vec, blk(g_tok), 5)
         vec = vec.reshape(-1)
         o = 0
         got = []
@@ -711,13 +895,14 @@
             o += a.size
         dgain, gpre, gpost, gtab = got
     else:
-        r_mid, r_qkv = scatter(gw_mid), scatter(gw_qkv)
+        r_mid, r_q, r_k, r_v = scatter(gw_mid), scatter(gw_q), scatter(gw_k), scatter(gw_v)
+        out, g_tok, g_enc = from_stream(out), from_stream(g_tok), from_stream(g_enc)
         dgain, gpre, gpost, gtab = lax.psum((dgain, gpre, gpost, gtab), AX)
     me = lax.axis_index("seq") * ndp + lax.axis_index("dp")
     dgain = lax.dynamic_slice_in_dim(dgain, me * rows, rows, 1)
     m = lambda a, j: a[:, j * D:(j + 1) * D]
-    return (from_stream(out), from_stream(g_tok).astype(F32), from_stream(g_enc).astype(F32),
-            m(r_qkv, 0), m(r_qkv, 1), m(r_qkv, 2), m(r_mid, 0), m(r_mid, 1), m(r_mid, 2), m(r_mid, 3), m(r_mid, 4),
+    return (out, g_tok.astype(F32), g_enc.astype(F32),
+            r_q, r_k, r_v, m(r_mid, 0), m(r_mid, 1), m(r_mid, 2), m(r_mid, 3), m(r_mid, 4),
             r_feed[:, :, 0].transpose(0, 2, 1).reshape(rows, nf * D), r_feed[:, :, 1].reshape(rows * nf, D),
             dgain[0], dgain[1], dgain[2], gpre, gpost, gtab)
 

time: 586 us -> 495 us (0.84)
  local copies, waits for them, and re-layouts: 66.8 us -> 30.5 us
  other arithmetic: 37.3 us -> 6.63 us
  starting transfers between devices: 22.6 us -> 0.08 us
  waiting for transfers between devices: 11.1 us -> 0.06 us
  Pallas kernels: 423 us -> 432 us
    unnamed x3 -> x0, other arithmetic: 36.1 us -> none
    unnamed x69 -> x79, local copies, waits for them, and re-layouts: 35.8 us -> 11.6 us
    all_to_all x5 -> x0, starting transfers between devices: 22 us -> none  [the longest x3 13.2 us: per_device(): lax.all_to_all(x.reshape(1, L, D), 'seq', 1, 0, tiled=True)]
    pallas_call x4, Pallas kernels: 259 us -> 272 us  [the longest x1 108 us: self_bwd(): pl.pallas_call(functools.partial(self_bwd_kernel, near), grid=(H,), in_sp...]
    reshape x3 -> x0, local copies, waits for them, and re-layouts: 11.5 us -> none  [per_device(): x.reshape(1, L, D)]
    all_gather x2 -> x1, waiting for transfers between devices: 10.8 us -> 0.02 us  [gather(): return lax.all_gather(w, AX, axis=0, tiled=True)]
  transfers between devices with their start and end apart: 8 -> 2, of which waited for: 2 -> 0; matrix products, arithmetic and copies ran while one was open for 16% -> 5% of each run, Pallas kernels for 66% -> 80%
where the time goes in v3:
time: 495 us; the launch traced here: 485 us
  Pallas kernels  432 us (87%)
  local copies, waits for them, and re-layouts  30.5 us (6%)
  between operations  14.9 us (3%)
  other arithmetic  6.63 us (1%)
    pallas_call x1, Pallas kernels, self_bwd(): pl.pallas_call(functools.partial(self_bwd_kernel, near), grid=(H,), in_sp...  108 us
    pallas_call x1, Pallas kernels, self_fwd(): pl.pallas_call(functools.partial(self_fwd_kernel, near), grid_spec=pltpu....  75.4 us
    pallas_call x1, Pallas kernels, weights_in(): pl.pallas_call(weights_in_kernel, in_specs=[ANY, ANY], out_specs=[ANY, AN...  54.1 us
    pallas_call x1, Pallas kernels, cross_bwd(): pl.pallas_call(cross_bwd_kernel, grid=(H // 2,), in_specs=[pair] * 4 + [p...  52.3 us
    pallas_call x1, Pallas kernels, grads_out(): pl.pallas_call(functools.partial(grads_out_kernel, len(gs)), in_specs=[AN...  48.3 us
    pallas_call x1, Pallas kernels, feed(): pl.pallas_call(feed_kernel, grid=(nf,), in_specs=[one, one, col((D, D), 4...  44.4 us
    pallas_call x1, Pallas kernels, cross_fwd(): pl.pallas_call(functools.partial(cross_fwd_kernel, near), grid=(H // 2,),...  40.3 us
    unnamed x79, local copies, waits for them, and re-layouts  11.6 us
  transfers between devices with their start and end apart: 2, of which 0 were waited for; matrix products, arithmetic and copies ran while one was open for 5% of the time, Pallas kernels for 80%

profile of v3, /device:TPU:0, one launch (start us, length us, event | category | flops | bytes accessed | tf_op | source)
XLA Modules:
  0.0 485.2 jit_solution(17247299619943225162)
XLA Ops:
  7.3 1.0 stack_reshape.3
  8.2 1.3 copy.94
  10.4 0.9 reshape.140
  16.4 9.6 %bias_tiles.1.bias_ref = f32[12,4,256,256]{3,2,1,0:T(8,128)} custom-call(f32[12,4,1,512]{3,2,1,0:T(1,128)} %broadcast_in_dim.15.base_ref), custom_call_target="tpu_custom_call" | custom-call | tf_op jit(solution)/shard_map/bias_tiles/pallas_call | solution.py:34
  26.0 54.1 %weights_in.1 = (bf16[32,24,2432]{2,1,0:T(8,128)(2,1)S(1)}, bf16[4,256,768]{2,1,0:T(8,128)(2,1)S(1)}) custom-call(bf16[24,2432]{1,0:T(8,128)(2,1)S(1)} %fusion.6.w_ref, bf16[4,256,768]{2,1,0:T(8,128)(2,1)S(1)} %copy-done.2), custom_call_target="tpu_custom_call" | custom-call | tf_op jit(solution)/shard_map/weights_in/pallas_call | solution.py:289
  80.2 1.8 copy-done.3
  82.0 1.1 copy-done.4
  83.1 1.2 dynamic-slice_bitcast_fusion.st_ref
  85.1 75.4 %self_fwd.1 = (bf16[1024,768]{1,0:T(8,128)(2,1)}, bf16[1024,768]{1,0:T(8,128)(2,1)}, bf16[1024,768]{1,0:T(8,128)(2,1)}, bf16[1024,768]{1,0:T(8,128)(2,1)}, f32[8...) custom-call(s32[4]{0:T(128)} %dynamic-slice_bitcast_fusion.st_ref, ...), custom_call_target="tpu_custom_call" | custom-call | flops 51999997952 | bytes 45000000 | tf_op jit(solution)/shard_map/self_fwd/pallas_call | solution.py:463
  160.5 40.3 %cross_fwd.1 = (f32[1024,768]{1,0:T(8,128)}, bf16[1024,768]{1,0:T(8,128)(2,1)}, bf16[1024,768]{1,0:T(8,128)(2,1)}, bf16[1024,768]{1,0:T(8,128)(2,1)}, bf16[1024,...) custom-call(bf16[1024,768]{1,0:T(8,128)(2,1)} %bitcast.66, ...), custom_call_target="tpu_custom_call" | custom-call | flops 31000000512 | bytes 50000000 | tf_op jit(solution)/shard_map/cross_fwd/pallas_call | solution.py:538
  200.9 44.4 %feed.1 = (bf16[1024,768]{1,0:T(8,128)(2,1)}, f32[1024,768]{1,0:T(8,128)}, bf16[1024,768]{1,0:T(8,128)(2,1)}, bf16[768,6144]{1,0:T(8,128)(2,1)}, f32[8,768]{1,0:T(8,128)}) custom-call(f32[1024,768]{1,0:T(8,128)} %get-tuple-element.75.h1_ref.h1_h, bf16[1024,768]{1,0:T(8,128)(2,1)} %get-tuple-element.76.catt_ref.catt_h, bf16[768,3840]{1,0:T(8,128)(2,1)} %bitcast.90, ...), custom_call_target="tpu_custom_call" | custom-call | flops 32000000000 | bytes 50000000 | tf_op jit(solution)/shard_map/feed/pallas_call | solution.py:595
  245.3 52.3 %cross_bwd.1 = (bf16[768,3840]{1,0:T(8,128)(2,1)}, bf16[1024,768]{1,0:T(8,128)(2,1)}, f32[1024,768]{1,0:T(8,128)}, bf16[1024,768]{1,0:T(8,128)(2,1)}, f32[8,768]{1,0:T(8,128)}) custom-call(bf16[1024,768]{1,0:T(8,128)(2,1)} %get-tuple-element.72.q_ref, bf16[1024,768]{1,0:T(8,128)(2,1)} %get-tuple-element.73.k_ref, bf16[1024,768]{1,0:T(8,128)(2,1)} %get-tuple-element.74.v_ref, ...), custom_call_target="tpu_custom_call" | custom-call | flops 36999999488 | bytes 70000000 | tf_op jit(solution)/shard_map/cross_bwd/pallas_call | solution.py:674
  297.6 107.6 %self_bwd.1 = (bf16[768,768]{1,0:T(8,128)(2,1)}, bf16[768,768]{1,0:T(8,128)(2,1)}, bf16[768,768]{1,0:T(8,128)(2,1)}, bf16[1024,768]{1,0:T(8,128)(2,1)}, f32[12,7...) custom-call(bf16[1024,768]{1,0:T(8,128)(2,1)} %get-tuple-element.65., ...), custom_call_target="tpu_custom_call" | custom-call | flops 128000000000 | bytes 50000000 | tf_op jit(solution)/shard_map/self_bwd/pallas_call | solution.py:800
  406.0 0.9 reshape.148
  407.2 0.9 reshape.150
  408.3 2.0 rev.31
  411.8 48.3 %grads_out.1 = (f32[24,768]{1,0:T(8,128)}, f32[24,768]{1,0:T(8,128)}, f32[24,768]{1,0:T(8,128)}, f32[24,128]{1,0:T(8,128)}, bf16[4,256,768]{2,1,0:T(8,128)(2,1)}) custom-call(bf16[32,24,768]{2,1,0:T(8,128)(2,1)} %bitcast.71, bf16[32,24,768]{2,1,0:T(8,128)(2,1)} %bitcast.72, bf16[32,24,768]{2,1,0:T(8,128)(2,1)} %bitcast.73, ...), custom_call_target="tpu_custom_call" | custom-call | tf_op jit(solution)/shard_map/grads_out/pallas_call | solution.py:341
  460.2 0.8 slice.111
  462.4 3.5 convert_element_type.20
  465.9 1.9 convert_element_type.21
  469.8 1.5 reshape.160
  471.3 1.0 slice_reduce_fusion
  473.9 1.2 copy.104
  475.1 1.1 copy.128
  (137 shorter events, 16.2 us)
Async XLA Ops:
  7.2 4.5 copy-start
  7.2 193.7 %all-gather.2.cloned.1.call-start = ((), (), s32[]{:S(2)}) async-start(), calls=%async_computation.1 | async-start | bytes 9732096 | tf_op jit(solution)/shard_map/all_gather | solution.py:819
  9.5 2.0 copy-start.24
  9.5 1.9 copy-start.25
  9.6 2.0 copy-start.21
  9.6 2.1 copy-start.27
  10.4 5.2 %copy-start.22 = (f32[12,12]{1,0:T(8,128)S(1)}, f32[12,12]{1,0:T(8,128)}, u32[]{:S(2)}) copy-start(f32[12,12]{1,0:T(8,128)} %param.40) | copy-start | bytes 1732
  11.3 458.4 %reduce-scatter.2.cloned.1.call-start = ((), (), s32[]{:S(2)}) async-start(), calls=%async_computation.2 | async-start | bytes 9732096 | tf_op jit(solution)/shard_map/reduce_scatter | solution.py:823
  16.3 9.6 %copy-start.11 = (bf16[24,768]{1,0:T(8,128)(2,1)S(1)}, bf16[24,768]{1,0:T(8,128)(2,1)}, u32[]{:S(2)}) copy-start(bf16[24,768]{1,0:T(8,128)(2,1)} %param.28) | copy-start | bytes 110596
  16.3 9.6 %copy-start.12 = (bf16[24,768]{1,0:T(8,128)(2,1)S(1)}, bf16[24,768]{1,0:T(8,128)(2,1)}, u32[]{:S(2)}) copy-start(bf16[24,768]{1,0:T(8,128)(2,1)} %param.27) | copy-start | bytes 110596
  16.4 9.6 %copy-start.13 = (bf16[24,768]{1,0:T(8,128)(2,1)S(1)}, bf16[24,768]{1,0:T(8,128)(2,1)}, u32[]{:S(2)}) copy-start(bf16[24,768]{1,0:T(8,128)(2,1)} %param.26) | copy-start | bytes 110596
  16.4 9.7 %copy-start.2 = (bf16[4,256,768]{2,1,0:T(8,128)(2,1)S(1)}, bf16[4,256,768]{2,1,0:T(8,128)(2,1)}, u32[]{:S(2)}) copy-start(bf16[4,256,768]{2,1,0:T(8,128)(2,1)} %x_ref.1) | copy-start | bytes 4718596
  25.9 58.4 %copy-start.14 = (bf16[24,768]{1,0:T(8,128)(2,1)S(1)}, bf16[24,768]{1,0:T(8,128)(2,1)}, u32[]{:S(2)}) copy-start(bf16[24,768]{1,0:T(8,128)(2,1)} %param.29) | copy-start | bytes 110596
  25.9 58.4 %copy-start.15 = (bf16[24,768]{1,0:T(8,128)(2,1)S(1)}, bf16[24,768]{1,0:T(8,128)(2,1)}, u32[]{:S(2)}) copy-start(bf16[24,768]{1,0:T(8,128)(2,1)} %param.30) | copy-start | bytes 110596
  25.9 58.4 %copy-start.16 = (bf16[24,768]{1,0:T(8,128)(2,1)S(1)}, bf16[24,768]{1,0:T(8,128)(2,1)}, u32[]{:S(2)}) copy-start(bf16[24,768]{1,0:T(8,128)(2,1)} %param.31) | copy-start | bytes 110596
  25.9 58.4 %copy-start.17 = (bf16[24,768]{1,0:T(8,128)(2,1)S(1)}, bf16[24,768]{1,0:T(8,128)(2,1)}, u32[]{:S(2)}) copy-start(bf16[24,768]{1,0:T(8,128)(2,1)} %param.32) | copy-start | bytes 110596
  26.0 58.4 %copy-start.18 = (bf16[24,768]{1,0:T(8,128)(2,1)S(1)}, bf16[24,768]{1,0:T(8,128)(2,1)}, u32[]{:S(2)}) copy-start(bf16[24,768]{1,0:T(8,128)(2,1)} %param.33) | copy-start | bytes 110596
  297.5 108.4 %copy-start.20 = (f32[8,768]{1,0:T(8,128)S(1)}, f32[8,768]{1,0:T(8,128)}, u32[]{:S(2)}) copy-start(f32[8,768]{1,0:T(8,128)} %get-tuple-element.93) | copy-start | bytes 73732
  297.5 108.4 %copy-start.19 = (f32[8,768]{1,0:T(8,128)S(1)}, f32[8,768]{1,0:T(8,128)}, u32[]{:S(2)}) copy-start(f32[8,768]{1,0:T(8,128)} %get-tuple-element.94) | copy-start | bytes 73732
  297.6 112.8 %copy-start.28 = (s32[1024]{0:T(1024)S(1)}, s32[1024]{0:T(1024)}, u32[]{:S(2)}) copy-start(s32[1024]{0:T(1024)} %param.25) | copy-start | bytes 12292
  462.4 3.5 copy-start.6
  465.9 3.1 copy-start.7
  475.1 3.1 copy-start.1
  475.1 2.4 copy-start.8
  (7 other events, 10.4 us)
Sparse Core Ops, SparseCore 0:
  11.6 109.3 all-gather.1
  245.4 176.3 reduce-scatter.1

commit v4 on v3

--- a/solution.py
+++ b/solution.py
@@ -19,20 +19,23 @@
     return lax.dot_general(a, b, (((ca,), (cb,)), ((), ())), preferred_element_type=F32)
 
 
-def toep_kernel(base_ref, out_ref):
+def bias_tiles(base_ref, h, out_ref):
     for d in range(NBK):
-        row = jnp.broadcast_to(base_ref[0, d], (BLK, 2 * BLK))
+        row = jnp.broadcast_to(base_ref[h, d], (BLK, 2 * BLK))
         t = pltpu.roll(row, 0, 1, stride=1, stride_axis=0)[:, :BLK]
         if d == 0:
             a = lax.broadcasted_iota(jnp.int32, (BLK, BLK), 0)
             b = lax.broadcasted_iota(jnp.int32, (BLK, BLK), 1)
             t = jnp.where(a >= b, t, NEG)
-        out_ref[0, d] = t
+        out_ref[d] = t
 
 
 def toeplitz(base):
+    def kernel(base_ref, out_ref):
+        bias_tiles(base_ref, 0, out_ref.at[0])
+
     return pl.pallas_call(
-        toep_kernel, grid=(H,), in_specs=[pl.BlockSpec((1, NBK, 1, 2 * BLK), lambda h: (h, 0, 0, 0))],
+        kernel, grid=(H,), in_specs=[pl.BlockSpec((1, NBK, 1, 2 * BLK), lambda h: (h, 0, 0, 0))],
         out_specs=pl.BlockSpec((1, NBK, BLK, BLK), lambda h: (h, 0, 0, 0)),
         out_shape=jax.ShapeDtypeStruct((H, NBK, BLK, BLK), F32), name="bias_tiles")(base)
 
@@ -91,6 +94,10 @@
     return zs, ss, {"seq": s, "dp": z * NCORE + 1 - c}
 
 
+def plane(s):
+    return s + 1 - 2 * (s % 2), (s + 2) % NS, NS - 1 - s
+
+
 def meet(devices):
     bar = pltpu.get_barrier_semaphore()
     for p in devices:
@@ -112,9 +119,11 @@
 
 
 class Exchange:
-    def __init__(self, src, dst, ss, rs, ls):
+    def __init__(self, src, dst, ss, rs, ls, part=(0, 1)):
         self.s, z, c = place()
         self.src, self.dst, self.ss, self.rs, self.ls = src, dst, ss, rs, ls
+        n = src.shape[1] // part[1]
+        self.rows = pl.ds(part[0] * n, n)
         self.to = partners(self.s, z, c)[1]
 
     @staticmethod
@@ -122,10 +131,10 @@
         return [DMA((3,)), DMA((3,)), DMA(())]
 
     def local(self):
-        return pltpu.make_async_copy(self.src.at[self.s], self.dst.at[self.s], self.ls)
+        return pltpu.make_async_copy(self.src.at[self.s, self.rows], self.dst.at[self.s, self.rows], self.ls)
 
     def copy(self, k):
-        return remote(self.src.at[(self.s + k) % NS], self.dst.at[self.s], self.ss.at[k - 1], self.rs.at[k - 1], self.to[k - 1])
+        return remote(self.src.at[(self.s + k) % NS, self.rows], self.dst.at[self.s, self.rows], self.ss.at[k - 1], self.rs.at[k - 1], self.to[k - 1])
 
     def start(self):
         for k in (2, 1, 3):
@@ -140,166 +149,346 @@
 
 
 class Gather:
-    def __init__(self, w, out, ssem, rsem, lsem):
-        self.w, self.out, self.ssem, self.rsem, self.lsem = w, out, ssem, rsem, lsem
+    def __init__(self, w, out, ssem, rsem, lsem, cols=None):
+        self.w, self.out, self.ssem, self.rsem, self.lsem, self.cols = w, out, ssem, rsem, lsem, cols
         self.s, self.z, self.c = place()
         self.zs, self.ss, self.co = partners(self.s, self.z, self.c)
-        self.own = flat(self.s, self.z, self.c)
+        self.px, self.py, self.pd = plane(self.s)
 
     @staticmethod
     def sems():
         return [DMA((ND - 1,)), DMA((ND,)), DMA(())]
 
+    def slot(self, i):
+        return self.out.at[i] if self.cols is None else self.out.at[i, :, self.cols]
+
+    def at(self, s, kz, c):
+        return flat(s, (self.z + NZ - kz) % NZ, c)
+
+    def there(self, s):
+        return {"seq": s, "dp": self.z * NCORE + self.c}
+
     def send(self, i, dev, n, src=None):
-        remote(self.out.at[i] if src is None else src, self.out.at[i], self.ssem.at[n], self.rsem.at[i], dev).start()
+        remote(self.slot(i) if src is None else src, self.slot(i), self.ssem.at[n], self.rsem.at[i], dev).start()
 
     def got(self, i):
-        remote(self.out.at[i], self.out.at[i], self.ssem.at[0], self.rsem.at[i], self.co).wait_recv()
+        remote(self.slot(i), self.slot(i), self.ssem.at[0], self.rsem.at[i], self.co).wait_recv()
 
     def local(self):
-        return pltpu.make_async_copy(self.w, self.out.at[self.own], self.lsem)
+        return pltpu.make_async_copy(self.w, self.slot(self.at(self.s, 0, self.c)), self.lsem)
 
     def start(self):
+        own = self.at(self.s, 0, self.c)
         for k in range(3):
-            self.send(self.own, self.zs[k], k, self.w)
-        for k in range(3):
-            self.send(self.own, self.ss[k], 3 + k, self.w)
-        self.send(self.own, self.co, 6, self.w)
+            self.send(own, self.zs[k], k, self.w)
+        self.send(own, self.there(self.px), 3, self.w)
+        self.send(own, self.there(self.py), 4, self.w)
+        self.send(own, self.co, 5, self.w)
         self.local().start()
 
     def line(self, k):
-        i = flat(self.s, (self.z + NZ - k) % NZ, self.c)
+        i = self.at(self.s, k, self.c)
         self.got(i)
-        for j in range(3):
-            self.send(i, self.ss[j], 4 * k + 3 + j)
-        self.send(i, self.co, 4 * k + 6)
-
-    def plane(self, kz):
-        for k in (1, 2, 3):
-            i = flat((self.s + NS - k) % NS, (self.z + NZ - kz) % NZ, self.c)
+        self.send(i, self.there(self.px), 3 * k + 3)
+        self.send(i, self.there(self.py), 3 * k + 4)
+        self.send(i, self.co, 3 * k + 5)
+
+    def hop(self, kz):
+        for j, (a, b) in enumerate(((self.px, self.py), (self.py, self.px))):
+            i = self.at(a, kz, self.c)
             self.got(i)
-            self.send(i, self.co, 19 + 3 * kz + k - 1)
+            if kz % 2 == j:
+                self.send(i, self.there(b), 15 + kz)
+            self.send(i, self.co, 19 + 3 * kz + j)
+
+    def diag(self, kz):
+        i = self.at(self.pd, kz, self.c)
+        self.got(i)
+        self.send(i, self.co, 21 + 3 * kz)
 
     def end(self):
         for kz in range(NZ):
             for k in range(NS):
-                self.got(flat((self.s + k) % NS, (self.z + kz) % NZ, 1 - self.c))
+                self.got(self.at((self.s + k) % NS, kz, 1 - self.c))
         for n in range(ND - 1):
-            remote(self.w, self.out.at[self.own], self.ssem.at[n], self.rsem.at[0], self.co).wait_send()
+            remote(self.w, self.slot(0), self.ssem.at[n], self.rsem.at[0], self.co).wait_send()
         self.local().wait()
 
 
-ORDER = [(k, kz) for k in (2, 1, 3, 0) for kz in (1, 2, 3, 0)]
+class LineGather:
+    def __init__(self, w, out, ss, rs, ls):
+        self.w, self.out, self.ss, self.rs, self.ls = w, out, ss, rs, ls
+        s, self.z, c = place()
+        self.zs = partners(s, self.z, c)[0]
+
+    @staticmethod
+    def sems():
+        return [DMA((3,)), DMA((3,)), DMA(())]
+
+    def local(self):
+        return pltpu.make_async_copy(self.w, self.out.at[self.z], self.ls)
+
+    def copy(self, k):
+        return remote(self.w, self.out.at[self.z], self.ss.at[k], self.rs.at[k], self.zs[k])
+
+    def start(self):
+        for k in range(3):
+            self.copy(k).start()
+        self.local().start()
+
+    def end(self):
+        for k in range(3):
+            self.copy(k).wait_recv()
+            self.copy(k).wait_send()
+        self.local().wait()
+
+
+class PlaneGather(Gather):
+    def src(self, kz):
+        return self.w.at[(self.z + NZ - kz) % NZ]
+
+    def local(self, kz):
+        return pltpu.make_async_copy(self.src(kz), self.slot(self.at(self.s, kz, self.c)), self.lsem.at[kz])
+
+    @staticmethod
+    def sems():
+        return [DMA((ND - 4,)), DMA((ND,)), DMA((4,))]
+
+    def start(self):
+        for kz in range(NZ):
+            i = self.at(self.s, kz, self.c)
+            self.send(i, self.there(self.px), 3 * kz, self.src(kz))
+            self.send(i, self.there(self.py), 3 * kz + 1, self.src(kz))
+            self.send(i, self.co, 3 * kz + 2, self.src(kz))
+            self.local(kz).start()
+
+    def hop(self, kz):
+        for j, (a, b) in enumerate(((self.px, self.py), (self.py, self.px))):
+            i = self.at(a, kz, self.c)
+            self.got(i)
+            if kz % 2 == j:
+                self.send(i, self.there(b), 12 + kz)
+            self.send(i, self.co, 16 + 3 * kz + j)
+
+    def diag(self, kz):
+        i = self.at(self.pd, kz, self.c)
+        self.got(i)
+        self.send(i, self.co, 18 + 3 * kz)
+
+    def end(self):
+        for kz in range(NZ):
+            for k in range(NS):
+                self.got(self.at((self.s + k) % NS, kz, 1 - self.c))
+        for n in range(ND - 4):
+            remote(self.src(0), self.slot(0), self.ssem.at[n], self.rsem.at[0], self.co).wait_send()
+        for kz in range(NZ):
+            self.local(kz).wait()
 
 
 class Scatter:
-    def __init__(self, g, out, mine, rc, acc, rx, own, sz, rz, lsem, cs, cr, xs, xr, zsem, zr):
-        self.g, self.out = g, out
-        self.mine, self.rc, self.acc, self.rx, self.own, self.sz, self.rz = mine, rc, acc, rx, own, sz, rz
-        self.lsem, self.cs, self.cr, self.xs, self.xr, self.zsem, self.zr = lsem, cs, cr, xs, xr, zsem, zr
+    def __init__(self, g, cols, outs, mine, rc, rd, rn, rz, lsem, cs, cr, xs, dr, nr, zsem, zr):
+        self.g, self.cols, self.outs = g, cols, outs
+        self.mine, self.rc, self.rd, self.rn, self.rz = mine, rc, rd, rn, rz
+        self.lsem, self.cs, self.cr, self.xs, self.dr, self.nr, self.zsem, self.zr = lsem, cs, cr, xs, dr, nr, zsem, zr
         self.s, self.z, self.c = place()
         self.zs, self.ss, self.co = partners(self.s, self.z, self.c)
+        self.col = (self.s,) + plane(self.s)
 
     @staticmethod
-    def bufs(shape):
-        b = tuple(shape[1:])
-        v = lambda *n: pltpu.VMEM(n + b, BF)
-        return [v(16), v(16), v(12), v(4, 3), pltpu.VMEM((4,) + b, F32), v(3), v(3),
-                DMA((16,)), DMA((16,)), DMA((16,)), DMA((12,)), DMA((4, 3)), DMA((3,)), DMA((3,))]
-
-    def dest(self, m):
-        k, kz = ORDER[m]
-        return (self.s + k) % NS, (self.z + kz) % NZ
+    def bufs(rows, cols):
+        v = lambda *n: pltpu.VMEM(n + (rows, cols), BF)
+        return [v(16), v(16), v(4), v(2, 4), v(3), DMA((16,)), DMA((16,)), DMA((16,)), DMA((12,)), DMA((4,)), DMA((2, 4)),
+                DMA((3,)), DMA((3,))]
+
+    def part(self, m, c):
+        return self.g.at[flat(self.col[m // 4], (self.z + m % 4) % NZ, c), :, self.cols]
 
     def core(self, m):
-        js, jz = self.dest(m)
-        return remote(self.g.at[flat(js, jz, 1 - self.c)], self.rc.at[js * NZ + jz], self.cs.at[m], self.cr.at[js * NZ + jz], self.co)
+        return remote(self.part(m, 1 - self.c), self.rc.at[m], self.cs.at[m], self.cr.at[m], self.co)
 
     def load(self, m):
-        js, jz = self.dest(m)
-        return pltpu.make_async_copy(self.g.at[flat(js, jz, self.c)], self.mine.at[m], self.lsem.at[m])
-
-    def xy(self, m):
-        k, kz = ORDER[m]
-        return remote(self.acc.at[m], self.rx.at[kz, k - 1], self.xs.at[m], self.xr.at[kz, k - 1], self.ss[k - 1])
+        return pltpu.make_async_copy(self.part(m, self.c), self.mine.at[m], self.lsem.at[m])
+
+    def to_plane(self, m, via, dst, sem):
+        return remote(self.mine.at[m], dst, self.xs.at[m - 4], sem, {"seq": self.col[via], "dp": self.z * NCORE + self.c})
+
+    def to_via(self, kz):
+        return self.to_plane(12 + kz, 2 - kz % 2, self.rd.at[kz], self.dr.at[kz])
+
+    def to_next(self, a, kz):
+        return self.to_plane(4 * a + kz, a, self.rn.at[a - 1, kz], self.nr.at[a - 1, kz])
 
     def zz(self, kz):
-        return remote(self.sz.at[kz - 1], self.rz.at[kz - 1], self.zsem.at[kz - 1], self.zr.at[kz - 1], self.zs[kz - 1])
-
-    def start(self):
-        for m in range(16):
-            self.core(m).start()
-        for m in range(16):
-            self.load(m).start()
-
-    def plane(self, lo, hi):
-        for m in range(lo, hi):
-            k, kz = ORDER[m]
-            js, jz = self.dest(m)
-            self.load(m).wait()
-            remote(self.mine.at[0], self.rc.at[js * NZ + jz], self.cs.at[m], self.cr.at[js * NZ + jz], self.co).wait_recv()
-            v = self.mine[m].astype(F32) + self.rc[js * NZ + jz].astype(F32)
-            if k:
-                self.acc[m] = v.astype(BF)
-                self.xy(m).start()
-            else:
-                self.own[kz] = v
-
-    def line(self, lo, hi):
-        for kz in (1, 2, 3, 0)[lo:hi]:
-            v = self.own[kz]
-            for k in (2, 1, 3):
-                remote(self.acc.at[0], self.rx.at[kz, k - 1], self.xs.at[0], self.xr.at[kz, k - 1], self.ss[k - 1]).wait_recv()
-                v = v + self.rx[kz, k - 1].astype(F32)
+        return remote(self.mine.at[kz], self.rz.at[kz - 1], self.zsem.at[kz - 1], self.zr.at[kz - 1], self.zs[kz - 1])
+
+    def start(self, which):
+        for a in which:
+            for kz in (1, 2, 3, 0):
+                self.core(4 * a + kz).start()
+                self.load(4 * a + kz).start()
+
+    def both(self, m):
+        self.load(m).wait()
+        self.core(m).wait_recv()
+        return self.mine[m].astype(F32) + self.rc[m].astype(F32)
+
+    def away(self, kzs):
+        for kz in kzs:
+            self.mine[12 + kz] = self.both(12 + kz).astype(BF)
+            self.to_via(kz).start()
+
+    def near(self, kzs):
+        for kz in kzs:
+            plain, joined = 2 - kz % 2, 1 + kz % 2
+            self.mine[4 * plain + kz] = self.both(4 * plain + kz).astype(BF)
+            self.to_next(plain, kz).start()
+            v = self.both(4 * joined + kz)
+            self.to_via(kz).wait_recv()
+            self.mine[4 * joined + kz] = (v + self.rd[kz].astype(F32)).astype(BF)
+            self.to_next(joined, kz).start()
+
+    def line(self, kzs):
+        for kz in kzs:
+            v = self.both(kz)
+            for a in (1, 2):
+                self.to_next(a, kz).wait_recv()
+                v = v + self.rn[a - 1, kz].astype(F32)
             if kz:
-                self.sz[kz - 1] = v.astype(BF)
+                self.mine[kz] = v.astype(BF)
                 self.zz(kz).start()
             else:
-                self.own[0] = v
+                self.put(v)
+
+    def stop(self, out):
+        for kz in range(NZ):
+            v = self.both(kz)
+            for a in (1, 2):
+                self.to_next(a, kz).wait_recv()
+                v = v + self.rn[a - 1, kz].astype(F32)
+            out[kz] = v.astype(BF)
+        for m in range(16):
+            self.core(m).wait_send()
+        for kz in range(NZ):
+            self.to_via(kz).wait_send()
+            for a in (1, 2):
+                self.to_next(a, kz).wait_send()
+
+    def put(self, v):
+        at = 0
+        for o in self.outs:
+            w = o.shape[1]
+            o[...] = v[:, at:at + w]
+            at += w
 
     def end(self):
-        v = self.own[0]
+        at = 0
         for kz in (1, 2, 3):
             self.zz(kz).wait_recv()
-            v = v + self.rz[kz - 1].astype(F32)
-        self.out[...] = v
+        for o in self.outs:
+            w = o.shape[1]
+            v = o[...]
+            for kz in (1, 2, 3):
+                v = v + self.rz[kz - 1, :, at:at + w].astype(F32)
+            o[...] = v
+            at += w
         for m in range(16):
             self.core(m).wait_send()
-        for m in range(12):
-            self.xy(m).wait_send()
+        for kz in range(4):
+            self.to_via(kz).wait_send()
+            for a in (1, 2):
+                self.to_next(a, kz).wait_send()
         for kz in (1, 2, 3):
             self.zz(kz).wait_send()
 
 
-def weights_in_kernel(w_ref, x_ref, out_ref, xo_ref, ga, gb, gc, xa, xb, xc):
+class LineScatter:
+    def __init__(self, part, out, mine, rz, lsem, ss, rs):
+        self.part, self.out, self.mine, self.rz, self.lsem, self.ss, self.rs = part, out, mine, rz, lsem, ss, rs
+        s, z, c = place()
+        self.zs = partners(s, z, c)[0]
+
+    @staticmethod
+    def bufs(rows, cols):
+        return [pltpu.VMEM((rows, cols), BF), pltpu.VMEM((3, rows, cols), BF), DMA(()), DMA((3,)), DMA((3,))]
+
+    def copy(self, k):
+        return remote(self.part.at[k + 1], self.rz.at[k], self.ss.at[k], self.rs.at[k], self.zs[k])
+
+    def local(self):
+        return pltpu.make_async_copy(self.part.at[0], self.mine, self.lsem)
+
+    def start(self):
+        for k in range(3):
+            self.copy(k).start()
+        self.local().start()
+
+    def end(self):
+        self.local().wait()
+        v = self.mine[...].astype(F32)
+        for k in range(3):
+            self.copy(k).wait_recv()
+            v = v + self.rz[k].astype(F32)
+        self.out[...] = v
+        for k in range(3):
+            self.copy(k).wait_send()
+
+
+def weights_in_kernel(w_ref, wm_ref, x_ref, base_ref, out_ref, zm_ref, xo_ref, bias_h, ga, gb, gc, la, lb, lc, xa, xb, xc, ya, yb, yc, tile, tsem):
     gat = Gather(w_ref, out_ref, ga, gb, gc)
-    exc = Exchange(x_ref, xo_ref, xa, xb, xc)
+    lin = LineGather(wm_ref, zm_ref, la, lb, lc)
+    exc = Exchange(x_ref, xo_ref, xa, xb, xc, (0, 2))
+    rest = Exchange(x_ref, xo_ref, ya, yb, yc, (1, 2))
     meet_all()
     gat.start()
     exc.start()
-    for k in (1, 2, 3):
-        gat.line(k)
-    for kz in range(NZ):
-        gat.plane(kz)
+
+    def flush(h):
+        return pltpu.make_async_copy(tile.at[h % 2], bias_h.at[h], tsem.at[h % 2])
+
+    def head(h, carry):
+        @pl.when(h >= 2)
+        def _():
+            flush(h - 2).wait()
+
+        bias_tiles(base_ref, h, tile.at[h % 2])
+        flush(h).start()
+        return carry
+
+    lax.fori_loop(0, H, head, 0)
+    gat.line(1)
+    gat.hop(0)
+    gat.line(2)
+    gat.line(3)
+    lin.start()
+    gat.diag(0)
+    for kz in range(1, NZ):
+        gat.hop(kz)
+    rest.start()
+    for kz in range(1, NZ):
+        gat.diag(kz)
+    flush(H - 2).wait()
+    flush(H - 1).wait()
     gat.end()
     exc.end()
-
-
-def weights_in(w, x, cid):
+    rest.end()
+    lin.end()
+
+
+def weights_in(w, wm, x, base, cid):
     return pl.pallas_call(
-        weights_in_kernel, in_specs=[ANY, ANY], out_specs=[ANY, ANY],
-        out_shape=[sds((ND,) + w.shape, w.dtype), sds(x.shape, x.dtype)],
-        scratch_shapes=Gather.sems() + Exchange.sems(),
-        compiler_params=params(16, cid), name="weights_in")(w, x)
+        weights_in_kernel, in_specs=[ANY, ANY, ANY, VM], out_specs=[ANY] * 4,
+        out_shape=[sds((ND,) + w.shape, w.dtype), sds((NZ,) + wm.shape, w.dtype), sds(x.shape, x.dtype), sds((H, NBK, BLK, BLK), F32)],
+        scratch_shapes=Gather.sems() + LineGather.sems() + Exchange.sems() * 2 + [pltpu.VMEM((2, NBK, BLK, BLK), F32), DMA((2,))],
+        compiler_params=params(24, cid), name="weights_in")(w, wm, x, base)
 
 
 def grads_out_kernel(n, *refs):
     gs, small, gt = refs[:n], refs[n], refs[n + 1]
     outs, osmall, go = refs[n + 2:2 * n + 2], refs[2 * n + 2], refs[2 * n + 3]
     refs = refs[2 * n + 4:]
-    nb = len(Scatter.bufs(gs[0].shape))
+    nb = len(Scatter.bufs(8, D))
     mc, mx, mz, ms, mr, e1, e2, e3 = refs[:8]
-    sca = [Scatter(gs[j], outs[j], *refs[8 + j * nb:8 + (j + 1) * nb]) for j in range(n)]
+    sca = [Scatter(gs[j], pl.ds(0, D), [outs[j]], *refs[8 + j * nb:8 + (j + 1) * nb]) for j in range(n)]
     s, z, c = place()
     zs, ss, co = partners(s, z, c)
     exc = Exchange(gt, go, e1, e2, e3)
@@ -307,24 +496,28 @@
     first = remote(small, mc, ms.at[0], mr.at[0], co)
     first.start()
     for a in sca:
-        a.start()
-    exc.start()
+        a.start((3,))
+    for a in sca:
+        a.start((2, 1, 0))
     first.wait_recv()
     mx[s] = small[...] + mc[...]
     xy = [remote(mx.at[s], mx.at[s], ms.at[k], mr.at[k], ss[k - 1]) for k in (1, 2, 3)]
     for cp in xy:
         cp.start()
-    sca[0].plane(0, 16)
+    every = (1, 2, 3, 0)
+    for a in sca:
+        a.away(every)
     for cp in xy:
         cp.wait_recv()
     mz[z] = (mx[0] + mx[1]) + (mx[2] + mx[3])
     zz = [remote(mz.at[z], mz.at[z], ms.at[3 + k], mr.at[3 + k], zs[k - 1]) for k in (1, 2, 3)]
     for cp in zz:
         cp.start()
-    for j in range(1, n):
-        sca[j].plane(0, 16)
-        sca[j - 1].line(0, 4)
-    sca[n - 1].line(0, 4)
+    for a in sca:
+        a.near(every)
+    exc.start()
+    for a in sca:
+        a.line(every)
     for cp in zz:
         cp.wait_recv()
     osmall[...] = (mz[0] + mz[1]) + (mz[2] + mz[3])
@@ -342,7 +535,7 @@
         functools.partial(grads_out_kernel, len(gs)),
         in_specs=[ANY] * len(gs) + [VM, ANY], out_specs=[VM] * (len(gs) + 1) + [ANY],
         out_shape=[sds(g.shape[1:], F32) for g in gs] + [sds(small.shape, F32), sds(gt.shape, BF)],
-        scratch_shapes=[sm, sm4, sm4, DMA((7,)), DMA((7,))] + Exchange.sems() + sum([Scatter.bufs(g.shape) for g in gs], []),
+        scratch_shapes=[sm, sm4, sm4, DMA((7,)), DMA((7,))] + Exchange.sems() + sum([Scatter.bufs(*g.shape[1:]) for g in gs], []),
         compiler_params=params(56, cid), name="grads_out")(*gs, small, gt)
 
 
@@ -386,11 +579,18 @@
     return [slice(i * BLK, (i + 1) * BLK) for i in range(n)]
 
 
+HOPS = [("hop", k) for k in range(NZ)]
+FWD_PLAN = ((2, [("exc", 0)]), (5, HOPS + [("exc", 1)]))
+CROSS_PLAN = ((4, HOPS),)
+
+
 def self_fwd_kernel(near, st_ref, x_ref, w_ref, gn_ref, bias_ref, mpre_ref, mpost_ref, *refs):
     if near:
-        wm_h, enc_h, q_ref, k_ref, v_ref, att_ref, gain_ref, p_ref, wo_h, eo_h, acc_ref, lo_ref, ags, exs = split(refs, 12, 3, 3)
-        gat = Gather(wm_h, wo_h, *ags)
-        exc = Exchange(enc_h, eo_h, *exs)
+        (zm_h, wf_h, enc_h, cot_h, q_ref, k_ref, v_ref, att_ref, gain_ref, p_ref, wo_h, zf_h, eo_h, co_h, acc_ref, lo_ref,
+         ags, lgs, ex1, ex2) = split(refs, 16, 3, 3, 3, 3)
+        gat = PlaneGather(zm_h, wo_h, *ags)
+        lin = LineGather(wf_h, zf_h, *lgs)
+        exc = [Exchange(enc_h, eo_h, *ex1), Exchange(cot_h, co_h, *ex2)]
     else:
         q_ref, k_ref, v_ref, att_ref, gain_ref, p_ref, acc_ref, lo_ref = refs
     h = pl.program_id(0)
@@ -400,14 +600,16 @@
         def _():
             meet_all()
             gat.start()
-            exc.start()
-
-        for hh, fns in ((2, [lambda: gat.line(1)]), (3, [lambda: gat.line(2), lambda: gat.line(3)]),
-                        (7, [lambda: gat.plane(0), lambda: gat.plane(1)]), (9, [lambda: gat.plane(2), lambda: gat.plane(3)])):
+            lin.start()
+
+        for hh, todo in FWD_PLAN:
             @pl.when(h == hh)
-            def _(fns=fns):
-                for f in fns:
-                    f()
+            def _(todo=todo):
+                for name, k in todo:
+                    if name == "exc":
+                        exc[k].start()
+                    else:
+                        getattr(gat, name)(k)
 
     @pl.when(h == 0)
     def _():
@@ -452,34 +654,40 @@
     def _():
         att_ref[...] = acc_ref[...].astype(BF)
         if near:
+            lin.end()
+            for k in range(NZ):
+                gat.diag(k)
             gat.end()
-            exc.end()
+            for e in exc:
+                e.end()
 
 
 def self_fwd(starts, x, w1, bias, mpre, mpost, far=None, cid=None):
     one = cst((L, D))
     near = far is not None
-    extra_out = [sds((ND,) + far[0].shape, BF), sds(far[1].shape, BF)] if near else []
+    extra_out = []
+    if near:
+        extra_out = [sds((ND,) + far[0].shape[1:], BF), sds((NZ,) + far[1].shape, BF)] + [sds(f.shape, BF) for f in far[2:]]
     return pl.pallas_call(
         functools.partial(self_fwd_kernel, near),
         grid_spec=pltpu.PrefetchScalarGridSpec(
             num_scalar_prefetch=1, grid=(H,),
             in_specs=[one, col((D, 3 * D), 0), col((D, 128), 18),
                       pl.BlockSpec((1, NBK, BLK, BLK), lambda h, st: (h, 0, 0, 0)), cst((H, D)), cst((H, D))]
-            + [ANY] * (2 * near),
-            out_specs=[one] * 4 + [cst((8, D)), pl.BlockSpec((1, L, L), lambda h, st: (h, 0, 0))] + [ANY] * (2 * near),
+            + [ANY] * (4 * near),
+            out_specs=[one] * 4 + [cst((8, D)), pl.BlockSpec((1, L, L), lambda h, st: (h, 0, 0))] + [ANY] * (4 * near),
             scratch_shapes=[pltpu.VMEM((L, D), F32), pltpu.VMEM((L, 128), jnp.int32)]
-            + (Gather.sems() + Exchange.sems() if near else [])),
+            + (PlaneGather.sems() + LineGather.sems() + Exchange.sems() * 2 if near else [])),
         out_shape=[sds((L, D), BF)] * 4 + [sds((8, D), F32), sds((H, L, L), BF)] + extra_out,
-        compiler_params=params(56, cid),
+        compiler_params=params(62, cid),
         cost_estimate=pl.CostEstimate(flops=52_000_000_000, bytes_accessed=45_000_000, transcendentals=8_000_000),
         name="self_fwd")(starts, x, w1, w1, bias, mpre, mpost, *(far or ()))
 
 
 def cross_fwd_kernel(near, x_ref, att_ref, wo_ref, wq_ref, wk_ref, wv_ref, enc_ref, gain_ref, *refs):
     if near:
-        cot_h, h1_ref, n2_ref, q_ref, k_ref, v_ref, catt_ref, p_ref, co_h, exs = split(refs, 9, 3)
-        exc = Exchange(cot_h, co_h, *exs)
+        zf_h, h1_ref, n2_ref, q_ref, k_ref, v_ref, catt_ref, p_ref, fo_h, ags = split(refs, 9, 3)
+        gat = PlaneGather(zf_h, fo_h, *ags)
     else:
         h1_ref, n2_ref, q_ref, k_ref, v_ref, catt_ref, p_ref = refs
     h = pl.program_id(0)
@@ -487,8 +695,14 @@
     if near:
         @pl.when(h == 0)
         def _():
-            meet_seq()
-            exc.start()
+            meet_all()
+            gat.start()
+
+        for hh, todo in CROSS_PLAN:
+            @pl.when(h == hh)
+            def _(todo=todo):
+                for name, k in todo:
+                    getattr(gat, name)(k)
 
     @pl.when(h == 0)
     def _():
@@ -529,7 +743,9 @@
     if near:
         @pl.when(h == H // 2 - 1)
         def _():
-            exc.end()
+            for k in range(NZ):
+                gat.diag(k)
+            gat.end()
 
 
 def cross_fwd(x, att, wmid, enc, gains, far=None, cid=None):
@@ -539,11 +755,12 @@
         functools.partial(cross_fwd_kernel, near), grid=(H // 2,),
         in_specs=[one, one] + [col((D, D), j) for j in range(4)] + [one, cst((8, D))] + [ANY] * near,
         out_specs=[one] * 6 + [pl.BlockSpec((2, L, L), lambda h: (h, 0, 0))] + [ANY] * near,
-        out_shape=[sds((L, D), F32)] + [sds((L, D), BF)] * 5 + [sds((H, L, L), BF)] + [sds(f.shape, BF) for f in far or ()],
-        scratch_shapes=Exchange.sems() if near else [],
-        compiler_params=params(56, cid),
+        out_shape=[sds((L, D), F32)] + [sds((L, D), BF)] * 5 + [sds((H, L, L), BF)]
+        + ([sds((ND,) + far.shape[1:], BF)] if near else []),
+        scratch_shapes=PlaneGather.sems() if near else [],
+        compiler_params=params(62, cid),
         cost_estimate=pl.CostEstimate(flops=31_000_000_000, bytes_accessed=50_000_000, transcendentals=12_000_000),
-        name="cross_fwd")(x, att, wmid, wmid, wmid, wmid, enc, gains, *(far or ()))
+        name="cross_fwd")(x, att, wmid, wmid, wmid, wmid, enc, gains, *([far] if near else []))
 
 
 def feed_kernel(h1_ref, catt_ref, wco_ref, cot_ref, gain_ref, fi_ref, fo_ref,
@@ -600,49 +817,66 @@
         out_shape=[sds((L, D), BF), sds((L, D), F32), sds((L, D), BF), sds((D, wfeed.shape[1]), BF), sds((8, D), F32)],
         scratch_shapes=[pltpu.VMEM((L, D), BF), pltpu.VMEM((D, L), BF), pltpu.VMEM((D, L), BF), pltpu.VMEM((L, D), F32),
                         pltpu.VMEM((L, D), F32), pltpu.VMEM((L, D), BF), pltpu.VMEM((L, D), BF)],
-        compiler_params=pltpu.CompilerParams(vmem_limit_bytes=60 << 20),
+        compiler_params=pltpu.CompilerParams(vmem_limit_bytes=62 << 20),
         cost_estimate=pl.CostEstimate(flops=32_000_000_000, bytes_accessed=50_000_000, transcendentals=3_000_000),
         name="feed")(h1, catt, wmid, cot, gains, wfeed, wfeed)
 
 
-def cross_bwd_kernel(q_ref, k_ref, v_ref, do_ref, p_ref, gain_ref,
-                     n2_h, enc_h, att_h, catt_h, h1_h, bh2_h, w_h,
-                     gw_ref, genc_ref, bh1_ref, bat_ref, dg_ref,
-                     qt, dot_, ds, dq, dk, dv, n2, enc, att, catt, h1, bh2, w, sems):
+def cross_bwd_kernel(near, q_ref, k_ref, v_ref, do_ref, p_ref, gain_ref, n2_h, enc_h, att_h, catt_h, h1_h, bh2_h, w_h, *refs):
+    if near:
+        gf_h = refs[0]
+        gw_ref, genc_ref, bh1_ref, bat_ref, dg_ref, rf_ref = refs[1:7]
+        qt, dot_, ds, dq, dk, dv, n2, enc, att, catt, h1, w, sems, sca = split(refs[7:], 13, len(Scatter.bufs(8, D)))
+        sca = Scatter(gf_h, pl.ds(0, gf_h.shape[2]), [], *sca)
+    else:
+        gw_ref, genc_ref, bh1_ref, bat_ref, dg_ref = refs[:5]
+        qt, dot_, ds, dq, dk, dv, n2, enc, att, catt, h1, w, sems = refs[5:]
     h = pl.program_id(0)
-    late = [(n2_h, n2), (enc_h, enc), (att_h, att), (catt_h, catt), (h1_h, h1), (bh2_h, bh2)]
+    late = [(n2_h, n2), (enc_h, enc), (att_h, att), (catt_h, catt), (h1_h, h1), (bh2_h, bh1_ref)]
     late += [(w_h.at[:, pl.ds(0, 4 * D)], w)]
     copies = [pltpu.make_async_copy(a, b, sems.at[i]) for i, (a, b) in enumerate(late)]
 
     @pl.when(h == 0)
+    def _():
+        if near:
+            meet_all()
+            sca.start((3,))
+
+    @pl.when(h == 3)
     def _():
         for c in copies:
             c.start()
 
-    cols = pl.ds(pl.multiple_of(h * 128, 128), 128)
-    first = lax.broadcasted_iota(jnp.int32, (1, 128), 1) < DH
-    top = lax.broadcasted_iota(jnp.int32, (128, 1), 0) < DH
+    if near:
+        for hh, name, kzs in BWD_PLAN:
+            @pl.when(h == hh)
+            def _(name=name, kzs=kzs):
+                getattr(sca, name)(kzs)
+
+    e = h % 2
+    cols = pl.ds(pl.multiple_of((h // 2) * 128, 128), 128)
+    fe = (lax.broadcasted_iota(jnp.int32, (1, 128), 1) // DH) == e
     k = k_ref[...]
     v = v_ref[...]
-    qt[...] = q_ref[...].T
-    dot_[...] = do_ref[...].T
-    dks, dvs = [], []
-    for e in range(2):
-        fe = first if e == 0 else ~first
-        for r in blocks():
-            do = do_ref[r, :]
-            dp = dot(jnp.where(fe, do, jnp.zeros_like(do)), v, 1, 1)
-            p = p_ref[e, r, :].astype(F32)
-            d = (p * (dp - jnp.sum(dp * p, 1, keepdims=True))).astype(BF)
-            ds[e, r, :] = d
-            o = dot(d, k, 1, 0).astype(BF)
-            dq[r, cols] = o if e == 0 else jnp.where(first, dq[r, cols], o)
-        dvs.append(dot(dot_[...], p_ref[e], 1, 0))
-        dks.append(dot(qt[...], ds[e], 1, 0))
-    dk[:, cols] = jnp.where(top, dks[0], dks[1]).T.astype(BF)
-    dv[:, cols] = jnp.where(top, dvs[0], dvs[1]).T.astype(BF)
-
-    @pl.when(h == H // 2 - 1)
+
+    @pl.when(e == 0)
+    def _():
+        qt[...] = q_ref[...].T
+        dot_[...] = do_ref[...].T
+
+    for r in blocks():
+        do = do_ref[r, :]
+        dp = dot(jnp.where(fe, do, jnp.zeros_like(do)), v, 1, 1)
+        p = p_ref[0, r, :].astype(F32)
+        d = (p * (dp - jnp.sum(dp * p, 1, keepdims=True))).astype(BF)
+        ds[r, :] = d
+        dq[r, cols] = jnp.where(fe, dot(d, k, 1, 0).astype(BF), dq[r, cols])
+    x = dot(dot_[...], p_ref[0], 1, 0).T.astype(BF)
+    dv[:, cols] = jnp.where(fe, x, dv[:, cols])
+    x = dot(qt[...], ds[...], 1, 0).T.astype(BF)
+    dk[:, cols] = jnp.where(fe, x, dk[:, cols])
+
+    @pl.when(h == H - 1)
     def _():
         for c in copies:
             c.wait()
@@ -655,7 +889,7 @@
             genc_ref[r, :] = (dot(dk[r, :], w[:, 2 * D:3 * D], 1, 1) + dot(dv[r, :], w[:, 3 * D:], 1, 1)).astype(genc_ref.dtype)
             dx, s = norm_grad(h1[r, :], g, dot(dq[r, :], w[:, D:2 * D], 1, 1))
             dg = dg + s
-            b2 = bh2[r, :]
+            b2 = bh1_ref[r, :]
             b1 = b2 + dx
             bh1_ref[r, :] = b1
             b1 = b1.astype(BF)
@@ -665,30 +899,44 @@
         gw_ref[:, :D] = dot(att[...], n2[...], 0, 0).astype(BF)
         gw_ref[:, 4 * D:] = dot(catt[...], enc[...], 0, 0).astype(BF)
         dg_ref[...] = dg
-
-
-def cross_bwd(q, k, v, do, p, gains, n2, enc, att, catt, h1, bh2, wmid):
+        if near:
+            sca.stop(rf_ref)
+
+
+EVERY = (1, 2, 3, 0)
+BWD_PLAN = ((1, "away", EVERY), (1, "start", (2, 1)), (3, "start", (0,)), (6, "near", EVERY))
+
+
+def cross_bwd(q, k, v, do, p, gains, n2, enc, att, catt, h1, bh2, wmid, far=None, cid=None):
     one = cst((L, D))
-    pair = pl.BlockSpec((L, 128), lambda h: (0, h))
+    near = far is not None
+    pair = pl.BlockSpec((L, 128), lambda h: (0, h // 2))
     act = pltpu.VMEM((L, D), BF)
+    more = [(NZ,) + far.shape[1:]] if near else []
     return pl.pallas_call(
-        cross_bwd_kernel, grid=(H // 2,),
-        in_specs=[pair] * 4 + [pl.BlockSpec((2, L, L), lambda h: (h, 0, 0)), cst((8, D))] + [ANY] * 7,
-        out_specs=[cst((D, 5 * D)), one, one, one, cst((8, D))],
-        out_shape=[sds((D, 5 * D), BF), sds((L, D), BF), sds((L, D), F32), sds((L, D), BF), sds((8, D), F32)],
-        scratch_shapes=[pltpu.VMEM((128, L), BF)] * 2 + [pltpu.VMEM((2, L, L), BF)] + [act] * 7
-        + [pltpu.VMEM((L, D), F32)] * 2 + [pltpu.VMEM((D, 4 * D), BF), DMA((7,))],
-        compiler_params=pltpu.CompilerParams(vmem_limit_bytes=60 << 20),
+        functools.partial(cross_bwd_kernel, near), grid=(H,),
+        in_specs=[pair] * 4 + [pl.BlockSpec((1, L, L), lambda h: (h, 0, 0)), cst((8, D))] + [ANY] * (7 + near),
+        out_specs=[cst((D, 5 * D)), one, one, one, cst((8, D))] + [cst(s) for s in more],
+        out_shape=[sds((D, 5 * D), BF), sds((L, D), BF), sds((L, D), F32), sds((L, D), BF), sds((8, D), F32)]
+        + [sds(s, BF) for s in more],
+        scratch_shapes=[pltpu.VMEM((128, L), BF)] * 2 + [pltpu.VMEM((L, L), BF)] + [act] * 7
+        + [pltpu.VMEM((L, D), F32), pltpu.VMEM((D, 4 * D), BF), DMA((7,))] + sum([Scatter.bufs(*s[1:]) for s in more], []),
+        compiler_params=params(62, cid),
         cost_estimate=pl.CostEstimate(flops=37_000_000_000, bytes_accessed=70_000_000, transcendentals=0),
-        name="cross_bwd")(q, k, v, do, p, gains, n2, enc, att, catt, h1, bh2, wmid)
+        name="cross_bwd")(q, k, v, do, p, gains, n2, enc, att, catt, h1, bh2, wmid, *([far] if near else []))
+
+
+SELF_PLAN = ((1, "away", EVERY), (1, "start", (2, 1, 0)), (3, "near", EVERY), (3, "exc", 0), (6, "exc", 1), (8, "line", EVERY))
 
 
 def self_bwd_kernel(near, q_ref, k_ref, v_ref, ba_ref, p_ref, mpre_ref, mpost_ref, gain_ref, x_h, bh1_h, w_h, *refs):
     if near:
-        gm_h, out_h, ge_h = refs[:3]
-        gq_ref, gk_ref, gv_ref, gtok_ref, gpre_ref, gpost_ref, diag_ref, dg_ref, rm_ref, oo_h, go_h = refs[3:14]
-        qt, bat, dqa, dkt, dvt, dm, x, bh1, w, sems, sca, ex1, ex2 = split(refs[14:], 10, len(Scatter.bufs(gm_h.shape)), 3, 3)
-        sca = Scatter(gm_h, rm_ref, *sca)
+        gm_h, zf_h, out_h, ge_h = refs[:4]
+        gq_ref, gk_ref, gv_ref, gtok_ref, gpre_ref, gpost_ref, diag_ref, dg_ref = refs[4:12]
+        rms, (rf_ref, oo_h, go_h) = refs[12:17], refs[17:20]
+        qt, bat, dqa, dkt, dvt, dm, x, bh1, w, sems, sca, lin, ex1, ex2 = split(refs[20:], 10, len(Scatter.bufs(8, D)), 5, 3, 3)
+        lin = LineScatter(zf_h, rf_ref, *lin)
+        sca = Scatter(gm_h, pl.ds(0, gm_h.shape[2]), rms, *sca)
         exc = [Exchange(out_h, oo_h, *ex1), Exchange(ge_h, go_h, *ex2)]
     else:
         gq_ref, gk_ref, gv_ref, gtok_ref, gpre_ref, gpost_ref, diag_ref, dg_ref = refs[:8]
@@ -699,19 +947,17 @@
         @pl.when(h == 0)
         def _():
             meet_all()
-            sca.start()
-            for e in exc:
-                e.start()
-
-        for hh, lo, hi in ((1, 0, 6), (2, 6, 12), (3, 12, 16)):
+            sca.start((3,))
+            lin.start()
+
+        for hh, name, kzs in SELF_PLAN:
             @pl.when(h == hh)
-            def _(lo=lo, hi=hi):
-                sca.plane(lo, hi)
-
-        for hh, lo, hi in ((9, 0, 2), (10, 2, 4)):
-            @pl.when(h == hh)
-            def _(lo=lo, hi=hi):
-                sca.line(lo, hi)
+            def _(name=name, kzs=kzs):
+                if name == "exc":
+                    exc[kzs].start()
+                else:
+                    getattr(sca, name)(kzs)
+
     late = [(x_h, x), (bh1_h, bh1), (w_h.at[:, pl.ds(0, 3 * D)], w)]
     copies = [pltpu.make_async_copy(a, b, sems.at[i]) for i, (a, b) in enumerate(late)]
 
@@ -787,6 +1033,7 @@
         gv_ref[...] = dot(bat[...], dvt[...].astype(BF), 1, 1).astype(BF)
         dg_ref[...] = dg
         if near:
+            lin.end()
             sca.end()
             for e in exc:
                 e.end()
@@ -795,19 +1042,22 @@
 def self_bwd(q, k, v, ba, p, mpre, mpost, gains, x, bh1, w1, far=None, cid=None):
     one = cst((L, D))
     near = far is not None
-    more = [cst(far[0].shape[1:]), ANY, ANY] if near else []
-    more_out = [sds(far[0].shape[1:], F32)] + [sds(f.shape, BF) for f in far[1:]] if near else []
+    rows = far[0].shape[1] if near else 0
+    more = [cst((rows, D))] * 5 + [cst(far[1].shape[1:]), ANY, ANY] if near else []
+    more_out = []
+    if near:
+        more_out = [sds((rows, D), F32)] * 5 + [sds(far[1].shape[1:], F32)] + [sds(f.shape, BF) for f in far[2:]]
     return pl.pallas_call(
         functools.partial(self_bwd_kernel, near), grid=(H,),
-        in_specs=[one] * 4 + [pl.BlockSpec((1, L, L), lambda h: (h, 0, 0)), cst((H, D)), cst((H, D)), cst((8, D))] + [ANY] * (3 + 3 * near),
+        in_specs=[one] * 4 + [pl.BlockSpec((1, L, L), lambda h: (h, 0, 0)), cst((H, D)), cst((H, D)), cst((8, D))] + [ANY] * (3 + 4 * near),
         out_specs=[cst((D, D))] * 3 + [one, cst((H, D)), cst((H, D)),
                    pl.BlockSpec((1, NBK, 1, 2 * BLK), lambda h: (h, 0, 0, 0)), cst((8, D))] + more,
         out_shape=[sds((D, D), BF)] * 3 + [sds((L, D), BF), sds((H, D), F32), sds((H, D), F32),
                    sds((H, NBK, 1, 2 * BLK), F32), sds((8, D), F32)] + more_out,
         scratch_shapes=[pltpu.VMEM((D, L), BF)] * 2 + [pltpu.VMEM((L, D), F32)] + [pltpu.VMEM((D, L), F32)] * 2
         + [pltpu.VMEM((L, L), BF), pltpu.VMEM((L, D), BF), pltpu.VMEM((L, D), F32), pltpu.VMEM((D, 3 * D), BF), DMA((3,))]
-        + (Scatter.bufs(far[0].shape) + Exchange.sems() * 2 if near else []),
-        compiler_params=params(61, cid),
+        + (Scatter.bufs(*far[0].shape[1:]) + LineScatter.bufs(*far[1].shape[1:]) + Exchange.sems() * 2 if near else []),
+        compiler_params=params(62, cid),
         cost_estimate=pl.CostEstimate(flops=128_000_000_000, bytes_accessed=50_000_000, transcendentals=0),
         name="self_bwd")(q, k, v, ba, p, mpre, mpost, gains, x, bh1, w1, *(far or ()))
 
@@ -833,43 +1083,49 @@
     near = nseq == NS and ndp == NZ * NCORE and rows % 8 == 0
     to_stream = lambda x: lax.all_to_all(x, "seq", 0, 1, tiled=True).reshape(L, D)
     from_stream = lambda x: lax.all_to_all(x.reshape(1, L, D), "seq", 1, 0, tiled=True)
+    hot = (rel_bucket[:, None] == jnp.arange(buckets)[None, :]).astype(F32)
+    trow = lax.dot_general(rel_table, hot, (((0,), (1,)), ((), ())), precision=lax.Precision.HIGHEST)
+    base = make_base(trow)
     gains = jnp.pad(jnp.stack([gs, gc, gf], 1), ((0, 0), (0, 125)))
     w1 = jnp.concatenate([sq, sk, sv, gains], 1)
     wmid = jnp.concatenate([so, cq, ck, cv, co], 1)
     wfeed = jnp.stack([fi.reshape(rows, D, nf).transpose(0, 2, 1), fo.reshape(rows, nf, D)], 2).reshape(rows, 2 * nf * D)
     if near:
-        w1, x = weights_in(w1, tokens, 1)
+        w1, zmid, x, bias = weights_in(w1, wmid, tokens, base, 1)
         w1 = w1.reshape(D, -1)
         x = x.reshape(L, D)
     else:
         w1 = gather(w1)
         x = to_stream(tokens)
+        bias = toeplitz(base)
         wmid = gather(wmid)
+        wfeed = gather(wfeed)
         enc = to_stream(encoded)
         cot = to_stream(cotangent)
-    wfeed = gather(wfeed)
     starts = lax.dynamic_index_in_dim(doc_starts, lax.axis_index("seq"), 0, keepdims=False)
-    hot = (rel_bucket[:, None] == jnp.arange(buckets)[None, :]).astype(F32)
-    trow = lax.dot_general(rel_table, hot, (((0,), (1,)), ((), ())), precision=lax.Precision.HIGHEST)
-    bias = toeplitz(make_base(trow))
     mpre = jnp.repeat(mix_pre.T, DH, axis=1)
     mpost = jnp.repeat(mix_post, DH, axis=1)
     if near:
-        q, k, v, att, gain, p, wmid, enc = self_fwd(starts, x, w1, bias, mpre, mpost, (wmid, encoded), 2)
+        q, k, v, att, gain, p, wmid, zfeed, enc, cot = self_fwd(starts, x, w1, bias, mpre, mpost, (zmid, wfeed, encoded, cotangent), 2)
         wmid = wmid.reshape(D, -1)
         enc = enc.reshape(L, D)
-        h1, n2, cqx, ckx, cvx, catt, cp, cot = cross_fwd(x, att, wmid, enc, gain, (cotangent,), 3)
+        h1, n2, cqx, ckx, cvx, catt, cp, wfeed = cross_fwd(x, att, wmid, enc, gain, zfeed, 3)
         cot = cot.reshape(L, D)
+        wfeed = wfeed.reshape(D, -1)
     else:
         q, k, v, att, gain, p = self_fwd(starts, x, w1, bias, mpre, mpost)
         h1, n2, cqx, ckx, cvx, catt, cp = cross_fwd(x, att, wmid, enc, gain)
     out, bh2, bca, gw_feed, dgf = feed(h1, catt, wmid, cot, gain, wfeed)
-    r_feed = scatter(gw_feed).reshape(rows, nf, 2, D)
-    gw_mid, g_enc, bh1, bat, dgc = cross_bwd(cqx, ckx, cvx, bca, cp, gain, n2, enc, att, catt, h1, bh2, wmid)
+    back = (cqx, ckx, cvx, bca, cp, gain, n2, enc, att, catt, h1, bh2, wmid)
+    if near:
+        gw_mid, g_enc, bh1, bat, dgc, zfeed = cross_bwd(*back, gw_feed.reshape(ndev, rows, -1), 6)
+    else:
+        gw_mid, g_enc, bh1, bat, dgc = cross_bwd(*back)
+        r_feed = scatter(gw_feed)
     blk = lambda a: a.reshape(nseq, L // nseq, D)
     if near:
-        far = (gw_mid.reshape(ndev, rows, -1), blk(out), blk(g_enc))
-        gw_q, gw_k, gw_v, g_tok, gpre, gpost, diag, dgs, r_mid, out, g_enc = self_bwd(
+        far = (gw_mid.reshape(ndev, rows, -1), zfeed, blk(out), blk(g_enc))
+        gw_q, gw_k, gw_v, g_tok, gpre, gpost, diag, dgs, *r_mid, r_feed, out, g_enc = self_bwd(
             q, k, v, bat, p, mpre, mpost, gain, x, bh1, w1, far, 4)
     else:
         gw_q, gw_k, gw_v, g_tok, gpre, gpost, diag, dgs = self_bwd(q, k, v, bat, p, mpre, mpost, gain, x, bh1, w1)
@@ -895,14 +1151,15 @@
             o += a.size
         dgain, gpre, gpost, gtab = got
     else:
-        r_mid, r_q, r_k, r_v = scatter(gw_mid), scatter(gw_q), scatter(gw_k), scatter(gw_v)
+        r_mid = jnp.split(scatter(gw_mid), 5, 1)
+        r_q, r_k, r_v = scatter(gw_q), scatter(gw_k), scatter(gw_v)
         out, g_tok, g_enc = from_stream(out), from_stream(g_tok), from_stream(g_enc)
         dgain, gpre, gpost, gtab = lax.psum((dgain, gpre, gpost, gtab), AX)
+    r_feed = r_feed.reshape(rows, nf, 2, D)
     me = lax.axis_index("seq") * ndp + lax.axis_index("dp")
     dgain = lax.dynamic_slice_in_dim(dgain, me * rows, rows, 1)
-    m = lambda a, j: a[:, j * D:(j + 1) * D]
     return (out, g_tok.astype(F32), g_enc.astype(F32),
-            r_q, r_k, r_v, m(r_mid, 0), m(r_mid, 1), m(r_mid, 2), m(r_mid, 3), m(r_mid, 4),
+            r_q, r_k, r_v, *r_mid,
             r_feed[:, :, 0].transpose(0, 2, 1).reshape(rows, nf * D), r_feed[:, :, 1].reshape(rows * nf, D),
             dgain[0], dgain[1], dgain[2], gpre, gpost, gtab)
 

time: 495 us -> 453 us (0.915)
  Pallas kernels: 432 us -> 400 us
  between operations: 14.9 us -> 1.49 us
    pallas_call x1, Pallas kernels: 108 us -> 92.7 us  [self_bwd(): pl.pallas_call(functools.partial(self_bwd_kernel, near), grid=(H,), in_sp...]
    pallas_call x3 -> x2, Pallas kernels: 116 us -> 101 us  [the longest x1 60.4 us: cross_bwd(): pl.pallas_call(functools.partial(cross_bwd_kernel, near), grid=(H,), in_s...]
    pallas_call x1, Pallas kernels: 40.3 us -> 54.7 us  [cross_fwd(): pl.pallas_call(functools.partial(cross_fwd_kernel, near), grid=(H // 2,),...]
    pallas_call x1, Pallas kernels: 48.3 us -> 39.6 us  [grads_out(): pl.pallas_call(functools.partial(grads_out_kernel, len(gs)), in_specs=[AN...]
    pallas_call x1, Pallas kernels: 75.4 us -> 67.2 us  [self_fwd(): pl.pallas_call(functools.partial(self_fwd_kernel, near), grid_spec=pltpu....]
    unnamed x79 -> x92, local copies, waits for them, and re-layouts: 11.6 us -> 18.5 us
  transfers between devices with their start and end apart: 2 -> 0, of which waited for: 0 -> 0; matrix products, arithmetic and copies ran while one was open for 5% -> 0% of each run, Pallas kernels for 80% -> 0%
where the time goes in v4:
time: 453 us; the launch traced here: 444 us
  Pallas kernels  400 us (88%)
  local copies, waits for them, and re-layouts  34.9 us (8%)
  other arithmetic  5.79 us (1%)
    pallas_call x1, Pallas kernels, self_bwd(): pl.pallas_call(functools.partial(self_bwd_kernel, near), grid=(H,), in_sp...  92.7 us
    pallas_call x1, Pallas kernels, self_fwd(): pl.pallas_call(functools.partial(self_fwd_kernel, near), grid_spec=pltpu....  67.2 us
    pallas_call x1, Pallas kernels, cross_bwd(): pl.pallas_call(functools.partial(cross_bwd_kernel, near), grid=(H,), in_s...  60.4 us
    pallas_call x1, Pallas kernels, cross_fwd(): pl.pallas_call(functools.partial(cross_fwd_kernel, near), grid=(H // 2,),...  54.7 us
    pallas_call x1, Pallas kernels, feed(): pl.pallas_call(feed_kernel, grid=(nf,), in_specs=[one, one, col((D, D), 4...  44.5 us
    pallas_call x1, Pallas kernels, weights_in(): pl.pallas_call(weights_in_kernel, in_specs=[ANY, ANY, ANY, VM], out_specs...  41 us
    pallas_call x1, Pallas kernels, grads_out(): pl.pallas_call(functools.partial(grads_out_kernel, len(gs)), in_specs=[AN...  39.6 us
    unnamed x92, local copies, waits for them, and re-layouts  18.5 us

profile of v4, /device:TPU:0, one launch (start us, length us, event | category | flops | bytes accessed | tf_op | source)
XLA Modules:
  0.0 443.9 jit_solution(7090420264432173462)
XLA Ops:
  0.8 1.3 dynamic-slice_bitcast_fusion.st_ref
  3.7 1.1 convolution_bitcast_fusion
  9.8 0.9 reshape.140.refs_1_
  10.8 41.0 %weights_in.1 = (bf16[32,24,2432]{2,1,0:T(8,128)(2,1)S(1)}, bf16[4,24,3840]{2,1,0:T(8,128)(2,1)S(1)}, bf16[4,256,768]{2,1,0:T(8,128)(2,1)S(1)}, f32[12,4,256,256]{3,2,1,0:T(8,128)S(1)}) custom-call(bf16[24,2432]{1,0:T(8,128)(2,1)S(1)} %fusion.6.w_ref, bf16[24,3840]{1,0:T(8,128)(2,1)S(1)} %constant_dynamic-update-slice_fusion.wm_ref, ...), custom_call_target="tpu_custom_call" | custom-call | tf_op jit(solution)/shard_map/weights_in/pallas_call | solution.py:478
  51.8 4.5 %copy-done.3 = f32[12,4,256,256]{3,2,1,0:T(8,128)} copy-done((f32[12,4,256,256]{3,2,1,0:T(8,128)}, f32[12,4,256,256]{3,2,1,0:T(8,128)S(1)}, u32[]{:S(2)}) %copy-start.3) | copy-done | bytes 12582936
  56.2 1.8 copy-done.4
  58.1 1.1 copy-done.5
  59.2 0.9 copy-done.6
  60.1 67.2 %self_fwd.1 = (bf16[1024,768]{1,0:T(8,128)(2,1)}, bf16[1024,768]{1,0:T(8,128)(2,1)}, bf16[1024,768]{1,0:T(8,128)(2,1)}, bf16[1024,768]{1,0:T(8,128)(2,1)}, f32[8...) custom-call(s32[4]{0:T(128)} %dynamic-slice_bitcast_fusion.st_ref, ...), custom_call_target="tpu_custom_call" | custom-call | flops 51999997952 | bytes 45000000 | tf_op jit(solution)/shard_map/self_fwd/pallas_call | solution.py:671
  127.3 54.7 %cross_fwd.1 = (f32[1024,768]{1,0:T(8,128)}, bf16[1024,768]{1,0:T(8,128)(2,1)}, bf16[1024,768]{1,0:T(8,128)(2,1)}, bf16[1024,768]{1,0:T(8,128)(2,1)}, bf16[1024,...) custom-call(bf16[1024,768]{1,0:T(8,128)(2,1)} %bitcast.68, ...), custom_call_target="tpu_custom_call" | custom-call | flops 31000000512 | bytes 50000000 | tf_op jit(solution)/shard_map/cross_fwd/pallas_call | solution.py:754
  181.9 44.5 %feed.1 = (bf16[1024,768]{1,0:T(8,128)(2,1)}, f32[1024,768]{1,0:T(8,128)}, bf16[1024,768]{1,0:T(8,128)(2,1)}, bf16[768,6144]{1,0:T(8,128)(2,1)}, f32[8,768]{1,0:T(8,128)}) custom-call(f32[1024,768]{1,0:T(8,128)} %get-tuple-element.88.h1_ref.h1_h, bf16[1024,768]{1,0:T(8,128)(2,1)} %get-tuple-element.89.catt_ref.catt_h, bf16[768,3840]{1,0:T(8,128)(2,1)} %bitcast.96, ...), custom_call_target="tpu_custom_call" | custom-call | flops 32000000000 | bytes 50000000 | tf_op jit(solution)/shard_map/feed/pallas_call | solution.py:812
  226.5 60.4 %cross_bwd.1 = (bf16[768,3840]{1,0:T(8,128)(2,1)}, bf16[1024,768]{1,0:T(8,128)(2,1)}, f32[1024,768]{1,0:T(8,128)}, bf16[1024,768]{1,0:T(8,128)(2,1)}, f32[8,768]{1,0:T(8,128)}, /*index=5*/bf16[4,24,6144]{2,1,0:T(8,128)(2,1)}) custom-call(bf16[1024,768]{1,0:T(8,128)(2,1)} %get-tuple-element.85.q_ref, bf16[1024,768]{1,0:T(8,128)(2,1)} %get-tuple-element.86.k_ref, ...), custom_call_target="tpu_custom_call" | custom-call | flops 36999999488 | bytes 70000000 | tf_op jit(solution)/shard_map/cross_bwd/pallas_call | solution.py:916
  286.9 92.7 %self_bwd.1 = (bf16[768,768]{1,0:T(8,128)(2,1)}, bf16[768,768]{1,0:T(8,128)(2,1)}, bf16[768,768]{1,0:T(8,128)(2,1)}, bf16[1024,768]{1,0:T(8,128)(2,1)}, f32[12,7...) custom-call(bf16[1024,768]{1,0:T(8,128)(2,1)} %get-tuple-element.77., ...), custom_call_target="tpu_custom_call" | custom-call | flops 128000000000 | bytes 50000000 | tf_op jit(solution)/shard_map/self_bwd/pallas_call | solution.py:1050
  380.5 0.9 reshape.153
  381.6 0.9 reshape.155
  382.7 2.0 rev.31
  386.3 39.6 %grads_out.1 = (f32[24,768]{1,0:T(8,128)}, f32[24,768]{1,0:T(8,128)}, f32[24,768]{1,0:T(8,128)}, f32[24,128]{1,0:T(8,128)}, bf16[4,256,768]{2,1,0:T(8,128)(2,1)}) custom-call(bf16[32,24,768]{2,1,0:T(8,128)(2,1)} %bitcast.73, bf16[32,24,768]{2,1,0:T(8,128)(2,1)} %bitcast.74, bf16[32,24,768]{2,1,0:T(8,128)(2,1)} %bitcast.75, ...), custom_call_target="tpu_custom_call" | custom-call | tf_op jit(solution)/shard_map/grads_out/pallas_call | solution.py:534
  427.2 0.8 slice.91
  429.8 1.0 slice_reduce_fusion
  430.8 0.8 reshape_squeeze.3
  432.4 1.2 copy.104
  433.6 1.9 convert_element_type.19
  435.5 1.9 convert_element_type.20
  437.5 1.1 copy.133
  (142 shorter events, 18.2 us)
Async XLA Ops:
  0.7 3.1 copy-start
  0.7 7.0 %copy-start.31 = (f32[12,12]{1,0:T(8,128)S(1)}, f32[12,12]{1,0:T(8,128)}, u32[]{:S(2)}) copy-start(f32[12,12]{1,0:T(8,128)} %param.40) | copy-start | bytes 1732
  0.7 7.8 %copy-start.12 = (bf16[96,768]{1,0:T(8,128)(2,1)S(1)}, bf16[96,768]{1,0:T(8,128)(2,1)}, u32[]{:S(2)}) copy-start(bf16[96,768]{1,0:T(8,128)(2,1)} %param.35) | copy-start | bytes 442372
  0.7 7.9 %copy-start.25 = (bf16[24,768]{1,0:T(8,128)(2,1)S(1)}, bf16[24,768]{1,0:T(8,128)(2,1)}, u32[]{:S(2)}) copy-start(bf16[24,768]{1,0:T(8,128)(2,1)} %param.30) | copy-start | bytes 110596
  0.7 7.8 %copy-start.24 = (bf16[24,768]{1,0:T(8,128)(2,1)S(1)}, bf16[24,768]{1,0:T(8,128)(2,1)}, u32[]{:S(2)}) copy-start(bf16[24,768]{1,0:T(8,128)(2,1)} %param.29) | copy-start | bytes 110596
  0.7 7.7 %copy-start.21 = (bf16[24,768]{1,0:T(8,128)(2,1)S(1)}, bf16[24,768]{1,0:T(8,128)(2,1)}, u32[]{:S(2)}) copy-start(bf16[24,768]{1,0:T(8,128)(2,1)} %param.28) | copy-start | bytes 110596
  0.7 7.7 %copy-start.22 = (bf16[24,768]{1,0:T(8,128)(2,1)S(1)}, bf16[24,768]{1,0:T(8,128)(2,1)}, u32[]{:S(2)}) copy-start(bf16[24,768]{1,0:T(8,128)(2,1)} %param.27) | copy-start | bytes 110596
  0.7 7.7 %copy-start.23 = (bf16[24,768]{1,0:T(8,128)(2,1)S(1)}, bf16[24,768]{1,0:T(8,128)(2,1)}, u32[]{:S(2)}) copy-start(bf16[24,768]{1,0:T(8,128)(2,1)} %param.26) | copy-start | bytes 110596
  2.9 5.7 %copy-start.26 = (bf16[24,768]{1,0:T(8,128)(2,1)S(1)}, bf16[24,768]{1,0:T(8,128)(2,1)}, u32[]{:S(2)}) copy-start(bf16[24,768]{1,0:T(8,128)(2,1)} %param.31) | copy-start | bytes 110596
  3.7 4.9 %copy-start.27 = (bf16[24,768]{1,0:T(8,128)(2,1)S(1)}, bf16[24,768]{1,0:T(8,128)(2,1)}, u32[]{:S(2)}) copy-start(bf16[24,768]{1,0:T(8,128)(2,1)} %param.32) | copy-start | bytes 110596
  4.9 3.8 copy-start.28
  5.0 3.7 copy-start.11
  51.8 4.5 %copy-start.3 = (f32[12,4,256,256]{3,2,1,0:T(8,128)}, f32[12,4,256,256]{3,2,1,0:T(8,128)S(1)}, u32[]{:S(2)}) copy-start(f32[12,4,256,256]{3,2,1,0:T(8,128)S(1)} %get-tuple-element.75.bias_ref) | copy-start | bytes 37748740
  286.9 93.5 %copy-start.30 = (f32[8,768]{1,0:T(8,128)S(1)}, f32[8,768]{1,0:T(8,128)}, u32[]{:S(2)}) copy-start(f32[8,768]{1,0:T(8,128)} %get-tuple-element.109) | copy-start | bytes 73732
  286.9 93.5 %copy-start.29 = (f32[8,768]{1,0:T(8,128)S(1)}, f32[8,768]{1,0:T(8,128)}, u32[]{:S(2)}) copy-start(f32[8,768]{1,0:T(8,128)} %get-tuple-element.110) | copy-start | bytes 73732
  379.6 5.3 %copy-start.32 = (s32[1024]{0:T(1024)S(1)}, s32[1024]{0:T(1024)}, u32[]{:S(2)}) copy-start(s32[1024]{0:T(1024)} %param.25) | copy-start | bytes 12292
  386.3 43.0 %copy-start.10 = (f32[24,6144]{1,0:T(8,128)S(1)}, f32[24,6144]{1,0:T(8,128)}, u32[]{:S(2)}) copy-start(f32[24,6144]{1,0:T(8,128)} %get-tuple-element.125) | copy-start | bytes 1769476
  435.5 8.2 %copy-start.1 = (f32[32,12]{0,1:T(8,128)S(1)}, f32[32,12]{0,1:T(8,128)}, u32[]{:S(2)}) copy-start(f32[32,12]{0,1:T(8,128)} %param.41) | copy-start | bytes 4612
  437.4 2.5 copy-start.18
  437.5 3.1 copy-start.17
  437.5 3.7 copy-start.16
  437.5 4.4 copy-start.15
  437.5 5.0 %copy-start.14 = (f32[24,768]{1,0:T(8,128)S(1)}, f32[24,768]{1,0:T(8,128)}, u32[]{:S(2)}) copy-start(f32[24,768]{1,0:T(8,128)} %get-tuple-element.238) | copy-start | bytes 221188
  437.5 5.6 %copy-start.13 = (f32[24,768]{1,0:T(8,128)S(1)}, f32[24,768]{1,0:T(8,128)}, u32[]{:S(2)}) copy-start(f32[24,768]{1,0:T(8,128)} %get-tuple-element.239) | copy-start | bytes 221188
  (9 other events, 14.4 us)

commit v5 on v4

--- a/solution.py
+++ b/solution.py
@@ -64,6 +64,10 @@
     return jax.ShapeDtypeStruct(shape, dt)
 
 
+def hbm(shape, dt):
+    return pltpu.HBM(shape, dt)
+
+
 def params(mib, cid):
     if cid is None:
         return pltpu.CompilerParams(vmem_limit_bytes=mib << 20)
@@ -149,8 +153,8 @@
 
 
 class Gather:
-    def __init__(self, w, out, ssem, rsem, lsem, cols=None):
-        self.w, self.out, self.ssem, self.rsem, self.lsem, self.cols = w, out, ssem, rsem, lsem, cols
+    def __init__(self, w, out, ssem, rsem, lsem):
+        self.w, self.out, self.ssem, self.rsem, self.lsem = w, out, ssem, rsem, lsem
         self.s, self.z, self.c = place()
         self.zs, self.ss, self.co = partners(self.s, self.z, self.c)
         self.px, self.py, self.pd = plane(self.s)
@@ -160,7 +164,7 @@
         return [DMA((ND - 1,)), DMA((ND,)), DMA(())]
 
     def slot(self, i):
-        return self.out.at[i] if self.cols is None else self.out.at[i, :, self.cols]
+        return self.out.at[i]
 
     def at(self, s, kz, c):
         return flat(s, (self.z + NZ - kz) % NZ, c)
@@ -243,53 +247,70 @@
         self.local().wait()
 
 
-class PlaneGather(Gather):
-    def src(self, kz):
-        return self.w.at[(self.z + NZ - kz) % NZ]
-
-    def local(self, kz):
-        return pltpu.make_async_copy(self.src(kz), self.slot(self.at(self.s, kz, self.c)), self.lsem.at[kz])
+class PlaneGather:
+    def __init__(self, w, out, ss, rx, rd, rc, ls):
+        self.w, self.out, self.ss, self.rx, self.rd, self.rc, self.ls = w, out, ss, rx, rd, rc, ls
+        self.s, self.z, self.c = place()
+        self.co = partners(self.s, self.z, self.c)[2]
+        self.col = (self.s,) + plane(self.s)
 
     @staticmethod
     def sems():
-        return [DMA((ND - 4,)), DMA((ND,)), DMA((4,))]
+        return [DMA((9,)), DMA((2,)), DMA((2,)), DMA((4,)), DMA(())]
+
+    def at(self, a):
+        return self.out.at[self.col[a], :, self.c]
+
+    def half(self, a, j):
+        return self.out.at[self.col[a], pl.ds(2 * j, 2), self.c]
+
+    def to(self, a):
+        return {"seq": self.col[a], "dp": self.z * NCORE + self.c}
+
+    def local(self):
+        return pltpu.make_async_copy(self.w, self.at(0), self.ls)
+
+    def direct(self, a):
+        return remote(self.w, self.at(0), self.ss.at[a], self.rx.at[a - 1], self.to(a))
+
+    def core(self, a):
+        return remote(self.at(a) if a else self.w, self.at(a), self.ss.at[5 + a], self.rc.at[a], self.co)
+
+    def on(self, a):
+        return remote(self.half(a, a - 1), self.half(a, a - 1), self.ss.at[2 + a], self.rd.at[a - 1], self.to(3 - a))
 
     def start(self):
-        for kz in range(NZ):
-            i = self.at(self.s, kz, self.c)
-            self.send(i, self.there(self.px), 3 * kz, self.src(kz))
-            self.send(i, self.there(self.py), 3 * kz + 1, self.src(kz))
-            self.send(i, self.co, 3 * kz + 2, self.src(kz))
-            self.local(kz).start()
-
-    def hop(self, kz):
-        for j, (a, b) in enumerate(((self.px, self.py), (self.py, self.px))):
-            i = self.at(a, kz, self.c)
-            self.got(i)
-            if kz % 2 == j:
-                self.send(i, self.there(b), 12 + kz)
-            self.send(i, self.co, 16 + 3 * kz + j)
-
-    def diag(self, kz):
-        i = self.at(self.pd, kz, self.c)
-        self.got(i)
-        self.send(i, self.co, 18 + 3 * kz)
+        self.direct(1).start()
+        self.direct(2).start()
+        self.core(0).start()
+        self.local().start()
+
+    def hop(self):
+        for a in (1, 2):
+            self.direct(a).wait_recv()
+            self.on(a).start()
+            self.core(a).start()
+
+    def diag(self):
+        self.on(1).wait_recv()
+        self.on(2).wait_recv()
+        self.core(3).start()
 
     def end(self):
-        for kz in range(NZ):
-            for k in range(NS):
-                self.got(self.at((self.s + k) % NS, kz, 1 - self.c))
-        for n in range(ND - 4):
-            remote(self.src(0), self.slot(0), self.ssem.at[n], self.rsem.at[0], self.co).wait_send()
-        for kz in range(NZ):
-            self.local(kz).wait()
+        for a in range(4):
+            self.core(a).wait_recv()
+            self.core(a).wait_send()
+        for a in (1, 2):
+            self.direct(a).wait_send()
+            self.on(a).wait_send()
+        self.local().wait()
 
 
 class Scatter:
-    def __init__(self, g, cols, outs, mine, rc, rd, rn, rz, lsem, cs, cr, xs, dr, nr, zsem, zr):
-        self.g, self.cols, self.outs = g, cols, outs
+    def __init__(self, g, outs, mine, rc, rd, rn, rz, lsem, cs, cr, xs, ds, dr, nr, zsem, zr):
+        self.g, self.outs = g, outs
         self.mine, self.rc, self.rd, self.rn, self.rz = mine, rc, rd, rn, rz
-        self.lsem, self.cs, self.cr, self.xs, self.dr, self.nr, self.zsem, self.zr = lsem, cs, cr, xs, dr, nr, zsem, zr
+        self.lsem, self.cs, self.cr, self.xs, self.ds, self.dr, self.nr, self.zsem, self.zr = lsem, cs, cr, xs, ds, dr, nr, zsem, zr
         self.s, self.z, self.c = place()
         self.zs, self.ss, self.co = partners(self.s, self.z, self.c)
         self.col = (self.s,) + plane(self.s)
@@ -297,125 +318,114 @@
     @staticmethod
     def bufs(rows, cols):
         v = lambda *n: pltpu.VMEM(n + (rows, cols), BF)
-        return [v(16), v(16), v(4), v(2, 4), v(3), DMA((16,)), DMA((16,)), DMA((16,)), DMA((12,)), DMA((4,)), DMA((2, 4)),
+        return [v(4, NZ), v(4, NZ), v(2, 2), v(2, NZ), v(3), DMA((4,)), DMA((4,)), DMA((4,)), DMA((2,)), DMA((2,)), DMA((2,)), DMA((2,)),
                 DMA((3,)), DMA((3,))]
 
-    def part(self, m, c):
-        return self.g.at[flat(self.col[m // 4], (self.z + m % 4) % NZ, c), :, self.cols]
-
-    def core(self, m):
-        return remote(self.part(m, 1 - self.c), self.rc.at[m], self.cs.at[m], self.cr.at[m], self.co)
-
-    def load(self, m):
-        return pltpu.make_async_copy(self.part(m, self.c), self.mine.at[m], self.lsem.at[m])
-
-    def to_plane(self, m, via, dst, sem):
-        return remote(self.mine.at[m], dst, self.xs.at[m - 4], sem, {"seq": self.col[via], "dp": self.z * NCORE + self.c})
-
-    def to_via(self, kz):
-        return self.to_plane(12 + kz, 2 - kz % 2, self.rd.at[kz], self.dr.at[kz])
-
-    def to_next(self, a, kz):
-        return self.to_plane(4 * a + kz, a, self.rn.at[a - 1, kz], self.nr.at[a - 1, kz])
-
-    def zz(self, kz):
-        return remote(self.mine.at[kz], self.rz.at[kz - 1], self.zsem.at[kz - 1], self.zr.at[kz - 1], self.zs[kz - 1])
+    def core(self, a):
+        return remote(self.g.at[self.col[a], :, 1 - self.c], self.rc.at[a], self.cs.at[a], self.cr.at[a], self.co)
+
+    def load(self, a):
+        return pltpu.make_async_copy(self.g.at[self.col[a], :, self.c], self.mine.at[a], self.lsem.at[a])
+
+    def to(self, a):
+        return {"seq": self.col[a], "dp": self.z * NCORE + self.c}
+
+    def via(self, a):
+        return remote(self.mine.at[3, pl.ds(2 * (a - 1), 2)], self.rd.at[a - 1], self.ds.at[a - 1], self.dr.at[a - 1], self.to(a))
+
+    def last(self, a):
+        return remote(self.mine.at[a], self.rn.at[a - 1], self.xs.at[a - 1], self.nr.at[a - 1], self.to(a))
+
+    def zz(self, k):
+        return remote(self.mine.at[0, (self.z + k) % NZ], self.rz.at[k - 1], self.zsem.at[k - 1], self.zr.at[k - 1], self.zs[k - 1])
 
     def start(self, which):
         for a in which:
-            for kz in (1, 2, 3, 0):
-                self.core(4 * a + kz).start()
-                self.load(4 * a + kz).start()
-
-    def both(self, m):
-        self.load(m).wait()
-        self.core(m).wait_recv()
-        return self.mine[m].astype(F32) + self.rc[m].astype(F32)
-
-    def away(self, kzs):
-        for kz in kzs:
-            self.mine[12 + kz] = self.both(12 + kz).astype(BF)
-            self.to_via(kz).start()
-
-    def near(self, kzs):
-        for kz in kzs:
-            plain, joined = 2 - kz % 2, 1 + kz % 2
-            self.mine[4 * plain + kz] = self.both(4 * plain + kz).astype(BF)
-            self.to_next(plain, kz).start()
-            v = self.both(4 * joined + kz)
-            self.to_via(kz).wait_recv()
-            self.mine[4 * joined + kz] = (v + self.rd[kz].astype(F32)).astype(BF)
-            self.to_next(joined, kz).start()
-
-    def line(self, kzs):
-        for kz in kzs:
-            v = self.both(kz)
-            for a in (1, 2):
-                self.to_next(a, kz).wait_recv()
-                v = v + self.rn[a - 1, kz].astype(F32)
-            if kz:
-                self.mine[kz] = v.astype(BF)
-                self.zz(kz).start()
-            else:
-                self.put(v)
+            self.core(a).start()
+            self.load(a).start()
+
+    def both(self, a, j, ready=True):
+        if ready:
+            self.load(a).wait()
+            self.core(a).wait_recv()
+        return None if j is None else self.mine[a, j].astype(F32) + self.rc[a, j].astype(F32)
+
+    def away(self):
+        self.both(3, None)
+        for a in (1, 2):
+            for j in range(2 * (a - 1), 2 * a):
+                self.mine[3, j] = self.both(3, j, False).astype(BF)
+            self.via(a).start()
+
+    def near(self):
+        for a in (1, 2):
+            self.both(a, None)
+            self.via(3 - a).wait_recv()
+            for j in range(NZ):
+                v = self.both(a, j, False)
+                if j // 2 == 2 - a:
+                    v = v + self.rd[2 - a, j % 2].astype(F32)
+                self.mine[a, j] = v.astype(BF)
+            self.last(a).start()
+
+    def total(self, j):
+        v = self.mine[0, j].astype(F32) + self.rc[0, j].astype(F32)
+        return v + (self.rn[0, j].astype(F32) + self.rn[1, j].astype(F32))
+
+    def come(self):
+        self.both(0, None)
+        self.last(1).wait_recv()
+        self.last(2).wait_recv()
+
+    def line(self):
+        self.come()
+        for k in (1, 2, 3):
+            j = (self.z + k) % NZ
+            self.mine[0, j] = self.total(j).astype(BF)
+            self.zz(k).start()
+
+    def sent(self):
+        for a in range(4):
+            self.core(a).wait_send()
+        for a in (1, 2):
+            self.via(a).wait_send()
+            self.last(a).wait_send()
 
     def stop(self, out):
-        for kz in range(NZ):
-            v = self.both(kz)
-            for a in (1, 2):
-                self.to_next(a, kz).wait_recv()
-                v = v + self.rn[a - 1, kz].astype(F32)
-            out[kz] = v.astype(BF)
-        for m in range(16):
-            self.core(m).wait_send()
-        for kz in range(NZ):
-            self.to_via(kz).wait_send()
-            for a in (1, 2):
-                self.to_next(a, kz).wait_send()
-
-    def put(self, v):
+        self.come()
+        for j in range(NZ):
+            out[j] = self.total(j).astype(BF)
+        self.sent()
+
+    def end(self):
+        v = self.total(self.z)
+        for k in (1, 2, 3):
+            self.zz(k).wait_recv()
+            v = v + self.rz[k - 1].astype(F32)
         at = 0
         for o in self.outs:
-            w = o.shape[1]
-            o[...] = v[:, at:at + w]
-            at += w
-
-    def end(self):
-        at = 0
-        for kz in (1, 2, 3):
-            self.zz(kz).wait_recv()
-        for o in self.outs:
-            w = o.shape[1]
-            v = o[...]
-            for kz in (1, 2, 3):
-                v = v + self.rz[kz - 1, :, at:at + w].astype(F32)
-            o[...] = v
-            at += w
-        for m in range(16):
-            self.core(m).wait_send()
-        for kz in range(4):
-            self.to_via(kz).wait_send()
-            for a in (1, 2):
-                self.to_next(a, kz).wait_send()
-        for kz in (1, 2, 3):
-            self.zz(kz).wait_send()
+            o[...] = v[:, at:at + o.shape[1]]
+            at += o.shape[1]
+        self.sent()
+        for k in (1, 2, 3):
+            self.zz(k).wait_send()
 
 
 class LineScatter:
     def __init__(self, part, out, mine, rz, lsem, ss, rs):
         self.part, self.out, self.mine, self.rz, self.lsem, self.ss, self.rs = part, out, mine, rz, lsem, ss, rs
-        s, z, c = place()
-        self.zs = partners(s, z, c)[0]
+        s, self.z, c = place()
+        self.zs = partners(s, self.z, c)[0]
 
     @staticmethod
     def bufs(rows, cols):
         return [pltpu.VMEM((rows, cols), BF), pltpu.VMEM((3, rows, cols), BF), DMA(()), DMA((3,)), DMA((3,))]
 
     def copy(self, k):
-        return remote(self.part.at[k + 1], self.rz.at[k], self.ss.at[k], self.rs.at[k], self.zs[k])
+        return remote(self.part.at[(self.z + k + 1) % NZ], self.rz.at[k], self.ss.at[k], self.rs.at[k], self.zs[k])
 
     def local(self):
-        return pltpu.make_async_copy(self.part.at[0], self.mine, self.lsem)
+        return pltpu.make_async_copy(self.part.at[self.z], self.mine, self.lsem)
 
     def start(self):
         for k in range(3):
@@ -477,66 +487,108 @@
 def weights_in(w, wm, x, base, cid):
     return pl.pallas_call(
         weights_in_kernel, in_specs=[ANY, ANY, ANY, VM], out_specs=[ANY] * 4,
-        out_shape=[sds((ND,) + w.shape, w.dtype), sds((NZ,) + wm.shape, w.dtype), sds(x.shape, x.dtype), sds((H, NBK, BLK, BLK), F32)],
+        out_shape=[hbm((ND,) + w.shape, w.dtype), hbm((NZ,) + wm.shape, w.dtype), hbm(x.shape, x.dtype), hbm((H, NBK, BLK, BLK), F32)],
         scratch_shapes=Gather.sems() + LineGather.sems() + Exchange.sems() * 2 + [pltpu.VMEM((2, NBK, BLK, BLK), F32), DMA((2,))],
         compiler_params=params(24, cid), name="weights_in")(w, wm, x, base)
 
 
-def grads_out_kernel(n, *refs):
-    gs, small, gt = refs[:n], refs[n], refs[n + 1]
-    outs, osmall, go = refs[n + 2:2 * n + 2], refs[2 * n + 2], refs[2 * n + 3]
-    refs = refs[2 * n + 4:]
-    nb = len(Scatter.bufs(8, D))
-    mc, mx, mz, ms, mr, e1, e2, e3 = refs[:8]
-    sca = [Scatter(gs[j], pl.ds(0, D), [outs[j]], *refs[8 + j * nb:8 + (j + 1) * nb]) for j in range(n)]
+def hsum(sel, v):
+    return lax.dot_general(sel, v, (((1,), (1,)), ((), ())), precision=lax.Precision.HIGHEST, preferred_element_type=F32)
+
+
+def grads_out_kernel(g, dgs, dgc, dgf, gpre, gpost, diag, bucket, gt, oq, ok, ov, o_gain, o_pre, o_post, o_tab, gt_o,
+                     mc, mx, mz, ms, mr, small, e1, e2, e3, *bufs):
+    sca = Scatter(g, [oq, ok, ov], *bufs)
     s, z, c = place()
     zs, ss, co = partners(s, z, c)
-    exc = Exchange(gt, go, e1, e2, e3)
+    exc = Exchange(gt, gt_o, e1, e2, e3)
     meet_all()
+    sca.start((3, 2, 1, 0))
+    nbk = o_tab.shape[1]
+    small[...] = jnp.zeros_like(small)
+    for i, d in enumerate((dgs, dgc, dgf)):
+        v = jnp.sum(d[...], 0, keepdims=True)
+        for j in range(D // 128):
+            small[6 * i + j:6 * i + j + 1, :] = v[:, j * 128:(j + 1) * 128]
+    sel = (lax.broadcasted_iota(jnp.int32, (H, D), 1) // DH == lax.broadcasted_iota(jnp.int32, (H, D), 0)).astype(F32)
+    small[24:24 + H, :H] = hsum(sel, gpre[...])
+    small[24:24 + H, 16:16 + H] = hsum(gpost[...], sel)
+    tab = jnp.zeros((H, nbk), F32)
+    for d in range(NBK):
+        hot = (lax.broadcasted_iota(jnp.int32, (nbk, 2 * BLK), 0) == bucket[d:d + 1, :]).astype(F32)
+        tab = tab + hsum(diag[:, d, 0, :], hot)
+    small[24:24 + H, 32:32 + nbk] = tab
     first = remote(small, mc, ms.at[0], mr.at[0], co)
     first.start()
-    for a in sca:
-        a.start((3,))
-    for a in sca:
-        a.start((2, 1, 0))
+    sca.away()
     first.wait_recv()
     mx[s] = small[...] + mc[...]
     xy = [remote(mx.at[s], mx.at[s], ms.at[k], mr.at[k], ss[k - 1]) for k in (1, 2, 3)]
     for cp in xy:
         cp.start()
-    every = (1, 2, 3, 0)
-    for a in sca:
-        a.away(every)
+    sca.near()
+    exc.start()
     for cp in xy:
         cp.wait_recv()
     mz[z] = (mx[0] + mx[1]) + (mx[2] + mx[3])
     zz = [remote(mz.at[z], mz.at[z], ms.at[3 + k], mr.at[3 + k], zs[k - 1]) for k in (1, 2, 3)]
     for cp in zz:
         cp.start()
-    for a in sca:
-        a.near(every)
-    exc.start()
-    for a in sca:
-        a.line(every)
+    sca.line()
     for cp in zz:
         cp.wait_recv()
-    osmall[...] = (mz[0] + mz[1]) + (mz[2] + mz[3])
-    for a in sca:
-        a.end()
+    v = (mz[0] + mz[1]) + (mz[2] + mz[3])
+    o_pre[...] = v[24:24 + H, :H]
+    o_post[...] = v[24:24 + H, 16:16 + H]
+    o_tab[...] = v[24:24 + H, 32:32 + nbk]
+    o_gain[...] = v[:24]
     exc.end()
+    sca.end()
     for cp in [first] + xy + zz:
         cp.wait_send()
 
 
-def grads_out(gs, small, gt, cid):
-    sm = pltpu.VMEM(small.shape, F32)
-    sm4 = pltpu.VMEM((4,) + small.shape, F32)
+def grads_out(g, small, gt, nbk, cid):
+    sm = (40, 128)
+    rows = g.shape[3]
     return pl.pallas_call(
-        functools.partial(grads_out_kernel, len(gs)),
-        in_specs=[ANY] * len(gs) + [VM, ANY], out_specs=[VM] * (len(gs) + 1) + [ANY],
-        out_shape=[sds(g.shape[1:], F32) for g in gs] + [sds(small.shape, F32), sds(gt.shape, BF)],
-        scratch_shapes=[sm, sm4, sm4, DMA((7,)), DMA((7,))] + Exchange.sems() + sum([Scatter.bufs(*g.shape[1:]) for g in gs], []),
-        compiler_params=params(56, cid), name="grads_out")(*gs, small, gt)
+        grads_out_kernel,
+        in_specs=[ANY] + [VM] * len(small) + [ANY], out_specs=[VM] * 7 + [ANY],
+        out_shape=[sds((rows, D), F32)] * 3
+        + [sds((24, 128), F32), sds((H, H), F32), sds((H, H), F32), sds((H, nbk), F32), sds(gt.shape, BF)],
+        scratch_shapes=[pltpu.VMEM(sm, F32), pltpu.VMEM((4,) + sm, F32), pltpu.VMEM((4,) + sm, F32), DMA((7,)), DMA((7,)),
+                        pltpu.VMEM(sm, F32)] + Exchange.sems() + Scatter.bufs(*g.shape[3:]),
+        compiler_params=params(56, cid), name="grads_out")(g, *small, gt)
+
+
+def finish_kernel(n, *refs):
+    acts, plain, rf = refs[:3], refs[3:3 + n], refs[3 + n]
+    o_acts, o_plain, o_fo, o_fi = refs[4 + n:7 + n], refs[7 + n:7 + 2 * n], refs[7 + 2 * n], refs[8 + 2 * n]
+    for a, b in zip(acts, o_acts):
+        b[...] = a[...].astype(b.dtype)
+
+    @pl.when(pl.program_id(0) == 0)
+    def _():
+        for a, b in zip(plain, o_plain):
+            b[...] = a[...]
+        nf = o_fi.shape[0]
+        for j in range(nf):
+            o_fi[j] = rf[:, 2 * j * D:(2 * j + 1) * D]
+            o_fo[:, j, :] = rf[:, (2 * j + 1) * D:(2 * j + 2) * D]
+
+
+def finish(acts, plain, rf):
+    rows = rf.shape[0]
+    nf = rf.shape[1] // (2 * D)
+    blk = pl.BlockSpec((1,) + acts[0].shape[1:], lambda i: (i, 0, 0))
+    whole = [pl.BlockSpec(p.shape, lambda i: (0, 0)) for p in plain]
+    return pl.pallas_call(
+        functools.partial(finish_kernel, len(plain)), grid=(acts[0].shape[0],),
+        in_specs=[blk] * 3 + whole + [pl.BlockSpec(rf.shape, lambda i: (0, 0))],
+        out_specs=[blk] * 3 + whole + [pl.BlockSpec((rows, nf, D), lambda i: (0, 0, 0)), pl.BlockSpec((nf, rows, D), lambda i: (0, 0, 0))],
+        out_shape=[sds(a.shape, t) for a, t in zip(acts, (BF, F32, F32))] + [sds(p.shape, F32) for p in plain]
+        + [sds((rows, nf, D), F32), sds((nf, rows, D), F32)],
+        name="finish")(*acts, *plain, rf)
 
 
 EPS = 1e-6
@@ -549,6 +601,14 @@
 
 def col(shape, j):
     return pl.BlockSpec(shape, lambda *a: (0, j), pipeline_mode=pl.Buffered(1))
+
+
+def each(f):
+    def step(i, carry):
+        f(pl.ds(pl.multiple_of(i * BLK, BLK), BLK))
+        return carry
+
+    lax.fori_loop(0, NBK, step, 0)
 
 
 def rows8(v):
@@ -579,20 +639,19 @@
     return [slice(i * BLK, (i + 1) * BLK) for i in range(n)]
 
 
-HOPS = [("hop", k) for k in range(NZ)]
-FWD_PLAN = ((2, [("exc", 0)]), (5, HOPS + [("exc", 1)]))
-CROSS_PLAN = ((4, HOPS),)
-
-
-def self_fwd_kernel(near, st_ref, x_ref, w_ref, gn_ref, bias_ref, mpre_ref, mpost_ref, *refs):
-    if near:
-        (zm_h, wf_h, enc_h, cot_h, q_ref, k_ref, v_ref, att_ref, gain_ref, p_ref, wo_h, zf_h, eo_h, co_h, acc_ref, lo_ref,
-         ags, lgs, ex1, ex2) = split(refs, 16, 3, 3, 3, 3)
+FWD_PLAN = ((2, "exc", 0), (5, "hop", 0), (5, "exc", 1), (9, "diag", 0))
+CROSS_PLAN = ((4, "hop"),)
+
+
+def self_fwd_kernel(near, st_ref, x_ref, w_ref, gn_ref, bias_ref, pre_ref, post_ref, *refs):
+    if near:
+        (zm_h, wf_h, enc_h, cot_h, q_ref, k_ref, v_ref, att_ref, gain_ref, mpre_ref, mpost_ref, p_ref, wo_h, zf_h, eo_h, co_h, acc_ref, lo_ref,
+         ags, lgs, ex1, ex2) = split(refs, 18, 5, 3, 3, 3)
         gat = PlaneGather(zm_h, wo_h, *ags)
         lin = LineGather(wf_h, zf_h, *lgs)
         exc = [Exchange(enc_h, eo_h, *ex1), Exchange(cot_h, co_h, *ex2)]
     else:
-        q_ref, k_ref, v_ref, att_ref, gain_ref, p_ref, acc_ref, lo_ref = refs
+        q_ref, k_ref, v_ref, att_ref, gain_ref, mpre_ref, mpost_ref, p_ref, acc_ref, lo_ref = refs
     h = pl.program_id(0)
 
     if near:
@@ -602,14 +661,13 @@
             gat.start()
             lin.start()
 
-        for hh, todo in FWD_PLAN:
+        for hh, name, k in FWD_PLAN:
             @pl.when(h == hh)
-            def _(todo=todo):
-                for name, k in todo:
-                    if name == "exc":
-                        exc[k].start()
-                    else:
-                        getattr(gat, name)(k)
+            def _(name=name, k=k):
+                if name == "exc":
+                    exc[k].start()
+                else:
+                    getattr(gat, name)()
 
     @pl.when(h == 0)
     def _():
@@ -617,16 +675,25 @@
         gt = gn_ref[...].astype(F32).T
         gain_ref[...] = gt[:8]
         g = gt[:1]
-        for r in blocks():
+
+        def project(r):
             n1 = norm(x_ref[r, :].astype(F32), g).astype(BF)
             for j, o in enumerate((q_ref, k_ref, v_ref)):
                 o[r, :] = dot(n1, w_ref[:, j * D:(j + 1) * D], 1, 0).astype(BF)
+
+        each(project)
         pos = lax.broadcasted_iota(jnp.int32, (L, 128), 0)
         lo = jnp.zeros((L, 128), jnp.int32)
-        for d in range(1, st_ref.shape[0]):
-            sd = st_ref[d]
+        me = lax.axis_index("seq")
+        for d in range(1, st_ref.shape[1]):
+            sd = st_ref[me, d]
             lo = jnp.where(pos >= sd, sd, lo)
         lo_ref[...] = lo
+        sel = (lax.broadcasted_iota(jnp.int32, (H, D), 1) // DH == lax.broadcasted_iota(jnp.int32, (H, D), 0)).astype(F32)
+        wide = lambda m, k: lax.dot_general(m[...], sel, (((k,), (0,)), ((), ())), precision=lax.Precision.HIGHEST,
+                                            preferred_element_type=F32)
+        mpre_ref[...] = wide(pre_ref, 0)
+        mpost_ref[...] = wide(post_ref, 1)
 
     mp = mpre_ref[pl.ds(h, 1), :]
     mo = mpost_ref[pl.ds(h, 1), :]
@@ -655,8 +722,6 @@
         att_ref[...] = acc_ref[...].astype(BF)
         if near:
             lin.end()
-            for k in range(NZ):
-                gat.diag(k)
             gat.end()
             for e in exc:
                 e.end()
@@ -667,18 +732,18 @@
     near = far is not None
     extra_out = []
     if near:
-        extra_out = [sds((ND,) + far[0].shape[1:], BF), sds((NZ,) + far[1].shape, BF)] + [sds(f.shape, BF) for f in far[2:]]
+        extra_out = [sds((NS, NZ, NCORE) + far[0].shape[1:], BF), sds((NZ,) + far[1].shape, BF)] + [sds(f.shape, BF) for f in far[2:]]
     return pl.pallas_call(
         functools.partial(self_fwd_kernel, near),
         grid_spec=pltpu.PrefetchScalarGridSpec(
             num_scalar_prefetch=1, grid=(H,),
             in_specs=[one, col((D, 3 * D), 0), col((D, 128), 18),
-                      pl.BlockSpec((1, NBK, BLK, BLK), lambda h, st: (h, 0, 0, 0)), cst((H, D)), cst((H, D))]
+                      pl.BlockSpec((1, NBK, BLK, BLK), lambda h, st: (h, 0, 0, 0)), cst((H, H)), cst((H, H))]
             + [ANY] * (4 * near),
-            out_specs=[one] * 4 + [cst((8, D)), pl.BlockSpec((1, L, L), lambda h, st: (h, 0, 0))] + [ANY] * (4 * near),
+            out_specs=[one] * 4 + [cst((8, D)), cst((H, D)), cst((H, D)), pl.BlockSpec((1, L, L), lambda h, st: (h, 0, 0))] + [ANY] * (4 * near),
             scratch_shapes=[pltpu.VMEM((L, D), F32), pltpu.VMEM((L, 128), jnp.int32)]
             + (PlaneGather.sems() + LineGather.sems() + Exchange.sems() * 2 if near else [])),
-        out_shape=[sds((L, D), BF)] * 4 + [sds((8, D), F32), sds((H, L, L), BF)] + extra_out,
+        out_shape=[sds((L, D), BF)] * 4 + [sds((8, D), F32), sds((H, D), F32), sds((H, D), F32), sds((H, L, L), BF)] + extra_out,
         compiler_params=params(62, cid),
         cost_estimate=pl.CostEstimate(flops=52_000_000_000, bytes_accessed=45_000_000, transcendentals=8_000_000),
         name="self_fwd")(starts, x, w1, w1, bias, mpre, mpost, *(far or ()))
@@ -686,7 +751,7 @@
 
 def cross_fwd_kernel(near, x_ref, att_ref, wo_ref, wq_ref, wk_ref, wv_ref, enc_ref, gain_ref, *refs):
     if near:
-        zf_h, h1_ref, n2_ref, q_ref, k_ref, v_ref, catt_ref, p_ref, fo_h, ags = split(refs, 9, 3)
+        zf_h, h1_ref, n2_ref, q_ref, k_ref, v_ref, catt_ref, p_ref, fo_h, ags = split(refs, 9, 5)
         gat = PlaneGather(zf_h, fo_h, *ags)
     else:
         h1_ref, n2_ref, q_ref, k_ref, v_ref, catt_ref, p_ref = refs
@@ -698,16 +763,16 @@
             meet_all()
             gat.start()
 
-        for hh, todo in CROSS_PLAN:
+        for hh, name in CROSS_PLAN:
             @pl.when(h == hh)
-            def _(todo=todo):
-                for name, k in todo:
-                    getattr(gat, name)(k)
+            def _(name=name):
+                getattr(gat, name)()
 
     @pl.when(h == 0)
     def _():
         g = gain_ref[1:2, :]
-        for r in blocks():
+
+        def project(r):
             h1 = x_ref[r, :].astype(F32) + dot(att_ref[r, :], wo_ref[...], 1, 0)
             h1_ref[r, :] = h1
             n2 = norm(h1, g).astype(BF)
@@ -715,6 +780,8 @@
             q_ref[r, :] = dot(n2, wq_ref[...], 1, 0).astype(BF)
             k_ref[r, :] = dot(enc_ref[r, :], wk_ref[...], 1, 0).astype(BF)
             v_ref[r, :] = dot(enc_ref[r, :], wv_ref[...], 1, 0).astype(BF)
+
+        each(project)
 
     cols = pl.ds(pl.multiple_of(h * 128, 128), 128)
     first = lax.broadcasted_iota(jnp.int32, (1, 128), 1) < DH
@@ -743,8 +810,7 @@
     if near:
         @pl.when(h == H // 2 - 1)
         def _():
-            for k in range(NZ):
-                gat.diag(k)
+            gat.diag()
             gat.end()
 
 
@@ -756,7 +822,7 @@
         in_specs=[one, one] + [col((D, D), j) for j in range(4)] + [one, cst((8, D))] + [ANY] * near,
         out_specs=[one] * 6 + [pl.BlockSpec((2, L, L), lambda h: (h, 0, 0))] + [ANY] * near,
         out_shape=[sds((L, D), F32)] + [sds((L, D), BF)] * 5 + [sds((H, L, L), BF)]
-        + ([sds((ND,) + far.shape[1:], BF)] if near else []),
+        + ([sds((NS, NZ, NCORE) + far.shape[1:], BF)] if near else []),
         scratch_shapes=PlaneGather.sems() if near else [],
         compiler_params=params(62, cid),
         cost_estimate=pl.CostEstimate(flops=31_000_000_000, bytes_accessed=50_000_000, transcendentals=12_000_000),
@@ -771,11 +837,14 @@
 
     @pl.when(a == 0)
     def _():
-        for r in blocks():
+
+        def enter(r):
             h2 = h1_ref[r, :] + dot(catt_ref[r, :], wco_ref[...], 1, 0)
             bh2_ref[r, :] = h2
             acc[r, :] = h2
             n3[r, :] = norm(h2, g).astype(BF)
+
+        each(enter)
         n3t[...] = n3[...].T
         cott[...] = cot_ref[...].T
         dn[...] = jnp.zeros_like(dn)
@@ -795,15 +864,17 @@
 
     @pl.when(a == pl.num_programs(0) - 1)
     def _():
-        dg = jnp.zeros((8, D), F32)
-        for r in blocks():
+        dg_ref[...] = jnp.zeros_like(dg_ref)
+
+        def leave(r):
             out_ref[r, :] = acc[r, :].astype(BF)
             dx, s = norm_grad(bh2_ref[r, :], g, dn[r, :])
-            dg = dg + s
+            dg_ref[...] += s
             b2 = cot_ref[r, :].astype(F32) + dx
             bh2_ref[r, :] = b2
             bca_ref[r, :] = dot(b2.astype(BF), wco_ref[...], 1, 1).astype(BF)
-        dg_ref[...] = dg
+
+        each(leave)
 
 
 def feed(h1, catt, wmid, cot, gains, wfeed):
@@ -827,7 +898,7 @@
         gf_h = refs[0]
         gw_ref, genc_ref, bh1_ref, bat_ref, dg_ref, rf_ref = refs[1:7]
         qt, dot_, ds, dq, dk, dv, n2, enc, att, catt, h1, w, sems, sca = split(refs[7:], 13, len(Scatter.bufs(8, D)))
-        sca = Scatter(gf_h, pl.ds(0, gf_h.shape[2]), [], *sca)
+        sca = Scatter(gf_h, [], *sca)
     else:
         gw_ref, genc_ref, bh1_ref, bat_ref, dg_ref = refs[:5]
         qt, dot_, ds, dq, dk, dv, n2, enc, att, catt, h1, w, sems = refs[5:]
@@ -848,10 +919,10 @@
             c.start()
 
     if near:
-        for hh, name, kzs in BWD_PLAN:
+        for hh, name, *more in BWD_PLAN:
             @pl.when(h == hh)
-            def _(name=name, kzs=kzs):
-                getattr(sca, name)(kzs)
+            def _(name=name, more=more):
+                getattr(sca, name)(*more)
 
     e = h % 2
     cols = pl.ds(pl.multiple_of((h // 2) * 128, 128), 128)
@@ -881,14 +952,15 @@
         for c in copies:
             c.wait()
         g = gain_ref[1:2, :]
-        dg = jnp.zeros((8, D), F32)
+        dg_ref[...] = jnp.zeros_like(dg_ref)
         gw_ref[:, D:2 * D] = dot(n2[...], dq[...], 0, 0).astype(BF)
         gw_ref[:, 2 * D:3 * D] = dot(enc[...], dk[...], 0, 0).astype(BF)
         gw_ref[:, 3 * D:4 * D] = dot(enc[...], dv[...], 0, 0).astype(BF)
-        for r in blocks():
+
+        def leave(r):
             genc_ref[r, :] = (dot(dk[r, :], w[:, 2 * D:3 * D], 1, 1) + dot(dv[r, :], w[:, 3 * D:], 1, 1)).astype(genc_ref.dtype)
             dx, s = norm_grad(h1[r, :], g, dot(dq[r, :], w[:, D:2 * D], 1, 1))
-            dg = dg + s
+            dg_ref[...] += s
             b2 = bh1_ref[r, :]
             b1 = b2 + dx
             bh1_ref[r, :] = b1
@@ -896,15 +968,15 @@
             n2[r, :] = b1
             enc[r, :] = b2.astype(BF)
             bat_ref[r, :] = dot(b1, w[:, :D], 1, 1).astype(BF)
+
+        each(leave)
         gw_ref[:, :D] = dot(att[...], n2[...], 0, 0).astype(BF)
         gw_ref[:, 4 * D:] = dot(catt[...], enc[...], 0, 0).astype(BF)
-        dg_ref[...] = dg
         if near:
             sca.stop(rf_ref)
 
 
-EVERY = (1, 2, 3, 0)
-BWD_PLAN = ((1, "away", EVERY), (1, "start", (2, 1)), (3, "start", (0,)), (6, "near", EVERY))
+BWD_PLAN = ((1, "away"), (1, "start", (2, 1)), (3, "start", (0,)), (6, "near"))
 
 
 def cross_bwd(q, k, v, do, p, gains, n2, enc, att, catt, h1, bh2, wmid, far=None, cid=None):
@@ -912,7 +984,7 @@
     near = far is not None
     pair = pl.BlockSpec((L, 128), lambda h: (0, h // 2))
     act = pltpu.VMEM((L, D), BF)
-    more = [(NZ,) + far.shape[1:]] if near else []
+    more = [(NZ,) + far.shape[3:]] if near else []
     return pl.pallas_call(
         functools.partial(cross_bwd_kernel, near), grid=(H,),
         in_specs=[pair] * 4 + [pl.BlockSpec((1, L, L), lambda h: (h, 0, 0)), cst((8, D))] + [ANY] * (7 + near),
@@ -926,21 +998,21 @@
         name="cross_bwd")(q, k, v, do, p, gains, n2, enc, att, catt, h1, bh2, wmid, *([far] if near else []))
 
 
-SELF_PLAN = ((1, "away", EVERY), (1, "start", (2, 1, 0)), (3, "near", EVERY), (3, "exc", 0), (6, "exc", 1), (8, "line", EVERY))
+SELF_PLAN = ((1, "away"), (1, "start", (2, 1, 0)), (3, "near"), (3, "exc", 0), (6, "exc", 1), (8, "line"))
 
 
 def self_bwd_kernel(near, q_ref, k_ref, v_ref, ba_ref, p_ref, mpre_ref, mpost_ref, gain_ref, x_h, bh1_h, w_h, *refs):
     if near:
         gm_h, zf_h, out_h, ge_h = refs[:4]
-        gq_ref, gk_ref, gv_ref, gtok_ref, gpre_ref, gpost_ref, diag_ref, dg_ref = refs[4:12]
-        rms, (rf_ref, oo_h, go_h) = refs[12:17], refs[17:20]
-        qt, bat, dqa, dkt, dvt, dm, x, bh1, w, sems, sca, lin, ex1, ex2 = split(refs[20:], 10, len(Scatter.bufs(8, D)), 5, 3, 3)
+        gw_ref, gtok_ref, gpre_ref, gpost_ref, diag_ref, dg_ref = refs[4:10]
+        rms, (rf_ref, oo_h, go_h) = refs[10:15], refs[15:18]
+        qt, bat, dqa, dkt, dvt, dm, x, bh1, w, sems, sca, lin, ex1, ex2 = split(refs[18:], 10, len(Scatter.bufs(8, D)), 5, 3, 3)
         lin = LineScatter(zf_h, rf_ref, *lin)
-        sca = Scatter(gm_h, pl.ds(0, gm_h.shape[2]), rms, *sca)
+        sca = Scatter(gm_h, rms, *sca)
         exc = [Exchange(out_h, oo_h, *ex1), Exchange(ge_h, go_h, *ex2)]
     else:
-        gq_ref, gk_ref, gv_ref, gtok_ref, gpre_ref, gpost_ref, diag_ref, dg_ref = refs[:8]
-        qt, bat, dqa, dkt, dvt, dm, x, bh1, w, sems = refs[8:]
+        gw_ref, gtok_ref, gpre_ref, gpost_ref, diag_ref, dg_ref = refs[:6]
+        qt, bat, dqa, dkt, dvt, dm, x, bh1, w, sems = refs[6:]
     h = pl.program_id(0)
 
     if near:
@@ -950,13 +1022,13 @@
             sca.start((3,))
             lin.start()
 
-        for hh, name, kzs in SELF_PLAN:
+        for hh, name, *more in SELF_PLAN:
             @pl.when(h == hh)
-            def _(name=name, kzs=kzs):
+            def _(name=name, more=more):
                 if name == "exc":
-                    exc[kzs].start()
+                    exc[more[0]].start()
                 else:
-                    getattr(sca, name)(kzs)
+                    getattr(sca, name)(*more)
 
     late = [(x_h, x), (bh1_h, bh1), (w_h.at[:, pl.ds(0, 3 * D)], w)]
     copies = [pltpu.make_async_copy(a, b, sems.at[i]) for i, (a, b) in enumerate(late)]
@@ -1014,8 +1086,9 @@
         for c in copies:
             c.wait()
         g = gain_ref[:1, :]
-        dg = jnp.zeros((8, D), F32)
-        for r in blocks():
+        dg_ref[...] = jnp.zeros_like(dg_ref)
+
+        def leave(r):
             xr = x[r, :].astype(F32)
             n1 = norm(xr, g).astype(BF)
             dk = dkt[:, r].T.astype(BF)
@@ -1026,12 +1099,13 @@
             dqa[r, :] = dk.astype(F32)
             back = dot(dq, w[:, :D], 1, 1) + dot(dk, w[:, D:2 * D], 1, 1) + dot(dv, w[:, 2 * D:], 1, 1)
             dx, s = norm_grad(xr, g, back)
-            dg = dg + s
+            dg_ref[...] += s
             gtok_ref[r, :] = (bh1[r, :] + dx).astype(gtok_ref.dtype)
-        gq_ref[...] = dot(bat[...], dm[:, :D], 1, 0).astype(BF)
-        gk_ref[...] = dot(bat[...], dqa[...].astype(BF), 1, 0).astype(BF)
-        gv_ref[...] = dot(bat[...], dvt[...].astype(BF), 1, 1).astype(BF)
-        dg_ref[...] = dg
+
+        each(leave)
+        gw_ref[:, :D] = dot(bat[...], dm[:, :D], 1, 0).astype(BF)
+        gw_ref[:, D:2 * D] = dot(bat[...], dqa[...].astype(BF), 1, 0).astype(BF)
+        gw_ref[:, 2 * D:] = dot(bat[...], dvt[...].astype(BF), 1, 1).astype(BF)
         if near:
             lin.end()
             sca.end()
@@ -1042,7 +1116,7 @@
 def self_bwd(q, k, v, ba, p, mpre, mpost, gains, x, bh1, w1, far=None, cid=None):
     one = cst((L, D))
     near = far is not None
-    rows = far[0].shape[1] if near else 0
+    rows = far[0].shape[3] if near else 0
     more = [cst((rows, D))] * 5 + [cst(far[1].shape[1:]), ANY, ANY] if near else []
     more_out = []
     if near:
@@ -1050,13 +1124,13 @@
     return pl.pallas_call(
         functools.partial(self_bwd_kernel, near), grid=(H,),
         in_specs=[one] * 4 + [pl.BlockSpec((1, L, L), lambda h: (h, 0, 0)), cst((H, D)), cst((H, D)), cst((8, D))] + [ANY] * (3 + 4 * near),
-        out_specs=[cst((D, D))] * 3 + [one, cst((H, D)), cst((H, D)),
+        out_specs=[cst((D, 3 * D))] + [one, cst((H, D)), cst((H, D)),
                    pl.BlockSpec((1, NBK, 1, 2 * BLK), lambda h: (h, 0, 0, 0)), cst((8, D))] + more,
-        out_shape=[sds((D, D), BF)] * 3 + [sds((L, D), BF), sds((H, D), F32), sds((H, D), F32),
+        out_shape=[sds((D, 3 * D), BF)] + [sds((L, D), BF), sds((H, D), F32), sds((H, D), F32),
                    sds((H, NBK, 1, 2 * BLK), F32), sds((8, D), F32)] + more_out,
         scratch_shapes=[pltpu.VMEM((D, L), BF)] * 2 + [pltpu.VMEM((L, D), F32)] + [pltpu.VMEM((D, L), F32)] * 2
         + [pltpu.VMEM((L, L), BF), pltpu.VMEM((L, D), BF), pltpu.VMEM((L, D), F32), pltpu.VMEM((D, 3 * D), BF), DMA((3,))]
-        + (Scatter.bufs(*far[0].shape[1:]) + LineScatter.bufs(*far[1].shape[1:]) + Exchange.sems() * 2 if near else []),
+        + (Scatter.bufs(*far[0].shape[3:]) + LineScatter.bufs(*far[1].shape[1:]) + Exchange.sems() * 2 if near else []),
         compiler_params=params(62, cid),
         cost_estimate=pl.CostEstimate(flops=128_000_000_000, bytes_accessed=50_000_000, transcendentals=0),
         name="self_bwd")(q, k, v, ba, p, mpre, mpost, gains, x, bh1, w1, *(far or ()))
@@ -1102,65 +1176,65 @@
         wfeed = gather(wfeed)
         enc = to_stream(encoded)
         cot = to_stream(cotangent)
-    starts = lax.dynamic_index_in_dim(doc_starts, lax.axis_index("seq"), 0, keepdims=False)
-    mpre = jnp.repeat(mix_pre.T, DH, axis=1)
-    mpost = jnp.repeat(mix_post, DH, axis=1)
-    if near:
-        q, k, v, att, gain, p, wmid, zfeed, enc, cot = self_fwd(starts, x, w1, bias, mpre, mpost, (zmid, wfeed, encoded, cotangent), 2)
+    if near:
+        q, k, v, att, gain, mpre, mpost, p, wmid, zfeed, enc, cot = self_fwd(doc_starts, x, w1, bias, mix_pre, mix_post, (zmid, wfeed, encoded, cotangent), 2)
         wmid = wmid.reshape(D, -1)
         enc = enc.reshape(L, D)
         h1, n2, cqx, ckx, cvx, catt, cp, wfeed = cross_fwd(x, att, wmid, enc, gain, zfeed, 3)
         cot = cot.reshape(L, D)
         wfeed = wfeed.reshape(D, -1)
     else:
-        q, k, v, att, gain, p = self_fwd(starts, x, w1, bias, mpre, mpost)
+        q, k, v, att, gain, mpre, mpost, p = self_fwd(doc_starts, x, w1, bias, mix_pre, mix_post)
         h1, n2, cqx, ckx, cvx, catt, cp = cross_fwd(x, att, wmid, enc, gain)
     out, bh2, bca, gw_feed, dgf = feed(h1, catt, wmid, cot, gain, wfeed)
+    by_dev = lambda a: a.reshape(NS, NZ, NCORE, rows, -1)
     back = (cqx, ckx, cvx, bca, cp, gain, n2, enc, att, catt, h1, bh2, wmid)
     if near:
-        gw_mid, g_enc, bh1, bat, dgc, zfeed = cross_bwd(*back, gw_feed.reshape(ndev, rows, -1), 6)
+        gw_mid, g_enc, bh1, bat, dgc, zfeed = cross_bwd(*back, by_dev(gw_feed), 6)
     else:
         gw_mid, g_enc, bh1, bat, dgc = cross_bwd(*back)
         r_feed = scatter(gw_feed)
     blk = lambda a: a.reshape(nseq, L // nseq, D)
     if near:
-        far = (gw_mid.reshape(ndev, rows, -1), zfeed, blk(out), blk(g_enc))
-        gw_q, gw_k, gw_v, g_tok, gpre, gpost, diag, dgs, *r_mid, r_feed, out, g_enc = self_bwd(
+        far = (by_dev(gw_mid), zfeed, blk(out), blk(g_enc))
+        gw_qkv, g_tok, gpre, gpost, diag, dgs, *r_mid, r_feed, out, g_enc = self_bwd(
             q, k, v, bat, p, mpre, mpost, gain, x, bh1, w1, far, 4)
     else:
-        gw_q, gw_k, gw_v, g_tok, gpre, gpost, diag, dgs = self_bwd(q, k, v, bat, p, mpre, mpost, gain, x, bh1, w1)
-    gpre = gpre.reshape(H, H, DH).sum(-1).T
-    gpost = gpost.reshape(H, H, DH).sum(-1)
-    dg = diag[:, :, 0, ::-1]
-    gt = 0.0
-    for d in range(NBK):
-        gt = gt + jnp.pad(dg[:, d], ((0, 0), (d * BLK + 1, L - d * BLK - 1)))
-    gt = gt[:, BLK:BLK + L]
-    gtab = lax.dot_general(hot, gt, (((0,), (1,)), ((), ())), precision=lax.Precision.HIGHEST)
-    dgain = jnp.stack([dgs.sum(0), dgc.sum(0), dgf.sum(0)])
-    if near:
-        parts = [dgain, gpre, gpost, gtab]
-        vec = jnp.concatenate([a.reshape(-1) for a in parts])
-        vec = jnp.pad(vec, (0, 3072 - vec.shape[0])).reshape(24, 128)
-        r_q, r_k, r_v, vec, g_tok = grads_out([a.reshape(ndev, rows, -1) for a in (gw_q, gw_k, gw_v)], vec, blk(g_tok), 5)
-        vec = vec.reshape(-1)
-        o = 0
-        got = []
-        for a in parts:
-            got.append(vec[o:o + a.size].reshape(a.shape))
-            o += a.size
-        dgain, gpre, gpost, gtab = got
+        gw_qkv, g_tok, gpre, gpost, diag, dgs = self_bwd(q, k, v, bat, p, mpre, mpost, gain, x, bh1, w1)
+    if near:
+        pad = jnp.pad(rel_bucket[::-1], (BLK, BLK), constant_values=-1)
+        bucket = jnp.stack([lax.slice(pad, (L + BLK - 1 - (d * BLK + BLK),), (L + BLK - 1 - (d * BLK + BLK) + 2 * BLK,))
+                            for d in range(NBK)])
+        r_q, r_k, r_v, dgain, gpre, gpost, gtab, g_tok = grads_out(
+            by_dev(gw_qkv), [dgs, dgc, dgf, gpre, gpost, diag, bucket], blk(g_tok), buckets, 5)
+        out, g_tok, g_enc, *plain, g_fo, g_fi = finish([out, g_tok, g_enc], [r_q, r_k, r_v, *r_mid, dgain, gpre, gpost, gtab], r_feed)
+        r_q, r_k, r_v = plain[:3]
+        r_mid, (dgain, gpre, gpost, gtab) = plain[3:8], plain[8:]
+        gtab = gtab.T
+        dgain = dgain[:18].reshape(3, D)
     else:
+        gpre = gpre.reshape(H, H, DH).sum(-1).T
+        gpost = gpost.reshape(H, H, DH).sum(-1)
+        dg = diag[:, :, 0, ::-1]
+        gt = 0.0
+        for d in range(NBK):
+            gt = gt + jnp.pad(dg[:, d], ((0, 0), (d * BLK + 1, L - d * BLK - 1)))
+        gt = gt[:, BLK:BLK + L]
+        gtab = lax.dot_general(hot, gt, (((0,), (1,)), ((), ())), precision=lax.Precision.HIGHEST)
+        dgain = jnp.stack([dgs.sum(0), dgc.sum(0), dgf.sum(0)])
         r_mid = jnp.split(scatter(gw_mid), 5, 1)
-        r_q, r_k, r_v = scatter(gw_q), scatter(gw_k), scatter(gw_v)
-        out, g_tok, g_enc = from_stream(out), from_stream(g_tok), from_stream(g_enc)
+        r_q, r_k, r_v = jnp.split(scatter(gw_qkv), 3, 1)
+        out, g_tok, g_enc = from_stream(out), from_stream(g_tok).astype(F32), from_stream(g_enc).astype(F32)
         dgain, gpre, gpost, gtab = lax.psum((dgain, gpre, gpost, gtab), AX)
-    r_feed = r_feed.reshape(rows, nf, 2, D)
+        r_feed = r_feed.reshape(rows, nf, 2, D)
+        g_fi, g_fo = r_feed[:, :, 0].transpose(1, 0, 2), r_feed[:, :, 1].reshape(rows * nf, D)
+    g_fi = g_fi.transpose(1, 2, 0).reshape(rows, nf * D)
+    g_fo = g_fo.reshape(rows * nf, D)
     me = lax.axis_index("seq") * ndp + lax.axis_index("dp")
     dgain = lax.dynamic_slice_in_dim(dgain, me * rows, rows, 1)
-    return (out, g_tok.astype(F32), g_enc.astype(F32),
+    return (out, g_tok, g_enc,
             r_q, r_k, r_v, *r_mid,
-            r_feed[:, :, 0].transpose(0, 2, 1).reshape(rows, nf * D), r_feed[:, :, 1].reshape(rows * nf, D),
+            g_fi, g_fo,
             dgain[0], dgain[1], dgain[2], gpre, gpost, gtab)
 
 

time: 453 us -> 439 us (0.969)
  local copies, waits for them, and re-layouts: 34.9 us -> 9.28 us
  Pallas kernels: 400 us -> 418 us
  other arithmetic: 5.79 us -> 0.86 us
    unnamed x92 -> x52, local copies, waits for them, and re-layouts: 18.5 us -> 3.13 us
    pallas_call x1 -> x2, Pallas kernels: 39.6 us -> 48.2 us  [the longest x1 41.2 us: grads_out(): pl.pallas_call(grads_out_kernel, in_specs=[ANY] + [VM] * len(small) + [AN...]
    pallas_call x1, Pallas kernels: 67.2 us -> 71.7 us  [self_fwd(): pl.pallas_call(functools.partial(self_fwd_kernel, near), grid_spec=pltpu....]
where the time goes in v5:
time: 439 us; the launch traced here: 431 us
  Pallas kernels  418 us (95%)
  local copies, waits for them, and re-layouts  9.28 us (2%)
    pallas_call x1, Pallas kernels, self_bwd(): pl.pallas_call(functools.partial(self_bwd_kernel, near), grid=(H,), in_sp...  92.4 us
    pallas_call x1, Pallas kernels, self_fwd(): pl.pallas_call(functools.partial(self_fwd_kernel, near), grid_spec=pltpu....  71.7 us
    pallas_call x1, Pallas kernels, cross_bwd(): pl.pallas_call(functools.partial(cross_bwd_kernel, near), grid=(H,), in_s...  64 us
    pallas_call x1, Pallas kernels, cross_fwd(): pl.pallas_call(functools.partial(cross_fwd_kernel, near), grid=(H // 2,),...  52.9 us
    pallas_call x1, Pallas kernels, feed(): pl.pallas_call(feed_kernel, grid=(nf,), in_specs=[one, one, col((D, D), 4...  46.4 us
    pallas_call x1, Pallas kernels, weights_in(): pl.pallas_call(weights_in_kernel, in_specs=[ANY, ANY, ANY, VM], out_specs...  42.5 us
    pallas_call x1, Pallas kernels, grads_out(): pl.pallas_call(grads_out_kernel, in_specs=[ANY] + [VM] * len(small) + [AN...  41.2 us

profile of v5, /device:TPU:0, one launch (start us, length us, event | category | flops | bytes accessed | tf_op | source)
XLA Modules:
  0.0 430.7 jit_solution(4782222886986905359)
XLA Ops:
  0.8 0.6 copy-done
  1.4 1.1 convolution_bitcast_fusion
  2.6 0.2 reverse.2
  2.8 0.1 reverse.3
  3.1 0.1 reverse.4
  3.6 0.2 rev.25
  3.9 0.1 rev.29
  4.9 42.5 %weights_in.1 = (bf16[32,24,2432]{2,1,0:T(8,128)(2,1)}, bf16[4,24,3840]{2,1,0:T(8,128)(2,1)}, bf16[4,256,768]{2,1,0:T(8,128)(2,1)}, f32[12,4,256,256]{3,2,1,0:T(8,128)}) custom-call(bf16[24,2432]{1,0:T(8,128)(2,1)S(1)} %fusion.2.w_ref, bf16[24,3840]{1,0:T(8,128)(2,1)S(1)} %constant_dynamic-update-slice_fusion.wm_ref, bf16[4,256,768]{2,1,0:T(8,128)(2,1)S(1)} %copy-done.2, ...), custom_call_target="tpu_custom_call" | custom-call | tf_op jit(solution)/shard_map/weights_in/pallas_call | solution.py:488
  47.4 0.4 copy.75
  47.8 0.5 copy.76
  48.4 0.2 copy.78
  48.6 0.9 reshape.93.refs_1_
  49.6 71.7 %self_fwd.1 = (bf16[1024,768]{1,0:T(8,128)(2,1)}, bf16[1024,768]{1,0:T(8,128)(2,1)}, bf16[1024,768]{1,0:T(8,128)(2,1)}, bf16[1024,768]{1,0:T(8,128)(2,1)}, f32[8...) custom-call(s32[4,4]{1,0:T(4,128)} %st_ref.1, ...), custom_call_target="tpu_custom_call" | custom-call | flops 51999997952 | bytes 45000000 | tf_op jit(solution)/shard_map/self_fwd/pallas_call | solution.py:736
  121.3 52.9 %cross_fwd.1 = (f32[1024,768]{1,0:T(8,128)}, bf16[1024,768]{1,0:T(8,128)(2,1)}, bf16[1024,768]{1,0:T(8,128)(2,1)}, bf16[1024,768]{1,0:T(8,128)(2,1)}, bf16[1024,...) custom-call(bf16[1024,768]{1,0:T(8,128)(2,1)} %bitcast.69, ...), custom_call_target="tpu_custom_call" | custom-call | flops 31000000512 | bytes 50000000 | tf_op jit(solution)/shard_map/cross_fwd/pallas_call | solution.py:820
  174.2 46.4 %feed.1 = (bf16[1024,768]{1,0:T(8,128)(2,1)}, f32[1024,768]{1,0:T(8,128)}, bf16[1024,768]{1,0:T(8,128)(2,1)}, bf16[768,6144]{1,0:T(8,128)(2,1)}, f32[8,768]{1,0:T(8,128)}) custom-call(f32[1024,768]{1,0:T(8,128)} %get-tuple-element.108.h1_ref.h1_h, bf16[1024,768]{1,0:T(8,128)(2,1)} %get-tuple-element.109.catt_ref.catt_h, bf16[768,3840]{1,0:T(8,128)(2,1)} %bitcast.80, ...), custom_call_target="tpu_custom_call" | custom-call | flops 32000000000 | bytes 50000000 | tf_op jit(solution)/shard_map/feed/pallas_call | solution.py:883
  220.5 64.0 %cross_bwd.1 = (bf16[768,3840]{1,0:T(8,128)(2,1)}, bf16[1024,768]{1,0:T(8,128)(2,1)}, f32[1024,768]{1,0:T(8,128)}, bf16[1024,768]{1,0:T(8,128)(2,1)}, f32[8,768]{1,0:T(8,128)}, /*index=5*/bf16[4,24,6144]{2,1,0:T(8,128)(2,1)}) custom-call(bf16[1024,768]{1,0:T(8,128)(2,1)} %get-tuple-element.105.q_ref, bf16[1024,768]{1,0:T(8,128)(2,1)} %get-tuple-element.106.k_ref, ...), custom_call_target="tpu_custom_call" | custom-call | flops 36999999488 | bytes 70000000 | tf_op jit(solution)/shard_map/cross_bwd/pallas_call | solution.py:988
  284.5 92.4 %self_bwd.1 = (bf16[768,2304]{1,0:T(8,128)(2,1)}, bf16[1024,768]{1,0:T(8,128)(2,1)}, f32[12,768]{1,0:T(8,128)}, f32[12,768]{1,0:T(8,128)}, f32[12,4,1,512]{3,2,1...) custom-call(bf16[1024,768]{1,0:T(8,128)(2,1)} %get-tuple-element.97., ...), custom_call_target="tpu_custom_call" | custom-call | flops 128000000000 | bytes 50000000 | tf_op jit(solution)/shard_map/self_bwd/pallas_call | solution.py:1124
  377.3 0.6 pad_add_fusion.bucket
  378.0 41.2 %grads_out.1 = (f32[24,768]{1,0:T(8,128)}, f32[24,768]{1,0:T(8,128)}, f32[24,768]{1,0:T(8,128)}, f32[24,128]{1,0:T(8,128)}, f32[12,12]{1,0:T(8,128)}, /*index=5*...) custom-call(bf16[4,4,2,24,2304]{4,3,2,1,0:T(8,128)(2,1)} %bitcast.48, f32[8,768]{1,0:T(8,128)} %get-tuple-element.128.dgs, ...), custom_call_target="tpu_custom_call" | custom-call | tf_op jit(solution)/shard_map/grads_out/pallas_call | solution.py:554
  419.2 7.0 %finish.1 = (bf16[4,256,768]{2,1,0:T(8,128)(2,1)}, f32[4,256,768]{2,1,0:T(8,128)}, f32[4,256,768]{2,1,0:T(8,128)}, f32[24,768]{1,0:T(8,128)}, f32[24,768]{1,0:T(...) custom-call(bf16[4,256,768]{2,1,0:T(8,128)(2,1)} %get-tuple-element., ...), custom_call_target="tpu_custom_call" | custom-call | tf_op jit(solution)/shard_map/finish/pallas_call | solution.py:585
  426.2 1.6 copy.79
  427.8 1.2 copy.80
  429.0 0.8 reshape.105
  429.9 0.5 slice_bitcast_fusion
  (74 shorter events, 2.1 us)
Async XLA Ops:
  0.7 0.7 copy-start
  0.7 3.9 copy-start.9
  0.7 3.9 copy-start.10
  0.7 3.9 copy-start.11
  0.7 3.9 copy-start.12
  0.7 3.9 copy-start.13
  0.7 3.9 copy-start.18
  0.7 3.9 copy-start.17
  0.7 3.9 copy-start.16
  0.8 4.1 copy-start.8
  0.8 4.1 copy-start.7
  0.8 4.0 copy-start.6
  0.8 4.1 copy-start.2
  4.3 43.1 %copy-start.4 = (bf16[24,3072]{1,0:T(8,128)(2,1)S(1)}, bf16[24,3072]{1,0:T(8,128)(2,1)}, u32[]{:S(2)}) copy-start(bf16[24,3072]{1,0:T(8,128)(2,1)} %param.34) | copy-start | bytes 442372
  4.9 43.4 %copy-start.5 = (bf16[96,768]{1,0:T(8,128)(2,1)S(1)}, bf16[96,768]{1,0:T(8,128)(2,1)}, u32[]{:S(2)}) copy-start(bf16[96,768]{1,0:T(8,128)(2,1)} %param.35) | copy-start | bytes 442372
  284.5 92.4 %copy-start.14 = (s32[1024]{0:T(1024)S(1)}, s32[1024]{0:T(1024)}, u32[]{:S(2)}) copy-start(s32[1024]{0:T(1024)} %param.25) | copy-start | bytes 12292
  426.2 2.8 copy-start.3
  426.2 4.2 copy-start.1
  427.8 2.0 copy-start.15

commit v6 on v5

--- a/solution.py
+++ b/solution.py
@@ -469,11 +469,11 @@
     gat.hop(0)
     gat.line(2)
     gat.line(3)
+    rest.start()
     lin.start()
     gat.diag(0)
     for kz in range(1, NZ):
         gat.hop(kz)
-    rest.start()
     for kz in range(1, NZ):
         gat.diag(kz)
     flush(H - 2).wait()
@@ -639,7 +639,7 @@
     return [slice(i * BLK, (i + 1) * BLK) for i in range(n)]
 
 
-FWD_PLAN = ((2, "exc", 0), (5, "hop", 0), (5, "exc", 1), (9, "diag", 0))
+FWD_PLAN = ((3, "exc", 0), (4, "hop", 0), (5, "exc", 1), (8, "diag", 0))
 CROSS_PLAN = ((4, "hop"),)
 
 
@@ -976,7 +976,7 @@
             sca.stop(rf_ref)
 
 
-BWD_PLAN = ((1, "away"), (1, "start", (2, 1)), (3, "start", (0,)), (6, "near"))
+BWD_PLAN = ((2, "away"), (2, "start", (2, 1)), (3, "start", (0,)), (6, "near"))
 
 
 def cross_bwd(q, k, v, do, p, gains, n2, enc, att, catt, h1, bh2, wmid, far=None, cid=None):

time: 439 us -> 436 us (level)
  no operation moved by 1% of the time
where the time goes in v6:
time: 436 us; the launch traced here: 429 us
  Pallas kernels  417 us (96%)
  local copies, waits for them, and re-layouts  9.28 us (2%)
    pallas_call x1, Pallas kernels, self_bwd(): pl.pallas_call(functools.partial(self_bwd_kernel, near), grid=(H,), in_sp...  92.1 us
    pallas_call x1, Pallas kernels, self_fwd(): pl.pallas_call(functools.partial(self_fwd_kernel, near), grid_spec=pltpu....  71.7 us
    pallas_call x1, Pallas kernels, cross_bwd(): pl.pallas_call(functools.partial(cross_bwd_kernel, near), grid=(H,), in_s...  61.9 us
    pallas_call x1, Pallas kernels, cross_fwd(): pl.pallas_call(functools.partial(cross_fwd_kernel, near), grid=(H // 2,),...  55.3 us
    pallas_call x1, Pallas kernels, feed(): pl.pallas_call(feed_kernel, grid=(nf,), in_specs=[one, one, col((D, D), 4...  46.4 us
    pallas_call x1, Pallas kernels, weights_in(): pl.pallas_call(weights_in_kernel, in_specs=[ANY, ANY, ANY, VM], out_specs...  41.3 us
    pallas_call x1, Pallas kernels, grads_out(): pl.pallas_call(grads_out_kernel, in_specs=[ANY] + [VM] * len(small) + [AN...  41.1 us

profile of v6, /device:TPU:0, one launch (start us, length us, event | category | flops | bytes accessed | tf_op | source)
XLA Modules:
  0.0 429.4 jit_solution(12510480009142968222)
XLA Ops:
  0.8 0.6 copy-done
  1.4 1.1 convolution_bitcast_fusion
  2.6 0.2 reverse.2
  2.8 0.1 reverse.3
  3.1 0.1 reverse.4
  3.3 0.1 reverse.5
  3.6 0.2 rev.25
  4.9 41.3 %weights_in.1 = (bf16[32,24,2432]{2,1,0:T(8,128)(2,1)}, bf16[4,24,3840]{2,1,0:T(8,128)(2,1)}, bf16[4,256,768]{2,1,0:T(8,128)(2,1)}, f32[12,4,256,256]{3,2,1,0:T(8,128)}) custom-call(bf16[24,2432]{1,0:T(8,128)(2,1)S(1)} %fusion.2.w_ref, bf16[24,3840]{1,0:T(8,128)(2,1)S(1)} %constant_dynamic-update-slice_fusion.wm_ref, bf16[4,256,768]{2,1,0:T(8,128)(2,1)S(1)} %copy-done.2, ...), custom_call_target="tpu_custom_call" | custom-call | tf_op jit(solution)/shard_map/weights_in/pallas_call | solution.py:488
  46.2 0.4 copy.75
  46.6 0.5 copy.76
  47.2 0.2 copy.78
  47.4 0.9 reshape.93.refs_1_
  48.3 71.7 %self_fwd.1 = (bf16[1024,768]{1,0:T(8,128)(2,1)}, bf16[1024,768]{1,0:T(8,128)(2,1)}, bf16[1024,768]{1,0:T(8,128)(2,1)}, bf16[1024,768]{1,0:T(8,128)(2,1)}, f32[8...) custom-call(s32[4,4]{1,0:T(4,128)} %st_ref.1, ...), custom_call_target="tpu_custom_call" | custom-call | flops 51999997952 | bytes 45000000 | tf_op jit(solution)/shard_map/self_fwd/pallas_call | solution.py:736
  120.1 55.3 %cross_fwd.1 = (f32[1024,768]{1,0:T(8,128)}, bf16[1024,768]{1,0:T(8,128)(2,1)}, bf16[1024,768]{1,0:T(8,128)(2,1)}, bf16[1024,768]{1,0:T(8,128)(2,1)}, bf16[1024,...) custom-call(bf16[1024,768]{1,0:T(8,128)(2,1)} %bitcast.69, ...), custom_call_target="tpu_custom_call" | custom-call | flops 31000000512 | bytes 50000000 | tf_op jit(solution)/shard_map/cross_fwd/pallas_call | solution.py:820
  175.4 46.4 %feed.1 = (bf16[1024,768]{1,0:T(8,128)(2,1)}, f32[1024,768]{1,0:T(8,128)}, bf16[1024,768]{1,0:T(8,128)(2,1)}, bf16[768,6144]{1,0:T(8,128)(2,1)}, f32[8,768]{1,0:T(8,128)}) custom-call(f32[1024,768]{1,0:T(8,128)} %get-tuple-element.108.h1_ref.h1_h, bf16[1024,768]{1,0:T(8,128)(2,1)} %get-tuple-element.109.catt_ref.catt_h, bf16[768,3840]{1,0:T(8,128)(2,1)} %bitcast.80, ...), custom_call_target="tpu_custom_call" | custom-call | flops 32000000000 | bytes 50000000 | tf_op jit(solution)/shard_map/feed/pallas_call | solution.py:883
  221.7 61.9 %cross_bwd.1 = (bf16[768,3840]{1,0:T(8,128)(2,1)}, bf16[1024,768]{1,0:T(8,128)(2,1)}, f32[1024,768]{1,0:T(8,128)}, bf16[1024,768]{1,0:T(8,128)(2,1)}, f32[8,768]{1,0:T(8,128)}, /*index=5*/bf16[4,24,6144]{2,1,0:T(8,128)(2,1)}) custom-call(bf16[1024,768]{1,0:T(8,128)(2,1)} %get-tuple-element.105.q_ref, bf16[1024,768]{1,0:T(8,128)(2,1)} %get-tuple-element.106.k_ref, ...), custom_call_target="tpu_custom_call" | custom-call | flops 36999999488 | bytes 70000000 | tf_op jit(solution)/shard_map/cross_bwd/pallas_call | solution.py:988
  283.7 92.1 %self_bwd.1 = (bf16[768,2304]{1,0:T(8,128)(2,1)}, bf16[1024,768]{1,0:T(8,128)(2,1)}, f32[12,768]{1,0:T(8,128)}, f32[12,768]{1,0:T(8,128)}, f32[12,4,1,512]{3,2,1...) custom-call(bf16[1024,768]{1,0:T(8,128)(2,1)} %get-tuple-element.97., ...), custom_call_target="tpu_custom_call" | custom-call | flops 128000000000 | bytes 50000000 | tf_op jit(solution)/shard_map/self_bwd/pallas_call | solution.py:1124
  376.2 0.6 pad_add_fusion.bucket
  376.8 41.1 %grads_out.1 = (f32[24,768]{1,0:T(8,128)}, f32[24,768]{1,0:T(8,128)}, f32[24,768]{1,0:T(8,128)}, f32[24,128]{1,0:T(8,128)}, f32[12,12]{1,0:T(8,128)}, /*index=5*...) custom-call(bf16[4,4,2,24,2304]{4,3,2,1,0:T(8,128)(2,1)} %bitcast.48, f32[8,768]{1,0:T(8,128)} %get-tuple-element.128.dgs, ...), custom_call_target="tpu_custom_call" | custom-call | tf_op jit(solution)/shard_map/grads_out/pallas_call | solution.py:554
  417.9 7.0 %finish.1 = (bf16[4,256,768]{2,1,0:T(8,128)(2,1)}, f32[4,256,768]{2,1,0:T(8,128)}, f32[4,256,768]{2,1,0:T(8,128)}, f32[24,768]{1,0:T(8,128)}, f32[24,768]{1,0:T(...) custom-call(bf16[4,256,768]{2,1,0:T(8,128)(2,1)} %get-tuple-element., ...), custom_call_target="tpu_custom_call" | custom-call | tf_op jit(solution)/shard_map/finish/pallas_call | solution.py:585
  424.9 1.6 copy.79
  426.5 1.2 copy.80
  427.7 0.8 reshape.105
  428.6 0.5 slice_bitcast_fusion
  (74 shorter events, 2.1 us)
Async XLA Ops:
  0.7 0.7 copy-start
  0.7 3.9 copy-start.9
  0.7 3.9 copy-start.10
  0.7 3.9 copy-start.11
  0.7 3.9 copy-start.12
  0.7 3.9 copy-start.13
  0.7 3.9 copy-start.18
  0.7 3.9 copy-start.17
  0.7 3.9 copy-start.16
  0.8 4.1 copy-start.8
  0.8 4.1 copy-start.7
  0.8 4.0 copy-start.6
  0.8 4.1 copy-start.2
  4.3 41.9 %copy-start.4 = (bf16[24,3072]{1,0:T(8,128)(2,1)S(1)}, bf16[24,3072]{1,0:T(8,128)(2,1)}, u32[]{:S(2)}) copy-start(bf16[24,3072]{1,0:T(8,128)(2,1)} %param.34) | copy-start | bytes 442372
  4.9 42.2 %copy-start.5 = (bf16[96,768]{1,0:T(8,128)(2,1)S(1)}, bf16[96,768]{1,0:T(8,128)(2,1)}, u32[]{:S(2)}) copy-start(bf16[96,768]{1,0:T(8,128)(2,1)} %param.35) | copy-start | bytes 442372
  283.7 92.1 %copy-start.14 = (s32[1024]{0:T(1024)S(1)}, s32[1024]{0:T(1024)}, u32[]{:S(2)}) copy-start(s32[1024]{0:T(1024)} %param.25) | copy-start | bytes 12292
  424.9 2.8 copy-start.3
  424.9 4.2 copy-start.1
  426.5 2.0 copy-start.15

commit v7 on v6

--- a/solution.py
+++ b/solution.py
@@ -497,13 +497,16 @@
 
 
 def grads_out_kernel(g, dgs, dgc, dgf, gpre, gpost, diag, bucket, gt, oq, ok, ov, o_gain, o_pre, o_post, o_tab, gt_o,
-                     mc, mx, mz, ms, mr, small, e1, e2, e3, *bufs):
+                     mc, mx, mz, ms, mr, small, e1, e2, e3, r1, r2, r3, *bufs):
     sca = Scatter(g, [oq, ok, ov], *bufs)
     s, z, c = place()
     zs, ss, co = partners(s, z, c)
-    exc = Exchange(gt, gt_o, e1, e2, e3)
+    exc = Exchange(gt, gt_o, e1, e2, e3, (0, 2))
+    rest = Exchange(gt, gt_o, r1, r2, r3, (1, 2))
     meet_all()
-    sca.start((3, 2, 1, 0))
+    sca.start((3,))
+    exc.start()
+    sca.start((2, 1, 0))
     nbk = o_tab.shape[1]
     small[...] = jnp.zeros_like(small)
     for i, d in enumerate((dgs, dgc, dgf)):
@@ -527,7 +530,7 @@
     for cp in xy:
         cp.start()
     sca.near()
-    exc.start()
+    rest.start()
     for cp in xy:
         cp.wait_recv()
     mz[z] = (mx[0] + mx[1]) + (mx[2] + mx[3])
@@ -543,6 +546,7 @@
     o_tab[...] = v[24:24 + H, 32:32 + nbk]
     o_gain[...] = v[:24]
     exc.end()
+    rest.end()
     sca.end()
     for cp in [first] + xy + zz:
         cp.wait_send()
@@ -557,7 +561,7 @@
         out_shape=[sds((rows, D), F32)] * 3
         + [sds((24, 128), F32), sds((H, H), F32), sds((H, H), F32), sds((H, nbk), F32), sds(gt.shape, BF)],
         scratch_shapes=[pltpu.VMEM(sm, F32), pltpu.VMEM((4,) + sm, F32), pltpu.VMEM((4,) + sm, F32), DMA((7,)), DMA((7,)),
-                        pltpu.VMEM(sm, F32)] + Exchange.sems() + Scatter.bufs(*g.shape[3:]),
+                        pltpu.VMEM(sm, F32)] + Exchange.sems() * 2 + Scatter.bufs(*g.shape[3:]),
         compiler_params=params(56, cid), name="grads_out")(g, *small, gt)
 
 
@@ -603,12 +607,12 @@
     return pl.BlockSpec(shape, lambda *a: (0, j), pipeline_mode=pl.Buffered(1))
 
 
-def each(f):
+def each(f, unroll=1):
     def step(i, carry):
         f(pl.ds(pl.multiple_of(i * BLK, BLK), BLK))
         return carry
 
-    lax.fori_loop(0, NBK, step, 0)
+    lax.fori_loop(0, NBK, step, 0, unroll=unroll)
 
 
 def rows8(v):
@@ -781,7 +785,7 @@
             k_ref[r, :] = dot(enc_ref[r, :], wk_ref[...], 1, 0).astype(BF)
             v_ref[r, :] = dot(enc_ref[r, :], wv_ref[...], 1, 0).astype(BF)
 
-        each(project)
+        each(project, 2)
 
     cols = pl.ds(pl.multiple_of(h * 128, 128), 128)
     first = lax.broadcasted_iota(jnp.int32, (1, 128), 1) < DH
@@ -844,7 +848,7 @@
             acc[r, :] = h2
             n3[r, :] = norm(h2, g).astype(BF)
 
-        each(enter)
+        each(enter, NBK)
         n3t[...] = n3[...].T
         cott[...] = cot_ref[...].T
         dn[...] = jnp.zeros_like(dn)
@@ -874,7 +878,7 @@
             bh2_ref[r, :] = b2
             bca_ref[r, :] = dot(b2.astype(BF), wco_ref[...], 1, 1).astype(BF)
 
-        each(leave)
+        each(leave, NBK)
 
 
 def feed(h1, catt, wmid, cot, gains, wfeed):

time: 436 us -> 434 us (level)
  no operation moved by 1% of the time
where the time goes in v7:
time: 434 us; the launch traced here: 428 us
  Pallas kernels  415 us (96%)
  local copies, waits for them, and re-layouts  9.28 us (2%)
    pallas_call x1, Pallas kernels, self_bwd(): pl.pallas_call(functools.partial(self_bwd_kernel, near), grid=(H,), in_sp...  92.3 us
    pallas_call x1, Pallas kernels, self_fwd(): pl.pallas_call(functools.partial(self_fwd_kernel, near), grid_spec=pltpu....  71.7 us
    pallas_call x1, Pallas kernels, cross_bwd(): pl.pallas_call(functools.partial(cross_bwd_kernel, near), grid=(H,), in_s...  62.2 us
    pallas_call x1, Pallas kernels, cross_fwd(): pl.pallas_call(functools.partial(cross_fwd_kernel, near), grid=(H // 2,),...  55.2 us
    pallas_call x1, Pallas kernels, feed(): pl.pallas_call(feed_kernel, grid=(nf,), in_specs=[one, one, col((D, D), 4...  44.4 us
    pallas_call x1, Pallas kernels, grads_out(): pl.pallas_call(grads_out_kernel, in_specs=[ANY] + [VM] * len(small) + [AN...  41.3 us
    pallas_call x1, Pallas kernels, weights_in(): pl.pallas_call(weights_in_kernel, in_specs=[ANY, ANY, ANY, VM], out_specs...  41.3 us

profile of v7, /device:TPU:0, one launch (start us, length us, event | category | flops | bytes accessed | tf_op | source)
XLA Modules:
  0.0 427.9 jit_solution(13040870561024997681)
XLA Ops:
  0.8 0.6 copy-done
  1.4 1.1 convolution_bitcast_fusion
  2.6 0.2 reverse.2
  2.8 0.1 reverse.3
  3.1 0.1 reverse.4
  3.3 0.1 reverse.5
  3.6 0.2 rev.25
  4.9 41.3 %weights_in.1 = (bf16[32,24,2432]{2,1,0:T(8,128)(2,1)}, bf16[4,24,3840]{2,1,0:T(8,128)(2,1)}, bf16[4,256,768]{2,1,0:T(8,128)(2,1)}, f32[12,4,256,256]{3,2,1,0:T(8,128)}) custom-call(bf16[24,2432]{1,0:T(8,128)(2,1)S(1)} %fusion.2.w_ref, bf16[24,3840]{1,0:T(8,128)(2,1)S(1)} %constant_dynamic-update-slice_fusion.wm_ref, bf16[4,256,768]{2,1,0:T(8,128)(2,1)S(1)} %copy-done.2, ...), custom_call_target="tpu_custom_call" | custom-call | tf_op jit(solution)/shard_map/weights_in/pallas_call | solution.py:488
  46.2 0.4 copy.75
  46.6 0.5 copy.76
  47.2 0.2 copy.78
  47.4 0.9 reshape.93.refs_1_
  48.3 71.7 %self_fwd.1 = (bf16[1024,768]{1,0:T(8,128)(2,1)}, bf16[1024,768]{1,0:T(8,128)(2,1)}, bf16[1024,768]{1,0:T(8,128)(2,1)}, bf16[1024,768]{1,0:T(8,128)(2,1)}, f32[8...) custom-call(s32[4,4]{1,0:T(4,128)} %st_ref.1, ...), custom_call_target="tpu_custom_call" | custom-call | flops 51999997952 | bytes 45000000 | tf_op jit(solution)/shard_map/self_fwd/pallas_call | solution.py:740
  120.1 55.2 %cross_fwd.1 = (f32[1024,768]{1,0:T(8,128)}, bf16[1024,768]{1,0:T(8,128)(2,1)}, bf16[1024,768]{1,0:T(8,128)(2,1)}, bf16[1024,768]{1,0:T(8,128)(2,1)}, bf16[1024,...) custom-call(bf16[1024,768]{1,0:T(8,128)(2,1)} %bitcast.69, ...), custom_call_target="tpu_custom_call" | custom-call | flops 31000000512 | bytes 50000000 | tf_op jit(solution)/shard_map/cross_fwd/pallas_call | solution.py:824
  175.2 44.4 %feed.1 = (bf16[1024,768]{1,0:T(8,128)(2,1)}, f32[1024,768]{1,0:T(8,128)}, bf16[1024,768]{1,0:T(8,128)(2,1)}, bf16[768,6144]{1,0:T(8,128)(2,1)}, f32[8,768]{1,0:T(8,128)}) custom-call(f32[1024,768]{1,0:T(8,128)} %get-tuple-element.108.h1_ref.h1_h, bf16[1024,768]{1,0:T(8,128)(2,1)} %get-tuple-element.109.catt_ref.catt_h, bf16[768,3840]{1,0:T(8,128)(2,1)} %bitcast.80, ...), custom_call_target="tpu_custom_call" | custom-call | flops 32000000000 | bytes 50000000 | tf_op jit(solution)/shard_map/feed/pallas_call | solution.py:887
  219.6 62.2 %cross_bwd.1 = (bf16[768,3840]{1,0:T(8,128)(2,1)}, bf16[1024,768]{1,0:T(8,128)(2,1)}, f32[1024,768]{1,0:T(8,128)}, bf16[1024,768]{1,0:T(8,128)(2,1)}, f32[8,768]{1,0:T(8,128)}, /*index=5*/bf16[4,24,6144]{2,1,0:T(8,128)(2,1)}) custom-call(bf16[1024,768]{1,0:T(8,128)(2,1)} %get-tuple-element.105.q_ref, bf16[1024,768]{1,0:T(8,128)(2,1)} %get-tuple-element.106.k_ref, ...), custom_call_target="tpu_custom_call" | custom-call | flops 36999999488 | bytes 70000000 | tf_op jit(solution)/shard_map/cross_bwd/pallas_call | solution.py:992
  281.8 92.3 %self_bwd.1 = (bf16[768,2304]{1,0:T(8,128)(2,1)}, bf16[1024,768]{1,0:T(8,128)(2,1)}, f32[12,768]{1,0:T(8,128)}, f32[12,768]{1,0:T(8,128)}, f32[12,4,1,512]{3,2,1...) custom-call(bf16[1024,768]{1,0:T(8,128)(2,1)} %get-tuple-element.97., ...), custom_call_target="tpu_custom_call" | custom-call | flops 128000000000 | bytes 50000000 | tf_op jit(solution)/shard_map/self_bwd/pallas_call | solution.py:1128
  374.6 0.6 pad_add_fusion.bucket
  375.2 41.3 %grads_out.1 = (f32[24,768]{1,0:T(8,128)}, f32[24,768]{1,0:T(8,128)}, f32[24,768]{1,0:T(8,128)}, f32[24,128]{1,0:T(8,128)}, f32[12,12]{1,0:T(8,128)}, /*index=5*...) custom-call(bf16[4,4,2,24,2304]{4,3,2,1,0:T(8,128)(2,1)} %bitcast.48, f32[8,768]{1,0:T(8,128)} %get-tuple-element.128.dgs, ...), custom_call_target="tpu_custom_call" | custom-call | tf_op jit(solution)/shard_map/grads_out/pallas_call | solution.py:558
  416.5 7.0 %finish.1 = (bf16[4,256,768]{2,1,0:T(8,128)(2,1)}, f32[4,256,768]{2,1,0:T(8,128)}, f32[4,256,768]{2,1,0:T(8,128)}, f32[24,768]{1,0:T(8,128)}, f32[24,768]{1,0:T(...) custom-call(bf16[4,256,768]{2,1,0:T(8,128)(2,1)} %get-tuple-element., ...), custom_call_target="tpu_custom_call" | custom-call | tf_op jit(solution)/shard_map/finish/pallas_call | solution.py:589
  423.5 1.6 copy.79
  425.1 1.2 copy.80
  426.3 0.8 reshape.105
  427.2 0.5 slice_bitcast_fusion
  (74 shorter events, 2.1 us)
Async XLA Ops:
  0.7 0.7 copy-start
  0.7 3.9 copy-start.9
  0.7 3.9 copy-start.10
  0.7 3.9 copy-start.11
  0.7 3.9 copy-start.12
  0.7 3.9 copy-start.13
  0.7 3.9 copy-start.18
  0.7 3.9 copy-start.17
  0.7 3.9 copy-start.16
  0.8 4.1 copy-start.8
  0.8 4.1 copy-start.7
  0.8 4.0 copy-start.6
  0.8 4.1 copy-start.2
  4.3 41.9 %copy-start.4 = (bf16[24,3072]{1,0:T(8,128)(2,1)S(1)}, bf16[24,3072]{1,0:T(8,128)(2,1)}, u32[]{:S(2)}) copy-start(bf16[24,3072]{1,0:T(8,128)(2,1)} %param.34) | copy-start | bytes 442372
  4.9 42.2 %copy-start.5 = (bf16[96,768]{1,0:T(8,128)(2,1)S(1)}, bf16[96,768]{1,0:T(8,128)(2,1)}, u32[]{:S(2)}) copy-start(bf16[96,768]{1,0:T(8,128)(2,1)} %param.35) | copy-start | bytes 442372
  281.8 92.3 %copy-start.14 = (s32[1024]{0:T(1024)S(1)}, s32[1024]{0:T(1024)}, u32[]{:S(2)}) copy-start(s32[1024]{0:T(1024)} %param.25) | copy-start | bytes 12292
  423.5 2.8 copy-start.3
  423.5 4.2 copy-start.1
  425.1 2.0 copy-start.15
